TPU v7x, 32 devices: a whole 2x2x4 slice. The times are simulated.
32 devices in a mesh: ctx: 16 (over z, y, x), head: 2 (over core).
Axes of the slice: x: 2, y: 2, z: 4, core: 2. Of those that a mesh axis runs over, the one named last changes fastest.
Arguments:
- kv_cache: bfloat16 [2, 32768, 8, 256], P(None, 'ctx', 'head'), may hold values from -12 to 12
- keep_rows: int32 [2, 128, 128], P(None, 'ctx'), may hold values from 0 to 256, as said below
- block_target: int32 [2, 128, 2], P(None, 'ctx'), may hold values from 0 to 15, as said below
- future_queries: bfloat16 [2, 256, 8192], P(None, 'ctx', 'head'), may hold values from -32 to 32
- new_tokens: bfloat16 [4, 2, 8192], P(None, None, 'ctx'), may hold values from -6 to 6
- w_query: bfloat16 [8192, 8192], P('ctx', 'head'), may hold values from -16 to 16
- w_keyval: bfloat16 [8192, 8, 256], P('ctx', 'head'), may hold values from -0.25 to 0.25
- w_out: bfloat16 [8192, 8192], P('head', 'ctx'), may hold values from -0.1875 to 0.1875
Outputs:
- packed_cache: bfloat16 [2, 16384, 8, 256], P(None, 'ctx', 'head')
- packed_scores: float32 [2, 8, 16384], P(None, 'head', 'ctx')
- decoded: bfloat16 [4, 2, 8192], P(None, None, 'ctx')
Inputs may be any that keep to these rules, and one draw needn't show every extreme that they name: `keep_rows`: in each list the kept offsets come first, distinct and increasing, then entries equal to 256 mark none; every list holds at least one kept offset, and in each request some list holds 128. `block_target`: entry 0 is the destination device, entry 1 the destination block slot. Both depend only on the request and on the list's place b among the 8 lists of its device: the device is (source device + d) modulo 16, where the 16 values of d are 0 to 15, each once; within a request the slots are a permutation of 0 to 7.
All inputs are finite; a program needn't handle non-finite values.
Results may differ from a plain program's by a relative error of at most 0.007.
The roundings to bfloat16 on the way count: a program that leaves them out, or rounds other values in their place, can miss the bound.
Values may be sent and summed in bfloat16 or wider, within the bound.
No kernel may reach another device: no remote copies, remote signals or barrier semaphores. Data moves between devices by JAX's collectives and lax.ppermute only.
A program may use at most 128 MiB of HBM per device.

v0:
```python
import math

import jax
import jax.numpy as jnp
from jax import lax
from jax.sharding import PartitionSpec as P

D = 8192
H = 64
KVH = 8
QS = 256


HIGHEST = lax.Precision.HIGHEST
EPSILON = 1e-05


def joined(value, axis, join):
    pieces = jax.tree.map(lambda part: lax.all_gather(part, axis), value)
    head = jax.tree.map(lambda part: part[0], pieces)
    tail = jax.tree.map(lambda part: part[1:], pieces)
    running, _ = lax.scan(lambda running, share: (join(running, share), None), head, tail)
    return running


def group_scores(keys, mean_q, cov_q):
    lifted = keys.astype(jnp.float32)
    linear = jnp.einsum("nkd,kgd->nkg", lifted, mean_q, precision=HIGHEST)
    turned = jnp.einsum("nkd,kgde->nkge", lifted, cov_q, precision=HIGHEST)
    quadratic = jnp.sum(turned * lifted[:, :, None, :], axis=-1)
    logits = linear / math.sqrt(keys.shape[-1]) + quadratic / (2.0 * keys.shape[-1])
    top = jnp.max(logits, axis=2)
    return top + jnp.log(jnp.mean(jnp.exp(logits - top[:, :, None]), axis=2))


def combine_parts(first, second):
    top_a, total_a, weighted_a = first
    top_b, total_b, weighted_b = second
    best = jnp.maximum(top_a, top_b)
    factor_a = jnp.exp(top_a - best)
    factor_b = jnp.exp(top_b - best)
    return (
        best,
        total_a * factor_a + total_b * factor_b,
        weighted_a * factor_a[..., None] + weighted_b * factor_b[..., None],
    )


def moments(sample):
    second = jnp.einsum("rshd,rshe->rhde", sample, sample, preferred_element_type=jnp.float32)
    summed = jnp.sum(sample.astype(jnp.float32), axis=1)
    return (second, summed)


def per_device(
    kv_cache, keep_rows, block_target, future_queries, new_tokens, w_query, w_keyval, w_out
):
    requests, cache_rows, local_kv, pair = kv_cache.shape
    head_size = pair // 2
    lists, width = (keep_rows.shape[1], keep_rows.shape[2])
    span = 2 * width
    group = H // KVH
    ctx_count = lax.axis_size("ctx")
    position = lax.axis_index("ctx")
    root_size = math.sqrt(head_size)
    sample = future_queries.reshape(requests, -1, local_kv * group, head_size)
    second, summed = moments(sample)
    second, summed = lax.psum((second, summed), "ctx")
    mean_q = summed / QS
    cov_q = second / QS - mean_q[..., :, None] * mean_q[..., None, :]
    mean_q = mean_q.reshape(requests, local_kv, group, head_size)
    cov_q = cov_q.reshape(requests, local_kv, group, head_size, head_size)
    span_index = jnp.arange(span, dtype=jnp.int32)
    block_kv, block_score, block_count = ([], [], [])
    for request in range(requests):
        listed = keep_rows[request]
        picker = (listed[:, :, None] == span_index[None, None, :]).astype(jnp.bfloat16)
        spans = kv_cache[request].reshape(lists, span, local_kv * pair)
        chosen = jnp.einsum(
            "bjs,bsc->bjc", picker, spans, preferred_element_type=jnp.float32
        ).astype(jnp.bfloat16)
        chosen = chosen.reshape(lists, width, local_kv, pair)
        every = group_scores(kv_cache[request][:, :, :head_size], mean_q[request], cov_q[request])
        every = every.reshape(lists, span, local_kv)
        picked = jnp.einsum("bjs,bsk->bkj", picker.astype(jnp.float32), every, precision=HIGHEST)
        block_kv.append(chosen)
        block_score.append(picked)
        block_count.append(jnp.sum((listed < span).astype(jnp.int32), axis=1))
    items_kv = jnp.concatenate(block_kv, axis=0)
    items_score = jnp.concatenate(block_score, axis=0)
    items_count = jnp.concatenate(block_count, axis=0)
    total_items = requests * lists
    targets = block_target.reshape(total_items, 2)
    offset = (targets[:, 0] - position) % ctx_count
    slot = targets[:, 1].reshape(requests, lists)
    peers = jnp.arange(ctx_count, dtype=jnp.int32)
    outgoing = targets[:, 0][None, :] == peers[:, None]
    send_kv = jnp.einsum(
        "pm,mjkc->pjkc", outgoing.astype(jnp.bfloat16), items_kv, preferred_element_type=jnp.float32
    ).astype(jnp.bfloat16)
    send_score = jnp.einsum(
        "pm,mkj->pkj", outgoing.astype(jnp.float32), items_score, precision=HIGHEST
    )
    send_count = jnp.sum(jnp.where(outgoing, items_count[None, :], 0), axis=1)
    recv_kv, recv_score, recv_count = (
        lax.all_to_all(send_kv, "ctx", split_axis=0, concat_axis=0, tiled=True),
        lax.all_to_all(
            send_score.astype(jnp.bfloat16), "ctx", split_axis=0, concat_axis=0, tiled=True
        ).astype(send_score.dtype),
        lax.all_to_all(send_count, "ctx", split_axis=0, concat_axis=0, tiled=True),
    )
    source = (position - offset) % ctx_count
    incoming = source[:, None] == peers[None, :]
    got_kv = jnp.einsum(
        "mp,pjkc->mjkc", incoming.astype(jnp.bfloat16), recv_kv, preferred_element_type=jnp.float32
    ).astype(jnp.bfloat16)
    got_score = jnp.einsum(
        "mp,pkj->mkj", incoming.astype(jnp.float32), recv_score, precision=HIGHEST
    )
    got_count = jnp.sum(jnp.where(incoming, recv_count[None, :], 0), axis=1)
    slot_table = slot[:, None, :] == jnp.arange(lists, dtype=jnp.int32)[None, :, None]
    placed_kv = jnp.einsum(
        "rsb,rbjkc->rsjkc",
        slot_table.astype(jnp.bfloat16),
        got_kv.reshape(requests, lists, width, local_kv, pair),
        preferred_element_type=jnp.float32,
    ).astype(jnp.bfloat16)
    packed_cache = placed_kv.reshape(requests, lists * width, local_kv, pair)
    placed_score = jnp.einsum(
        "rsb,rbkj->rksj",
        slot_table.astype(jnp.float32),
        got_score.reshape(requests, lists, local_kv, width),
        precision=HIGHEST,
    )
    packed_scores = placed_score.reshape(requests, local_kv, lists * width)
    placed_count = jnp.sum(jnp.where(slot_table, got_count.reshape(requests, 1, lists), 0), axis=2)
    live = (jnp.arange(width, dtype=jnp.int32)[None, None, :] < placed_count[:, :, None]).reshape(
        requests, lists * width
    )
    steps = new_tokens.shape[0]
    local_width = new_tokens.shape[2]
    flat = new_tokens.reshape(steps * requests, local_width)
    wide = flat.astype(jnp.float32)
    squares = jnp.sum(wide * wide, axis=1)
    query_part = jnp.dot(flat, w_query, preferred_element_type=jnp.float32)
    pair_part = jnp.dot(
        flat, w_keyval.reshape(local_width, local_kv * pair), preferred_element_type=jnp.float32
    )
    squares, query_part, pair_part = lax.psum((squares, query_part, pair_part), "ctx")
    inverse = lax.rsqrt(squares / D + EPSILON)
    query = (
        (query_part * inverse[:, None])
        .astype(jnp.bfloat16)
        .reshape(steps, requests, local_kv, group, head_size)
    )
    fresh = (
        (pair_part * inverse[:, None]).astype(jnp.bfloat16).reshape(steps, requests, local_kv, pair)
    )
    query = jnp.transpose(query, (1, 2, 0, 3, 4)).reshape(
        requests, local_kv, steps * group, head_size
    )
    fresh = jnp.transpose(fresh, (1, 2, 0, 3))
    logits = (
        jnp.einsum(
            "rkqd,rnkd->rkqn",
            query,
            packed_cache[..., :head_size],
            preferred_element_type=jnp.float32,
        )
        / root_size
    )
    logits = jnp.where(live[:, None, None, :], logits, -jnp.inf)
    top = jnp.max(logits, axis=3)
    weights = jnp.exp(logits - top[..., None])
    totals = jnp.sum(weights, axis=3)
    weighted = jnp.einsum(
        "rkqn,rnkd->rkqd",
        weights.astype(jnp.bfloat16),
        packed_cache[..., head_size:],
        preferred_element_type=jnp.float32,
    )
    top, totals, weighted = joined((top, totals, weighted), "ctx", combine_parts)
    recent = (
        jnp.einsum(
            "rkqd,rkud->rkqu", query, fresh[..., :head_size], preferred_element_type=jnp.float32
        )
        / root_size
    )
    causal = (jnp.arange(steps * group, dtype=jnp.int32) // group)[:, None] >= jnp.arange(
        steps, dtype=jnp.int32
    )[None, :]
    recent = jnp.where(causal[None, None], recent, -jnp.inf)
    best = jnp.maximum(top, jnp.max(recent, axis=3))
    weight_new = jnp.exp(recent - best[..., None])
    factor_old = jnp.exp(top - best)
    normalizer = totals * factor_old + jnp.sum(weight_new, axis=3)
    weighted = weighted * factor_old[..., None] + jnp.einsum(
        "rkqu,rkud->rkqd",
        weight_new.astype(jnp.bfloat16),
        fresh[..., head_size:],
        preferred_element_type=jnp.float32,
    )
    attended = (weighted / normalizer[..., None]).astype(jnp.bfloat16)
    attended = attended.reshape(requests, local_kv, steps, group, head_size)
    attended = jnp.transpose(attended, (2, 0, 1, 3, 4)).reshape(
        steps * requests, local_kv * group * head_size
    )
    partial_value = jnp.dot(attended, w_out, preferred_element_type=jnp.float32)
    summed_out = lax.psum(partial_value, "head")
    decoded = summed_out.astype(jnp.bfloat16).reshape(steps, requests, local_width)
    return (packed_cache, packed_scores, decoded)


def solution(mesh):
    in_specs = (
        P(None, "ctx", "head", None),
        P(None, "ctx", None),
        P(None, "ctx", None),
        P(None, "ctx", "head"),
        P(None, None, "ctx"),
        P("ctx", "head"),
        P("ctx", "head", None),
        P("head", "ctx"),
    )
    out_specs = (P(None, "ctx", "head", None), P(None, "head", "ctx"), P(None, None, "ctx"))
    return jax.shard_map(
        per_device, mesh=mesh, in_specs=in_specs, out_specs=out_specs, check_vma=False
    )
```

profile of v0, /device:TPU:0, one launch (start us, length us, event | category | flops | bytes accessed | tf_op | source)
XLA Modules:
  0.0 580.1 jit_solution(1433450122064738486)
XLA Ops:
  7.2 0.7 copy.71
  7.9 0.8 convert_reduce_fusion.2
  9.0 0.7 copy.92
  9.7 8.3 %all-to-all-start.2 = ((s32[16,1,1]{2,1,0:T(1,128)}), s32[16,1,1]{2,1,0:T(1,128)S(1)}, u32[]{:S(2)}, u32[]{:S(2)}) async-start(s32[16,1,1]{2,1,0:T(1,128)} %copy.92), calls=%async_computation.2 | async-start | bytes 16384 | tf_op jit(solution)/shard_map/all_to_all | solution.py:110
  18.0 0.7 slice_bitcast_fusion.5
  18.7 8.1 %fusion.96 = (bf16[1,2048,4,256]{3,2,1,0:T(4,128)(2,1)}, bf16[1,2048,4,256]{3,2,1,0:T(4,128)(2,1)}) fusion(bf16[2,2048,4,256]{3,2,1,0:T(4,128)(2,1)} %param.10), kind=kLoop, calls=%fused_computation.148 | loop fusion | bytes 16777216 | tf_op jit(solution)/shard_map/slice | solution.py:78
  26.8 7.7 %reshape_squeeze.6 = bf16[8,256,1024]{2,1,0:T(8,128)(2,1)} reshape(bf16[1,2048,4,256]{3,2,1,0:T(4,128)(2,1)} %get-tuple-element.84) | data formatting | bytes 8388608 | tf_op jit(solution)/shard_map/reshape;squeeze | solution.py:78
  34.5 4.3 convolution_convert_fusion.1
  38.8 3.3 reshape.152
  42.2 3.6 copy.76
  45.7 7.7 %reshape_squeeze.7 = bf16[8,256,1024]{2,1,0:T(8,128)(2,1)} reshape(bf16[1,2048,4,256]{3,2,1,0:T(4,128)(2,1)} %get-tuple-element.85) | data formatting | bytes 8388608 | tf_op jit(solution)/shard_map/reshape;squeeze | solution.py:78
  53.5 4.3 convolution_convert_fusion
  57.8 3.3 reshape.153
  61.1 2.3 copy.77
  63.4 1.4 fusion.18
  64.8 4.1 copy.78
  69.0 7.1 %all-to-all-start = ((bf16[16,128,4,256]{3,2,1,0:T(4,128)(2,1)}), bf16[16,128,4,256]{3,2,1,0:T(4,128)(2,1)}, u32[]{:S(2)}, u32[]{:S(2)}) async-start(bf16[16,128,4,256]{3,2,1,0:T(4,128)(2,1)} %copy.78), calls=%async_computation | async-start | bytes 8388608 | tf_op jit(solution)/shard_map/all_to_all | solution.py:106
  76.7 0.6 copy.149
  77.4 0.6 reduce_sum.133
  78.0 0.9 fusion.103
  78.9 2.7 fusion.55
  81.7 0.6 copy-done.5
  82.3 1.3 fusion.102
  83.7 6.5 %copy_bitcast_fusion = (bf16[2048,4,256]{2,0,1:T(8,128)(2,1)}, bf16[2048,4,256]{2,0,1:T(8,128)(2,1)S(1)}) fusion(bf16[1,2048,4,256]{3,2,1,0:T(4,128)(2,1)} %get-tuple-element.85, bf16[1,2048,4,256]{3,2,1,0:T(4,128)(2,1)} %get-tuple-element.84), kind=kLoop, calls=%fused_computation.16 | loop fusion | bytes 16777216 | tf_op jit(solution)/shard_map/squeeze | solution.py:83
  90.2 2.0 copy-done.2
  92.2 2.3 slice_convert_fusion.1
  94.5 5.4 copy.85
  99.8 3.9 slice_convert_fusion
  103.7 5.4 copy.87
  109.1 0.4 reduce.3
  110.0 116.6 %all-reduce.5.cloned.1.call-done = (f32[2,32,128]{2,1,0:T(8,128)}, f32[8]{0:T(128)}, f32[8,1024]{1,0:T(8,128)}) async-done(((f32[2,32,128]{2,1,0:T(8,128)}, f32[8]{0:T(128)}, f32[8,1024]{1,0:T(8,128)}), (f32[2,32,128]{2,1,0:T(8,128)}, f32[8]{0:T(128)}, f32[8,1024]{1,0:T(8,128)})) %all-reduce.5.cloned.1.call-update) | async-done | bytes 65584 | tf_op jit(solution)/shard_map/psum | solution.py:68
  226.6 0.6 add_rsqrt_fusion
  227.2 0.8 multiply_convert_fusion.1
  228.1 0.8 broadcast_multiply_fusion
  228.8 175.6 %all-reduce.7.cloned.1.call-done = (f32[2,32,128,128]{3,2,1,0:T(8,128)}, f32[8,4096]{1,0:T(8,128)}) async-done(((f32[2,32,128,128]{3,2,1,0:T(8,128)}, f32[8,4096]{1,0:T(8,128)}), (f32[2,32,128,128]{3,2,1,0:T(8,128)}, f32[8,4096]{1,0:T(8,128)})) %all-reduce.7.cloned.1.call-update) | async-done | bytes 4325392 | tf_op jit(solution)/shard_map/psum | solution.py:68
  404.4 1.0 fusion.58
  405.4 3.6 multiply_subtract_fusion
  409.1 0.5 fusion.97
  409.5 1.7 copy-done.3
  411.2 1.3 copy-done.6
  412.5 16.4 %fusion.4 = f32[2048,4,8]{0,2,1:T(8,128)S(1)} fusion(f32[4,8,128,128]{3,2,1,0:T(8,128)S(1)} %bitcast.184, f32[2048,4,128]{0,2,1:T(8,128)S(1)} %copy-done.6, bf16[2048,4,256]{2,0,1:T(8,128)(2,1)S(1)} %copy-done.3), kind=kOutput, calls=%fused_computation.11 | convolution fusion | flops 12901613568 | bytes 8650752 | tf_op jit(solution)/shard_map/nkd,kgde->nkge/dot_general | solution.py:29
  428.9 4.7 convert_bitcast_fusion
  433.7 1.2 fusion.15
  434.9 2.4 copy.81
  437.3 0.9 fusion.100
  438.2 1.0 copy-done
  439.2 1.2 fusion.25
  440.5 3.4 fusion.99
  443.9 18.3 %fusion.3 = f32[2048,4,8]{0,2,1:T(8,128)S(1)} fusion(f32[4,8,128,128]{3,2,1,0:T(8,128)S(1)} %bitcast.183, f32[2048,4,128]{0,2,1:T(8,128)} %copy.87, bf16[2048,4,256]{2,0,1:T(8,128)(2,1)} %get-tuple-element.101), kind=kOutput, calls=%fused_computation.9 | convolution fusion | flops 12901613568 | bytes 8650752 | tf_op jit(solution)/shard_map/nkd,kgde->nkge/dot_general | solution.py:29
  462.2 1.8 fusion.98
  464.1 0.6 fusion.46
  464.8 0.6 fusion.45
  465.6 0.6 copy.89
  466.2 4.6 all-to-all-start.1
  471.0 7.2 %all-to-all-done.1 = bf16[16,4,128]{2,1,0:T(4,128)(2,1)S(1)} async-done(((bf16[16,4,128]{2,1,0:T(4,128)(2,1)}), bf16[16,4,128]{2,1,0:T(4,128)(2,1)S(1)}, u32[]{:S(2)}, u32[]{:S(2)}) %all-to-all-start.1) | async-done | bytes 16416 | tf_op jit(solution)/shard_map/all_to_all | solution.py:107
  478.6 0.6 reshape.158
  479.5 36.8 %all-gather.1 = f32[32,4,32]{2,1,0:T(4,128)S(1)} all-gather(f32[2,4,32]{2,1,0:T(4,128)S(1)} %fusion.48), channel_id=3, replica_groups=mesh['ctx'=16,'head'=2] {'ctx'}, dimensions={0}, use_global_device_ids=true | all-gather | bytes 17408 | tf_op jit(solution)/shard_map/all_gather | solution.py:19
  516.3 37.2 %all-gather = f32[32,4,32]{2,1,0:T(4,128)S(1)} all-gather(f32[2,4,32]{2,1,0:T(4,128)S(1)} %get-tuple-element.97), channel_id=2, replica_groups=mesh['ctx'=16,'head'=2] {'ctx'}, dimensions={0}, use_global_device_ids=true | all-gather | bytes 17408 | tf_op jit(solution)/shard_map/all_gather | solution.py:19
  553.5 7.4 %copy.96 = bf16[2,1024,4,256]{3,2,1,0:T(4,128)(2,1)} copy(bf16[2,1024,4,256]{3,1,2,0:T(8,128)(2,1)} %bitcast.180) | data formatting | bytes 8388608
  561.0 1.8 slice.114
  562.8 3.2 while.14
  566.3 2.8 fusion.104
  569.1 3.4 psum.47
  572.5 0.6 reshape.166
  (96 shorter events, 6.2 us)
Async XLA Ops:
  9.7 59.3 %all-to-all-start.2 = ((s32[16,1,1]{2,1,0:T(1,128)}), s32[16,1,1]{2,1,0:T(1,128)S(1)}, u32[]{:S(2)}, u32[]{:S(2)}) async-start(s32[16,1,1]{2,1,0:T(1,128)} %copy.92), calls=%async_computation.2 | async-start | bytes 16384 | tf_op jit(solution)/shard_map/all_to_all | solution.py:110
  61.1 2.3 copy-start.4
  68.9 7.3 %copy-start.9 = (bf16[4,2,512]{2,1,0:T(2,128)(2,1)S(1)}, bf16[4,2,512]{2,1,0:T(2,128)(2,1)}, u32[]{:S(2)}) copy-start(bf16[4,2,512]{2,1,0:T(2,128)(2,1)} %param.14) | copy-start | bytes 24580
  68.9 7.4 %copy-start.8 = (bf16[512,4,256]{2,1,0:T(4,128)(2,1)S(1)}, bf16[512,4,256]{2,1,0:T(4,128)(2,1)}, u32[]{:S(2)}) copy-start(bf16[512,4,256]{2,1,0:T(4,128)(2,1)} %param.16) | copy-start | bytes 3145732
  68.9 7.6 %copy-start.7 = (bf16[2,16,4096]{2,1,0:T(8,128)(2,1)S(1)}, bf16[2,16,4096]{2,1,0:T(8,128)(2,1)}, u32[]{:S(2)}) copy-start(bf16[2,16,4096]{2,1,0:T(8,128)(2,1)} %param.13) | copy-start | bytes 786436
  69.0 360.0 %all-to-all-start = ((bf16[16,128,4,256]{3,2,1,0:T(4,128)(2,1)}), bf16[16,128,4,256]{3,2,1,0:T(4,128)(2,1)}, u32[]{:S(2)}, u32[]{:S(2)}) async-start(bf16[16,128,4,256]{3,2,1,0:T(4,128)(2,1)} %copy.78), calls=%async_computation | async-start | bytes 8388608 | tf_op jit(solution)/shard_map/all_to_all | solution.py:106
  76.1 150.6 %all-reduce.5.cloned.1.call-start = ((), (), s32[]{:S(2)}) async-start(), calls=%async_computation.4 | async-start | bytes 132096 | tf_op jit(solution)/shard_map/psum | solution.py:68
  78.9 325.6 %all-reduce.7.cloned.1.call-start = ((), (), s32[]{:S(2)}) async-start(), calls=%async_computation.5 | async-start | bytes 8650752 | tf_op jit(solution)/shard_map/psum | solution.py:68
  78.9 3.4 copy-start.5
  83.6 477.4 %all-gather.5.cloned.1.call-start = ((), (), s32[]{:S(2)}) async-start(), calls=%async_computation.3 | async-start | bytes 2228224 | tf_op jit(solution)/shard_map/all_gather | solution.py:19
  90.2 2.0 copy-start.2
  409.0 2.2 copy-start.3
  409.0 3.5 copy-start.6
  437.3 1.9 copy-start
  443.9 18.3 %copy-start.1 = (bf16[2048,4,256]{2,0,1:T(8,128)(2,1)S(1)}, bf16[2048,4,256]{2,0,1:T(8,128)(2,1)}, u32[]{:S(2)}) copy-start(bf16[2048,4,256]{2,0,1:T(8,128)(2,1)} %get-tuple-element.101) | copy-start | bytes 12582916
  466.2 12.1 %all-to-all-start.1 = ((bf16[16,4,128]{2,1,0:T(4,128)(2,1)}), bf16[16,4,128]{2,1,0:T(4,128)(2,1)S(1)}, u32[]{:S(2)}, u32[]{:S(2)}) async-start(bf16[16,4,128]{2,1,0:T(4,128)(2,1)} %copy.89), calls=%async_computation.1 | async-start | bytes 32768 | tf_op jit(solution)/shard_map/all_to_all | solution.py:107
  561.0 1.8 slice-start
Sparse Core Ops, SparseCore 0:
  83.4 143.2 all-reduce.4
  232.3 172.0 all-reduce.6
  440.6 60.6 all-gather.4
where the time goes:
time: 590 us; the launch traced here: 580 us
  waiting for transfers between devices  299 us (51%)
  local copies, waits for them, and re-layouts  81.9 us (14%)
  blocking collectives  77.4 us (13%)
  matrix products  67.7 us (11%)
  starting transfers between devices  20.4 us (3%)
  other arithmetic  18.5 us (3%)
  between operations  14.6 us (2%)
    psum x2, waiting for transfers between devices, per_device(): second, summed = lax.psum((second, summed), 'ctx')  292 us
    all_gather x2, blocking collectives, joined(): pieces = jax.tree.map(lambda part: lax.all_gather(part, axis), value)  74 us
    dot_general x2, matrix products, group_scores(): turned = jnp.einsum('nkd,kgde->nkge', lifted, cov_q, precision=HIGHEST)  34.7 us
    unnamed x26, local copies, waits for them, and re-layouts  15.6 us
    another operation x2, local copies, waits for them, and re-layouts, per_device(): spans = kv_cache[request].reshape(lists, span, local_kv * pair)  15.4 us
    reshape x4, local copies, waits for them, and re-layouts, per_device(): chosen = chosen.reshape(lists, width, local_kv, pair)  12.5 us
  transfers between devices with their start and end apart: 6, of which 3 were waited for; matrix products, arithmetic and copies ran while one was open for 24% of the time, Pallas kernels for 0%

commit v1 on v0

--- a/solution.py
+++ b/solution.py
@@ -3,18 +3,410 @@
 import jax
 import jax.numpy as jnp
 from jax import lax
+from jax.experimental import pallas as pl
+from jax.experimental.pallas import tpu as pltpu
 from jax.sharding import PartitionSpec as P
 
 D = 8192
 H = 64
-KVH = 8
 QS = 256
-
-
+EPSILON = 1e-05
 HIGHEST = lax.Precision.HIGHEST
-EPSILON = 1e-05
-
-
+BF = jnp.bfloat16
+F32 = jnp.float32
+STAT = 144
+LARGE = 1e30
+VMEM_LIMIT = 48 << 20
+ANY = pl.BlockSpec(memory_space=pl.ANY)
+SMEM = pl.BlockSpec(memory_space=pltpu.SMEM)
+VMEM = pl.BlockSpec(memory_space=pltpu.VMEM)
+NT = (((1,), (1,)), ((), ()))
+TN = (((0,), (0,)), ((), ()))
+
+
+def params():
+    return pltpu.CompilerParams(vmem_limit_bytes=VMEM_LIMIT)
+
+
+def pack_kernel(keep, target, kv, send, spans, blocks, in_sem, out_sem):
+    items, width = keep.shape
+    span = 2 * width
+    lists = items // kv.shape[0]
+
+    def fetch(m):
+        return pltpu.make_async_copy(
+            kv.at[m // lists, pl.ds((m % lists) * span, span)], spans.at[m, pl.ds(0, span)], in_sem.at[m]
+        )
+
+    def put(m):
+        return pltpu.make_async_copy(blocks.at[m], send.at[target[m, 0]], out_sem.at[m])
+
+    for m in range(items):
+        fetch(m).start()
+        spans[m, span] = jnp.zeros(spans.shape[2:], spans.dtype)
+
+    def one(m, carry):
+        fetch(m).wait()
+
+        def rows(j, inner):
+            for u in range(16):
+                at = j * 16 + u
+                blocks[m, at] = spans[m, keep[m, at]]
+            return inner
+
+        lax.fori_loop(0, width // 16, rows, 0)
+        put(m).start()
+        return carry
+
+    lax.fori_loop(0, items, one, 0)
+    for m in range(items):
+        put(m).wait()
+
+
+def pack(kv_cache, keep, target):
+    items, width = keep.shape
+    tail = kv_cache.shape[2:]
+    return pl.pallas_call(
+        pack_kernel,
+        out_shape=jax.ShapeDtypeStruct((items, width, *tail), kv_cache.dtype),
+        in_specs=[SMEM, SMEM, ANY],
+        out_specs=ANY,
+        scratch_shapes=[
+            pltpu.VMEM((items, 2 * width + 8, *tail), kv_cache.dtype),
+            pltpu.VMEM((items, width, *tail), kv_cache.dtype),
+            pltpu.SemaphoreType.DMA((items,)),
+            pltpu.SemaphoreType.DMA((items,)),
+        ],
+        compiler_params=params(),
+        name="pack_rows",
+    )(keep, target, kv_cache)
+
+
+def project_kernel(tokens, wq, wkv, out):
+    i = pl.program_id(0)
+    x = tokens[...]
+    part = jnp.dot(x, wq[...], preferred_element_type=F32)
+    for r in range(2):
+        for g in range(8):
+            out[r * 8 + i * 2 + g // 4, (g % 4) * 4 : (g % 4) * 4 + 4, :] = part[
+                r * 4 : r * 4 + 4, g * 128 : g * 128 + 128
+            ]
+
+    @pl.when(i == 0)
+    def _():
+        heads = pltpu.einshape("nhd->hnd", wkv[...])
+        wide = x.astype(F32)
+        squares = jnp.sum(wide * wide, axis=1, keepdims=True)
+        row = lax.broadcasted_iota(jnp.int32, (8, 128), 0)
+        lane = lax.broadcasted_iota(jnp.int32, (8, 128), 1)
+        line = jnp.sum(jnp.where(row == lane, squares, 0.0), axis=0, keepdims=True)
+        line = jnp.concatenate([line, jnp.zeros((3, 128), F32)], axis=0)
+        for p in range(16):
+            out[p, 20:24, :] = line
+        for j in range(4):
+            pair = jnp.dot(x, heads[j], preferred_element_type=F32)
+            for r in range(2):
+                for half in range(2):
+                    out[r * 8 + j * 2 + half, 16:20, :] = pair[
+                        r * 4 : r * 4 + 4, half * 128 : half * 128 + 128
+                    ]
+
+
+def project(tokens, w_query, w_keyval):
+    depth, columns = w_query.shape
+    step = columns // 4
+    return pl.pallas_call(
+        project_kernel,
+        out_shape=jax.ShapeDtypeStruct((16, 24, 128), F32),
+        grid=(4,),
+        in_specs=[
+            pl.BlockSpec((8, depth), lambda i: (0, 0)),
+            pl.BlockSpec((depth, step), lambda i: (0, i)),
+            pl.BlockSpec(w_keyval.shape, lambda i: (0, 0, 0)),
+        ],
+        out_specs=pl.BlockSpec((16, 24, 128), lambda i: (0, 0, 0)),
+        compiler_params=params(),
+        name="project_tokens",
+    )(tokens, w_query, w_keyval)
+
+
+def normalize_kernel(place, parts, out):
+    total = jnp.sum(parts[...], axis=0)
+    request = place[0] // 8
+    row = lax.broadcasted_iota(jnp.int32, (24, 128), 0)
+    lane = lax.broadcasted_iota(jnp.int32, (24, 128), 1)
+    squares = jnp.where(lane == request * 4 + row % 4, total[20:21, :], 0.0)
+    inverse = lax.rsqrt(jnp.sum(squares, axis=1, keepdims=True) / D + EPSILON)
+    scaled = jnp.where(row < 20, total * inverse, 0.0)
+    rounded = jnp.concatenate([scaled, jnp.zeros((8, 128), F32)], axis=0).astype(BF)
+    out[...] = jnp.broadcast_to(rounded[None], out.shape)
+
+
+def normalize(place, parts):
+    return pl.pallas_call(
+        normalize_kernel,
+        out_shape=jax.ShapeDtypeStruct((16, 32, 128), BF),
+        in_specs=[SMEM, VMEM],
+        out_specs=VMEM,
+        compiler_params=params(),
+        name="normalize_tokens",
+    )(place, parts)
+
+
+def attend_kernel(target, query, bias, send, out, rows, logits, sem):
+    items = rows.shape[0]
+    width = rows.shape[1]
+    wide = width * 4
+
+    def fetch(m):
+        return pltpu.make_async_copy(send.at[target[m, 0]], rows.at[m], sem.at[m])
+
+    for m in range(items):
+        fetch(m).start()
+    head = lax.broadcasted_iota(jnp.int32, (128, wide), 0) // 32
+    lane = lax.broadcasted_iota(jnp.int32, (128, wide), 1) % 4
+    own = head == lane
+    for r in range(2):
+        q = query[r * 8 : r * 8 + 8, 0:16, :].reshape(128, 128)
+        for b in range(8):
+            m = r * 8 + b
+            fetch(m).wait()
+            keys = rows[m, :, :, 0:128].reshape(wide, 128)
+            scores = lax.dot_general(q, keys, NT, preferred_element_type=F32) / math.sqrt(128)
+            scores = jnp.where(own, scores, -LARGE) + bias[m : m + 1, :]
+            logits[:, b * wide : b * wide + wide] = scores
+        top = jnp.max(logits[...], axis=1, keepdims=True)
+        total = jnp.zeros((128, 1), F32)
+        weighted = jnp.zeros((128, 128), F32)
+        for b in range(8):
+            weights = jnp.exp(logits[:, b * wide : b * wide + wide] - top)
+            total = total + jnp.sum(weights, axis=1, keepdims=True)
+            values = rows[r * 8 + b, :, :, 128:256].reshape(wide, 128)
+            weighted = weighted + jnp.dot(weights.astype(BF), values, preferred_element_type=F32)
+        top_line = jnp.broadcast_to(top, (128, 128)).T[0:1, :]
+        total_line = jnp.broadcast_to(total, (128, 128)).T[0:1, :]
+        lines = jnp.concatenate([top_line, total_line, jnp.zeros((6, 128), F32)], axis=0)
+        for i in range(8):
+            out[r * 8 + i, 0:16, :] = weighted[i * 16 : i * 16 + 16, :]
+            out[r * 8 + i, 16:24, :] = lines
+
+
+def attend(target, query, bias, send):
+    items, width = send.shape[:2]
+    return pl.pallas_call(
+        attend_kernel,
+        out_shape=jax.ShapeDtypeStruct((16, 24, 128), F32),
+        in_specs=[SMEM, VMEM, VMEM, ANY],
+        out_specs=VMEM,
+        scratch_shapes=[
+            pltpu.VMEM(send.shape, send.dtype),
+            pltpu.VMEM((128, 8 * width * 4), F32),
+            pltpu.SemaphoreType.DMA((items,)),
+        ],
+        compiler_params=params(),
+        name="attend_kept",
+    )(target, query, bias, send)
+
+
+def combine_kernel(place, parts, query, out):
+    p = place[0]
+    mine = query[p, 0:16, :]
+    pair = (p // 2) * 2
+    fresh_key = query[pair, 16:32, :]
+    fresh_value = query[pair + 1, 16:32, :]
+    recent = lax.dot_general(mine, fresh_key, NT, preferred_element_type=F32) / math.sqrt(128)
+    step = lax.broadcasted_iota(jnp.int32, (16, 16), 0) % 4
+    column = lax.broadcasted_iota(jnp.int32, (16, 16), 1)
+    recent = jnp.where(column <= step, recent, -LARGE)
+    row = lax.broadcasted_iota(jnp.int32, (16, 128), 0)
+    lane = lax.broadcasted_iota(jnp.int32, (16, 128), 1)
+    chosen = lane == (p % 8) * 16 + row
+    tops, totals = [], []
+    for s in range(16):
+        tops.append(jnp.sum(jnp.where(chosen, parts[s, 16:17, :], 0.0), axis=1, keepdims=True))
+        totals.append(jnp.sum(jnp.where(chosen, parts[s, 17:18, :], 0.0), axis=1, keepdims=True))
+    best = jnp.max(recent, axis=1, keepdims=True)
+    for s in range(16):
+        best = jnp.maximum(best, tops[s])
+    weights = jnp.exp(recent - best)
+    total = jnp.sum(weights, axis=1, keepdims=True)
+    weighted = jnp.dot(weights.astype(BF), fresh_value, preferred_element_type=F32)
+    for s in range(16):
+        factor = jnp.exp(tops[s] - best)
+        total = total + totals[s] * factor
+        weighted = weighted + parts[s, 0:16, :] * factor
+    out[...] = jnp.broadcast_to((weighted / total).astype(BF)[None], out.shape)
+
+
+def combine(place, parts, query):
+    return pl.pallas_call(
+        combine_kernel,
+        out_shape=jax.ShapeDtypeStruct((16, 16, 128), BF),
+        in_specs=[SMEM, VMEM, VMEM],
+        out_specs=VMEM,
+        compiler_params=params(),
+        name="combine_parts",
+    )(place, parts, query)
+
+
+def moments_kernel(samples, out):
+    for i in range(4):
+        q = samples[:, i * 128 : i * 128 + 128]
+        second = lax.dot_general(q, q, TN, preferred_element_type=F32)
+        mean = jnp.sum(q.astype(F32), axis=0, keepdims=True) / QS
+        first = jnp.concatenate([mean, jnp.zeros((7, 128), F32)], axis=0)
+        outer = lax.dot_general(first, first, TN, preferred_element_type=F32, precision=HIGHEST)
+        cov = second / QS - outer
+        scaled = mean / math.sqrt(128)
+        high = scaled.astype(BF).astype(F32)
+        low = scaled - high
+        lines = jnp.concatenate([high, low, jnp.zeros((14, 128), F32)], axis=0)
+        out[i, 0:128, :] = cov.astype(BF)
+        out[i, 128:144, :] = lines.astype(BF)
+
+
+def head_moments(samples):
+    return pl.pallas_call(
+        moments_kernel,
+        out_shape=jax.ShapeDtypeStruct((4, STAT, 128), BF),
+        in_specs=[VMEM],
+        out_specs=VMEM,
+        compiler_params=params(),
+        name="moments",
+    )(samples)
+
+
+def reverse_bits(value, order):
+    place = 0
+    for at, bit in enumerate(order):
+        place = place + ((value // bit) % 2) * (1 << at)
+    return place
+
+
+def score_kernel(orders, place, target, arrived, stat_a, stat_b, packed, scores, blocks, stats, in_sem, out_sem, a_sem, b_sem):
+    items = blocks.shape[0]
+    lists = items // 2
+    me = place[0]
+
+    def at(m):
+        return (m // lists) * lists + target[m, 1]
+
+    def fetch(m):
+        source = (2 * me - target[m, 0] + 16) % 16
+        return pltpu.make_async_copy(arrived.at[source], blocks.at[at(m)], in_sem.at[m])
+
+    def put(m):
+        return pltpu.make_async_copy(blocks.at[m], packed.at[m], out_sem.at[m])
+
+    def take(o, half, stat, sem):
+        index = reverse_bits(jnp.bitwise_xor(me, o), orders[half])
+        return pltpu.make_async_copy(stat.at[index], stats.at[o, pl.ds(half * 2, 2)], sem.at[o])
+
+    for m in range(items):
+        fetch(m).start()
+    for o in range(16):
+        take(o, 0, stat_a, a_sem).start()
+        take(o, 1, stat_b, b_sem).start()
+    for m in range(items):
+        fetch(m).wait()
+    for m in range(items):
+        put(m).start()
+    for o in range(16):
+        take(o, 0, stat_a, a_sem).wait()
+        take(o, 1, stat_b, b_sem).wait()
+    for r in range(2):
+        for j in range(4):
+            first = r * 8 + j * 2
+            table = stats[first : first + 2].reshape(8 * STAT, 128)
+            for c in range(4):
+                keys = blocks[r * 8 + c * 2 : r * 8 + c * 2 + 2, :, j, 0:128].reshape(256, 128)
+                turned = lax.dot_general(table, keys, NT, preferred_element_type=F32)
+                flipped = keys.astype(F32).T
+                lines = []
+                for g in range(8):
+                    base = g * STAT
+                    quadratic = jnp.sum(turned[base : base + 128] * flipped, axis=0, keepdims=True)
+                    linear = turned[base + 128 : base + 129] + turned[base + 129 : base + 130]
+                    lines.append(linear + quadratic / 256.0)
+                logit = jnp.concatenate(lines, axis=0)
+                top = jnp.max(logit, axis=0, keepdims=True)
+                mean = jnp.sum(jnp.exp(logit - top), axis=0, keepdims=True) / 8.0
+                scores[r, j : j + 1, c * 256 : c * 256 + 256] = top + jnp.log(mean)
+    for m in range(items):
+        put(m).wait()
+
+
+def score(orders, place, target, arrived, stat_a, stat_b):
+    items, width = arrived.shape[:2]
+
+    def kernel(*refs):
+        score_kernel(orders, *refs)
+
+    return pl.pallas_call(
+        kernel,
+        out_shape=(
+            jax.ShapeDtypeStruct(arrived.shape, arrived.dtype),
+            jax.ShapeDtypeStruct((2, 4, items // 2 * width), F32),
+        ),
+        in_specs=[SMEM, SMEM, ANY, ANY, ANY],
+        out_specs=(ANY, VMEM),
+        scratch_shapes=[
+            pltpu.VMEM(arrived.shape, arrived.dtype),
+            pltpu.VMEM((16, 4, STAT, 128), BF),
+            pltpu.SemaphoreType.DMA((items,)),
+            pltpu.SemaphoreType.DMA((items,)),
+            pltpu.SemaphoreType.DMA((16,)),
+            pltpu.SemaphoreType.DMA((16,)),
+        ],
+        compiler_params=params(),
+        name="place_and_score",
+    )(place, target, arrived, stat_a, stat_b)
+
+
+def exchange(value):
+    return lax.all_to_all(value, "ctx", split_axis=0, concat_axis=0, tiled=True)
+
+
+def doubled(value, order):
+    value = value[None]
+    for bit in order:
+        pairs = [(i, i ^ bit) for i in range(16)]
+        value = jnp.concatenate([value, lax.ppermute(value, "ctx", pairs)], axis=0)
+    return value
+
+
+def sixteen(
+    kv_cache, keep_rows, block_target, future_queries, new_tokens, w_query, w_keyval, w_out
+):
+    requests, cache_rows, local_kv, pair = kv_cache.shape
+    lists, width = keep_rows.shape[1:]
+    items = requests * lists
+    keep = keep_rows.reshape(items, width)
+    target = block_target.reshape(items, 2)
+    place = lax.axis_index("ctx").astype(jnp.int32).reshape(1)
+    tokens = jnp.transpose(new_tokens, (1, 0, 2)).reshape(8, new_tokens.shape[2])
+    samples = future_queries.reshape(2, 16, 8, 512)
+    samples = jnp.transpose(samples, (0, 2, 1, 3)).reshape(16, 16, 512)
+    samples = exchange(samples).reshape(256, 512)
+    parts = exchange(project(tokens, w_query, w_keyval))
+    send = pack(kv_cache, keep, target)
+    bias = jnp.where(keep < 2 * width, 0.0, -LARGE).astype(F32)
+    bias = jnp.broadcast_to(bias[:, :, None], (items, width, 4)).reshape(items, width * 4)
+    query = exchange(normalize(place, parts))
+    stat = head_moments(samples)
+    orders = ((8, 4, 2, 1), (8, 4, 1, 2))
+    stat_a = doubled(stat[:2], orders[0])
+    stat_b = doubled(stat[2:], orders[1])
+    joined = exchange(attend(target, query, bias, send))
+    attended = exchange(combine(place, joined, query))
+    send, attended = lax.optimization_barrier((send, attended))
+    arrived = exchange(send)
+    packed, scores = score(orders, place, target, arrived, stat_a, stat_b)
+    rows = attended.reshape(requests, 32, 4, 128)
+    rows = jnp.transpose(rows, (2, 0, 1, 3)).reshape(8, 4096)
+    partial_value = jnp.dot(rows, w_out, preferred_element_type=F32)
+    decoded = lax.psum(partial_value, "head").astype(BF).reshape(4, requests, w_out.shape[1])
+    return packed.reshape(requests, lists * width, local_kv, pair), scores, decoded
 def joined(value, axis, join):
     pieces = jax.tree.map(lambda part: lax.all_gather(part, axis), value)
     head = jax.tree.map(lambda part: part[0], pieces)
@@ -50,6 +442,9 @@
     second = jnp.einsum("rshd,rshe->rhde", sample, sample, preferred_element_type=jnp.float32)
     summed = jnp.sum(sample.astype(jnp.float32), axis=1)
     return (second, summed)
+
+
+KVH = 8
 
 
 def per_device(
@@ -223,6 +618,7 @@
         P("head", "ctx"),
     )
     out_specs = (P(None, "ctx", "head", None), P(None, "head", "ctx"), P(None, None, "ctx"))
+    body = sixteen if mesh.shape["ctx"] == 16 and mesh.shape["head"] == 2 else per_device
     return jax.shard_map(
-        per_device, mesh=mesh, in_specs=in_specs, out_specs=out_specs, check_vma=False
-    )
+        body, mesh=mesh, in_specs=in_specs, out_specs=out_specs, check_vma=False
+    )

time: 590 us -> 237 us (0.40); the launches traced: 580 us -> 236 us
  waiting for transfers between devices: 299 us -> 135 us
  blocking collectives: 77.4 us -> 4 us
  local copies, waits for them, and re-layouts: 81.9 us -> 12.2 us
  matrix products: 67.7 us -> 1.26 us
  Pallas kernels: 0 us -> 38.9 us
  starting transfers between devices: 20.4 us -> 42.6 us
  other arithmetic: 18.5 us -> 1.06 us
  between operations: 14.6 us -> 1.04 us
    psum x2 -> x0, waiting for transfers between devices: 292 us -> none  [per_device(): second, summed = lax.psum((second, summed), 'ctx')]
    ppermute x0 -> x8, waiting for transfers between devices: none -> 103 us  [doubled(): value = jnp.concatenate([value, lax.ppermute(value, 'ctx', pairs)], axis=0)]
    all_gather x2 -> x0, blocking collectives: 74 us -> none  [joined(): pieces = jax.tree.map(lambda part: lax.all_gather(part, axis), value)]
    dot_general x22 -> x1, matrix products: 67.7 us -> 1.26 us  [sixteen(): partial_value = jnp.dot(rows, w_out, preferred_element_type=F32)]
    pallas_call x0 -> x7, Pallas kernels: none -> 38.9 us  [the longest x1 18.4 us: score(): pl.pallas_call(kernel, out_shape=(jax.ShapeDtypeStruct(arrived.shape, arr...]
    all_to_all x3 -> x6, waiting for transfers between devices: 7.25 us -> 31.8 us  [exchange(): return lax.all_to_all(value, 'ctx', split_axis=0, concat_axis=0, tiled=True)]
    convert_element_type x5 -> x0, local copies, waits for them, and re-layouts: 17.9 us -> none  [the longest x2 10.8 us: group_scores(): lifted = keys.astype(jnp.float32)]
    another operation x2 -> x0, local copies, waits for them, and re-layouts: 15.4 us -> none  [per_device(): spans = kv_cache[request].reshape(lists, span, local_kv * pair)]
  transfers between devices with their start and end apart: 6 -> 14, of which waited for: 3 -> 12; matrix products, arithmetic and copies ran while one was open for 24% -> 2% of each run, Pallas kernels for 0% -> 4%
where the time goes in v1:
time: 237 us; the launch traced here: 236 us
  waiting for transfers between devices  135 us (57%)
  starting transfers between devices  42.6 us (18%)
  Pallas kernels  38.9 us (16%)
  local copies, waits for them, and re-layouts  12.2 us (5%)
  blocking collectives  4 us (2%)
    ppermute x8, waiting for transfers between devices, doubled(): value = jnp.concatenate([value, lax.ppermute(value, 'ctx', pairs)], axis=0)  103 us
    all_to_all x6, waiting for transfers between devices, exchange(): return lax.all_to_all(value, 'ctx', split_axis=0, concat_axis=0, tiled=True)  31.8 us
    all_to_all x6, starting transfers between devices, exchange(): return lax.all_to_all(value, 'ctx', split_axis=0, concat_axis=0, tiled=True)  30.3 us
    pallas_call x1, Pallas kernels, score(): pl.pallas_call(kernel, out_shape=(jax.ShapeDtypeStruct(arrived.shape, arr...  18.4 us
    ppermute x8, starting transfers between devices, doubled(): value = jnp.concatenate([value, lax.ppermute(value, 'ctx', pairs)], axis=0)  12.3 us
    pallas_call x1, Pallas kernels, pack(): pl.pallas_call(pack_kernel, out_shape=jax.ShapeDtypeStruct((items, width,...  9.3 us
    unnamed x28, local copies, waits for them, and re-layouts  8.5 us
    pallas_call x1, Pallas kernels, attend(): pl.pallas_call(attend_kernel, out_shape=jax.ShapeDtypeStruct((16, 24, 128...  6.52 us
  transfers between devices with their start and end apart: 14, of which 12 were waited for; matrix products, arithmetic and copies ran while one was open for 2% of the time, Pallas kernels for 4%

profile of v1, /device:TPU:0, one launch (start us, length us, event | category | flops | bytes accessed | tf_op | source)
XLA Modules:
  0.0 235.8 jit_solution(16642537178042784993)
XLA Ops:
  0.6 0.7 copy.19
  1.3 0.0 copy-start.2
  1.4 2.2 copy-done.2
  3.5 0.0 copy-start.3
  3.5 1.2 copy-done.3
  4.8 0.0 copy-start.9
  4.8 0.0 copy-start.4
  4.8 2.4 %project_tokens.1 = f32[16,24,128]{2,1,0:T(8,128)} custom-call(bf16[8,512]{1,0:T(8,128)(2,1)S(1)} %reshape.51.tokens, bf16[512,4096]{1,0:T(8,128)(2,1)S(1)} %copy-done.2, bf16[512,4,256]{2,1,0:T(4,128)(2,1)S(1)} %copy-done.3), custom_call_target="tpu_custom_call" | custom-call | tf_op jit(solution)/shard_map/project_tokens/pallas_call | solution.py:118
  7.2 8.3 %all-to-all-start = ((f32[16,24,128]{2,1,0:T(8,128)}), f32[16,24,128]{2,1,0:T(8,128)S(1)}, u32[]{:S(2)}, u32[]{:S(2)}) async-start(f32[16,24,128]{2,1,0:T(8,128)} %project_tokens.1), calls=%async_computation | async-start | bytes 393216 | tf_op jit(solution)/shard_map/all_to_all | solution.py:367
  15.5 8.6 %all-to-all-done.parts = f32[16,24,128]{2,1,0:T(8,128)S(1)} async-done(((f32[16,24,128]{2,1,0:T(8,128)}), f32[16,24,128]{2,1,0:T(8,128)S(1)}, u32[]{:S(2)}, u32[]{:S(2)}) %all-to-all-start) | async-done | bytes 196640 | tf_op jit(solution)/shard_map/all_to_all | solution.py:367
  24.1 0.8 normalize_tokens.1
  24.9 3.5 %all-to-all-start.1 = ((bf16[16,32,128]{2,1,0:T(8,128)(2,1)}), bf16[16,32,128]{2,1,0:T(8,128)(2,1)S(1)}, u32[]{:S(2)}, u32[]{:S(2)}) async-start(bf16[16,32,128]{2,1,0:T(8,128)(2,1)} %normalize_tokens.1), calls=%async_computation.1 | async-start | bytes 262144 | tf_op jit(solution)/shard_map/all_to_all | solution.py:367
  28.4 0.0 copy-done.9
  28.4 0.1 copy.26
  28.5 0.0 copy-done.4
  28.5 0.1 copy.20
  28.7 0.1 copy.22.bias
  28.8 9.3 %pack_rows.1.send = bf16[16,128,4,256]{3,2,1,0:T(4,128)(2,1)S(1)} custom-call(s32[16,128]{1,0:T(8,128)S(1)} %bitcast.37, s32[16,2]{1,0:T(8,128)S(1)} %bitcast.34, bf16[2,2048,4,256]{3,2,1,0:T(4,128)(2,1)} %kv.1), custom_call_target="tpu_custom_call" | custom-call | tf_op jit(solution)/shard_map/pack_rows/pallas_call | solution.py:69
  38.1 0.0 copy-start
  38.1 2.0 copy-done
  40.1 0.0 all-to-all-done.1.query
  40.1 0.0 copy-start.1
  40.1 2.2 copy-done.1
  42.3 6.5 %attend_kept.1 = f32[16,24,128]{2,1,0:T(8,128)} custom-call(s32[16,2]{1,0:T(8,128)S(1)} %bitcast.35, bf16[16,32,128]{2,1,0:T(8,128)(2,1)S(1)} %all-to-all-done.1.query, f32[16,512]{1,0:T(8,128)S(1)} %copy.22.bias, bf16[16,128,4,256]{3,2,1,0:T(4,128)(2,1)S(1)} %copy-done.1), custom_call_target="tpu_custom_call" | custom-call | tf_op jit(solution)/shard_map/attend_kept/pallas_call | solution.py:196
  48.8 6.9 %all-to-all-start.2 = ((f32[16,24,128]{2,1,0:T(8,128)}), f32[16,24,128]{2,1,0:T(8,128)S(1)}, u32[]{:S(2)}, u32[]{:S(2)}) async-start(f32[16,24,128]{2,1,0:T(8,128)} %attend_kept.1), calls=%async_computation.2 | async-start | bytes 393216 | tf_op jit(solution)/shard_map/all_to_all | solution.py:367
  55.7 0.0 copy-done.6
  55.7 0.1 copy.28
  55.8 8.0 %all-to-all-done.2.parts = f32[16,24,128]{2,1,0:T(8,128)S(1)} async-done(((f32[16,24,128]{2,1,0:T(8,128)}), f32[16,24,128]{2,1,0:T(8,128)S(1)}, u32[]{:S(2)}, u32[]{:S(2)}) %all-to-all-start.2) | async-done | bytes 196640 | tf_op jit(solution)/shard_map/all_to_all | solution.py:367
  63.8 1.0 combine_parts.1
  64.8 3.5 %all-to-all-start.3 = ((bf16[16,16,128]{2,1,0:T(8,128)(2,1)}), bf16[16,16,128]{2,1,0:T(8,128)(2,1)S(1)}, u32[]{:S(2)}, u32[]{:S(2)}) async-start(bf16[16,16,128]{2,1,0:T(8,128)(2,1)} %combine_parts.1), calls=%async_computation.3 | async-start | bytes 131072 | tf_op jit(solution)/shard_map/all_to_all | solution.py:367
  68.3 0.8 copy.23
  69.1 6.7 %all-to-all-done.3 = bf16[16,16,128]{2,1,0:T(8,128)(2,1)S(1)} async-done(((bf16[16,16,128]{2,1,0:T(8,128)(2,1)}), bf16[16,16,128]{2,1,0:T(8,128)(2,1)S(1)}, u32[]{:S(2)}, u32[]{:S(2)}) %all-to-all-start.3) | async-done | bytes 65568 | tf_op jit(solution)/shard_map/all_to_all | solution.py:367
  75.8 0.6 copy-done.7
  76.4 3.5 %all-to-all-start.5 = ((bf16[16,16,512]{2,1,0:T(8,128)(2,1)}), bf16[16,16,512]{2,1,0:T(8,128)(2,1)S(1)}, u32[]{:S(2)}, u32[]{:S(2)}) async-start(bf16[16,16,512]{2,1,0:T(8,128)(2,1)} %bitcast.5), calls=%async_computation.5 | async-start | bytes 524288 | tf_op jit(solution)/shard_map/all_to_all | solution.py:367
  79.9 8.5 %all-to-all-done.5 = bf16[16,16,512]{2,1,0:T(8,128)(2,1)S(1)} async-done(((bf16[16,16,512]{2,1,0:T(8,128)(2,1)}), bf16[16,16,512]{2,1,0:T(8,128)(2,1)S(1)}, u32[]{:S(2)}, u32[]{:S(2)}) %all-to-all-start.5) | async-done | bytes 262176 | tf_op jit(solution)/shard_map/all_to_all | solution.py:367
  88.4 4.6 %all-to-all-start.4 = ((bf16[16,128,4,256]{3,2,1,0:T(4,128)(2,1)}), bf16[16,128,4,256]{3,2,1,0:T(4,128)(2,1)}, u32[]{:S(2)}, u32[]{:S(2)}) async-start(bf16[16,128,4,256]{3,2,1,0:T(4,128)(2,1)} %copy-done), calls=%async_computation.4 | async-start | bytes 8388608 | tf_op jit(solution)/shard_map/all_to_all | solution.py:367
  93.0 0.5 moments.1
  93.5 2.8 %collective-permute-start.4 = (bf16[1,2,144,128]{3,2,1,0:T(8,128)(2,1)S(1)}, bf16[1,2,144,128]{3,2,1,0:T(8,128)(2,1)S(1)}, u32[]{:S(2)}, u32[]{:S(2)}) collective-permute-start(bf16[1,2,144,128]{3,2,1,0:T(8,128)(2,1)S(1)} %get-tuple-element.11), channel_id=1, source_target_pairs={{0,16},{2,18},{4,20},{6,22},{8,24},{10,26},{12,28},{14,30},{16,0},... | collective-permute-start | bytes 221192 | tf_op jit(solution)/shard_map/ppermute | solution.py:374
  96.3 0.3 collective-permute-start
  96.6 90.5 %collective-permute-done.4 = bf16[1,2,144,128]{3,2,1,0:T(8,128)(2,1)S(1)} collective-permute-done((bf16[1,2,144,128]{3,2,1,0:T(8,128)(2,1)S(1)}, bf16[1,2,144,128]{3,2,1,0:T(8,128)(2,1)S(1)}, u32[]{:S(2)}, u32[]{:S(2)}) %collective-permute-start.4) | collective-permute-done | bytes 73760 | tf_op jit(solution)/shard_map/ppermute | solution.py:374
  187.1 0.1 collective-permute-start.5
  187.1 0.7 collective-permute-done
  187.9 1.4 collective-permute-start.1
  189.3 3.4 %collective-permute-done.5 = bf16[2,2,144,128]{3,2,1,0:T(8,128)(2,1)S(1)} collective-permute-done((bf16[2,2,144,128]{3,2,1,0:T(8,128)(2,1)S(1)}, bf16[2,2,144,128]{3,2,1,0:T(8,128)(2,1)S(1)}, u32[]{:S(2)}, u32[]{:S(2)}) %collective-permute-start.5) | collective-permute-done | bytes 147488 | tf_op jit(solution)/shard_map/ppermute | solution.py:374
  192.7 1.5 collective-permute-start.6
  194.2 0.1 collective-permute-done.1
  194.3 2.8 %collective-permute-start.2 = (bf16[4,2,144,128]{3,2,1,0:T(8,128)(2,1)S(1)}, bf16[4,2,144,128]{3,2,1,0:T(8,128)(2,1)S(1)}, u32[]{:S(2)}, u32[]{:S(2)}) collective-permute-start(bf16[4,2,144,128]{3,2,1,0:T(8,128)(2,1)S(1)} %pad_maximum_fusion.2), channel_id=1, source_target_pairs={{0,4},{2,6},{4,0},{6,2},{8,12},{10,14},{12,8},{14,10},{16,20},{18,... | collective-permute-start | bytes 884744 | tf_op jit(solution)/shard_map/ppermute | solution.py:374
  197.2 2.3 collective-permute-done.6
  199.5 0.1 pad_maximum_fusion.1
  199.6 2.8 %collective-permute-start.7 = (bf16[8,2,144,128]{3,2,1,0:T(8,128)(2,1)S(1)}, bf16[8,2,144,128]{3,2,1,0:T(8,128)(2,1)S(1)}, u32[]{:S(2)}, u32[]{:S(2)}) collective-permute-start(bf16[8,2,144,128]{3,2,1,0:T(8,128)(2,1)S(1)} %pad_maximum_fusion.1), channel_id=1, source_target_pairs={{0,4},{2,6},{4,0},{6,2},{8,12},{10,14},{12,8},{14,10},{16,20},{18,... | collective-permute-start | bytes 1769480 | tf_op jit(solution)/shard_map/ppermute | solution.py:374
  202.4 2.6 %collective-permute-done.2 = bf16[4,2,144,128]{3,2,1,0:T(8,128)(2,1)S(1)} collective-permute-done((bf16[4,2,144,128]{3,2,1,0:T(8,128)(2,1)S(1)}, bf16[4,2,144,128]{3,2,1,0:T(8,128)(2,1)S(1)}, u32[]{:S(2)}, u32[]{:S(2)}) %collective-permute-start.2) | collective-permute-done | bytes 294944 | tf_op jit(solution)/shard_map/ppermute | solution.py:374
  205.0 0.9 pad_maximum_fusion
  205.9 0.7 collective-permute-start.3
  206.7 0.0 copy-done.8
  206.7 0.0 copy-done.5
  206.7 1.3 fusion
  208.0 4.0 %psum.7 = bf16[8,512]{1,0:T(8,128)(2,1)S(1)} all-reduce(f32[8,512]{1,0:T(8,128)} %fusion), channel_id=1, replica_groups=mesh['ctx'=16,'head'=2] {'head'}, use_global_device_ids=true, to_apply=%region_0.1 | all-reduce | flops 4096 | bytes 24576 | tf_op jit(solution)/shard_map/psum | solution.py:408
  212.0 0.6 reshape.59
  212.6 1.9 collective-permute-done.7
  214.4 0.1 constant_dynamic-update-slice_fusion.5.refs_4_
  214.5 1.6 collective-permute-done.3
  216.1 1.1 constant_dynamic-update-slice_fusion.refs_3_
  217.2 0.0 all-to-all-done.4.refs_2_
  217.2 18.4 %place_and_score.1 = (bf16[16,128,4,256]{3,2,1,0:T(4,128)(2,1)}, f32[2,4,1024]{2,1,0:T(4,128)}) custom-call(s32[1]{0:T(128)} %bitcast.place.refs_0_, s32[16,2]{1,0:T(8,128)S(1)} %bitcast.36, bf16[16,128,4,256]{3,2,1,0:T(4,128)(2,1)} %all-to-all-done.4.refs_2_, bf16[16,2,144,128]{3,2,1,0:T(8,128)(2,1)S(1)} %constant_dynamic-update-slice_fusion.refs_3_, ...), custom_call_target="tpu_custom_call" | custom-call | tf_op jit(solution)/shard_map/place_and_score/pallas_call | solution.py:345
  (21 shorter events, 0.4 us)
Async XLA Ops:
  1.3 2.2 copy-start.2
  3.5 1.2 copy-start.3
  4.8 23.7 %copy-start.9 = (s32[2,8,2]{1,2,0:T(2,128)S(1)}, s32[2,8,2]{1,2,0:T(2,128)}, u32[]{:S(2)}) copy-start(s32[2,8,2]{1,2,0:T(2,128)} %param.10) | copy-start | bytes 388
  4.8 23.8 %copy-start.4 = (s32[2,8,128]{2,1,0:T(8,128)S(1)}, s32[2,8,128]{2,1,0:T(8,128)}, u32[]{:S(2)}) copy-start(s32[2,8,128]{2,1,0:T(8,128)} %param.9) | copy-start | bytes 24580
  7.2 17.0 %all-to-all-start = ((f32[16,24,128]{2,1,0:T(8,128)}), f32[16,24,128]{2,1,0:T(8,128)S(1)}, u32[]{:S(2)}, u32[]{:S(2)}) async-start(f32[16,24,128]{2,1,0:T(8,128)} %project_tokens.1), calls=%async_computation | async-start | bytes 393216 | tf_op jit(solution)/shard_map/all_to_all | solution.py:367
  24.9 15.2 %all-to-all-start.1 = ((bf16[16,32,128]{2,1,0:T(8,128)(2,1)}), bf16[16,32,128]{2,1,0:T(8,128)(2,1)S(1)}, u32[]{:S(2)}, u32[]{:S(2)}) async-start(bf16[16,32,128]{2,1,0:T(8,128)(2,1)} %normalize_tokens.1), calls=%async_computation.1 | async-start | bytes 262144 | tf_op jit(solution)/shard_map/all_to_all | solution.py:367
  38.1 2.0 copy-start
  40.1 2.2 copy-start.1
  42.3 13.4 %copy-start.6 = (bf16[2,16,4096]{2,1,0:T(8,128)(2,1)S(1)}, bf16[2,16,4096]{2,1,0:T(8,128)(2,1)}, u32[]{:S(2)}) copy-start(bf16[2,16,4096]{2,1,0:T(8,128)(2,1)} %param.11) | copy-start | bytes 786436
  48.8 15.0 %all-to-all-start.2 = ((f32[16,24,128]{2,1,0:T(8,128)}), f32[16,24,128]{2,1,0:T(8,128)S(1)}, u32[]{:S(2)}, u32[]{:S(2)}) async-start(f32[16,24,128]{2,1,0:T(8,128)} %attend_kept.1), calls=%async_computation.2 | async-start | bytes 393216 | tf_op jit(solution)/shard_map/all_to_all | solution.py:367
  64.8 11.0 %all-to-all-start.3 = ((bf16[16,16,128]{2,1,0:T(8,128)(2,1)}), bf16[16,16,128]{2,1,0:T(8,128)(2,1)S(1)}, u32[]{:S(2)}, u32[]{:S(2)}) async-start(bf16[16,16,128]{2,1,0:T(8,128)(2,1)} %combine_parts.1), calls=%async_computation.3 | async-start | bytes 131072 | tf_op jit(solution)/shard_map/all_to_all | solution.py:367
  75.8 0.6 copy-start.7
  76.4 12.0 %all-to-all-start.5 = ((bf16[16,16,512]{2,1,0:T(8,128)(2,1)}), bf16[16,16,512]{2,1,0:T(8,128)(2,1)S(1)}, u32[]{:S(2)}, u32[]{:S(2)}) async-start(bf16[16,16,512]{2,1,0:T(8,128)(2,1)} %bitcast.5), calls=%async_computation.5 | async-start | bytes 524288 | tf_op jit(solution)/shard_map/all_to_all | solution.py:367
  88.4 128.8 %all-to-all-start.4 = ((bf16[16,128,4,256]{3,2,1,0:T(4,128)(2,1)}), bf16[16,128,4,256]{3,2,1,0:T(4,128)(2,1)}, u32[]{:S(2)}, u32[]{:S(2)}) async-start(bf16[16,128,4,256]{3,2,1,0:T(4,128)(2,1)} %copy-done), calls=%async_computation.4 | async-start | bytes 8388608 | tf_op jit(solution)/shard_map/all_to_all | solution.py:367
  93.5 93.5 %collective-permute-start.4 = (bf16[1,2,144,128]{3,2,1,0:T(8,128)(2,1)S(1)}, bf16[1,2,144,128]{3,2,1,0:T(8,128)(2,1)S(1)}, u32[]{:S(2)}, u32[]{:S(2)}) collective-permute-start(bf16[1,2,144,128]{3,2,1,0:T(8,128)(2,1)S(1)} %get-tuple-element.11), channel_id=1, source_target_pairs={{0,16},{2,18},{4,20},{6,22},{8,24},{10,26},{12,28},{14,30},{16,0},... | collective-permute-start | bytes 221192 | tf_op jit(solution)/shard_map/ppermute | solution.py:374
  96.3 91.6 %collective-permute-start = (bf16[1,2,144,128]{3,2,1,0:T(8,128)(2,1)S(1)}, bf16[1,2,144,128]{3,2,1,0:T(8,128)(2,1)S(1)}, u32[]{:S(2)}, u32[]{:S(2)}) collective-permute-start(bf16[1,2,144,128]{3,2,1,0:T(8,128)(2,1)S(1)} %get-tuple-element.12), channel_id=1, source_target_pairs={{0,16},{2,18},{4,20},{6,22},{8,24},{10,26},{12,28},{14,30},{16,0},... | collective-permute-start | bytes 221192 | tf_op jit(solution)/shard_map/ppermute | solution.py:374
  187.1 5.6 %collective-permute-start.5 = (bf16[2,2,144,128]{3,2,1,0:T(8,128)(2,1)S(1)}, bf16[2,2,144,128]{3,2,1,0:T(8,128)(2,1)S(1)}, u32[]{:S(2)}, u32[]{:S(2)}) collective-permute-start(bf16[2,2,144,128]{3,2,1,0:T(8,128)(2,1)S(1)} %pad_maximum_fusion.5), channel_id=1, source_target_pairs={{0,8},{2,10},{4,12},{6,14},{8,0},{10,2},{12,4},{14,6},{16,24},{18,... | collective-permute-start | bytes 442376 | tf_op jit(solution)/shard_map/ppermute | solution.py:374
  187.9 6.4 %collective-permute-start.1 = (bf16[2,2,144,128]{3,2,1,0:T(8,128)(2,1)S(1)}, bf16[2,2,144,128]{3,2,1,0:T(8,128)(2,1)S(1)}, u32[]{:S(2)}, u32[]{:S(2)}) collective-permute-start(bf16[2,2,144,128]{3,2,1,0:T(8,128)(2,1)S(1)} %pad_maximum_fusion.4), channel_id=1, source_target_pairs={{0,8},{2,10},{4,12},{6,14},{8,0},{10,2},{12,4},{14,6},{16,24},{18,... | collective-permute-start | bytes 442376 | tf_op jit(solution)/shard_map/ppermute | solution.py:374
  192.7 6.8 %collective-permute-start.6 = (bf16[4,2,144,128]{3,2,1,0:T(8,128)(2,1)S(1)}, bf16[4,2,144,128]{3,2,1,0:T(8,128)(2,1)S(1)}, u32[]{:S(2)}, u32[]{:S(2)}) collective-permute-start(bf16[4,2,144,128]{3,2,1,0:T(8,128)(2,1)S(1)} %pad_maximum_fusion.3), channel_id=1, source_target_pairs={{0,2},{2,0},{4,6},{6,4},{8,10},{10,8},{12,14},{14,12},{16,18},{18,... | collective-permute-start | bytes 884744 | tf_op jit(solution)/shard_map/ppermute | solution.py:374
  194.3 12.4 %copy-start.8 = (bf16[16,16,128]{2,1,0:T(8,128)(2,1)S(1)}, bf16[16,16,128]{2,1,0:T(8,128)(2,1)}, u32[]{:S(2)}) copy-start(bf16[16,16,128]{2,1,0:T(8,128)(2,1)} %copy-done.7) | copy-start | bytes 196612
  194.3 10.7 %collective-permute-start.2 = (bf16[4,2,144,128]{3,2,1,0:T(8,128)(2,1)S(1)}, bf16[4,2,144,128]{3,2,1,0:T(8,128)(2,1)S(1)}, u32[]{:S(2)}, u32[]{:S(2)}) collective-permute-start(bf16[4,2,144,128]{3,2,1,0:T(8,128)(2,1)S(1)} %pad_maximum_fusion.2), channel_id=1, source_target_pairs={{0,4},{2,6},{4,0},{6,2},{8,12},{10,14},{12,8},{14,10},{16,20},{18,... | collective-permute-start | bytes 884744 | tf_op jit(solution)/shard_map/ppermute | solution.py:374
  197.1 9.6 %copy-start.5 = (bf16[4096,512]{1,0:T(8,128)(2,1)S(1)}, bf16[4096,512]{1,0:T(8,128)(2,1)}, u32[]{:S(2)}) copy-start(bf16[4096,512]{1,0:T(8,128)(2,1)} %param.15) | copy-start | bytes 12582916
  199.6 14.9 %collective-permute-start.7 = (bf16[8,2,144,128]{3,2,1,0:T(8,128)(2,1)S(1)}, bf16[8,2,144,128]{3,2,1,0:T(8,128)(2,1)S(1)}, u32[]{:S(2)}, u32[]{:S(2)}) collective-permute-start(bf16[8,2,144,128]{3,2,1,0:T(8,128)(2,1)S(1)} %pad_maximum_fusion.1), channel_id=1, source_target_pairs={{0,4},{2,6},{4,0},{6,2},{8,12},{10,14},{12,8},{14,10},{16,20},{18,... | collective-permute-start | bytes 1769480 | tf_op jit(solution)/shard_map/ppermute | solution.py:374
  205.9 10.2 %collective-permute-start.3 = (bf16[8,2,144,128]{3,2,1,0:T(8,128)(2,1)}, bf16[8,2,144,128]{3,2,1,0:T(8,128)(2,1)}, u32[]{:S(2)}, u32[]{:S(2)}) collective-permute-start(bf16[8,2,144,128]{3,2,1,0:T(8,128)(2,1)} %pad_maximum_fusion), channel_id=1, source_target_pairs={{0,2},{2,0},{4,6},{6,4},{8,10},{10,8},{12,14},{14,12},{16,18},{18,... | collective-permute-start | bytes 1769480 | tf_op jit(solution)/shard_map/ppermute | solution.py:374

commit v2 on v1

--- a/solution.py
+++ b/solution.py
@@ -17,13 +17,17 @@
 STAT = 144
 LARGE = 1e30
 VMEM_LIMIT = 48 << 20
-ANY = pl.BlockSpec(memory_space=pl.ANY)
+ANY = pl.BlockSpec(memory_space=pltpu.HBM)
 SMEM = pl.BlockSpec(memory_space=pltpu.SMEM)
 VMEM = pl.BlockSpec(memory_space=pltpu.VMEM)
 NT = (((1,), (1,)), ((), ()))
 TN = (((0,), (0,)), ((), ()))
 
 
+def hbm(value):
+    return pltpu.with_memory_space_constraint(value, pltpu.HBM)
+
+
 def params():
     return pltpu.CompilerParams(vmem_limit_bytes=VMEM_LIMIT)
 
@@ -49,9 +53,9 @@
         fetch(m).wait()
 
         def rows(j, inner):
+            values = [spans[m, keep[m, j * 16 + u]] for u in range(16)]
             for u in range(16):
-                at = j * 16 + u
-                blocks[m, at] = spans[m, keep[m, at]]
+                blocks[m, j * 16 + u] = values[u]
             return inner
 
         lax.fori_loop(0, width // 16, rows, 0)
@@ -68,7 +72,7 @@
     tail = kv_cache.shape[2:]
     return pl.pallas_call(
         pack_kernel,
-        out_shape=jax.ShapeDtypeStruct((items, width, *tail), kv_cache.dtype),
+        out_shape=pltpu.HBM((items, width, *tail), kv_cache.dtype),
         in_specs=[SMEM, SMEM, ANY],
         out_specs=ANY,
         scratch_shapes=[
@@ -82,18 +86,30 @@
     )(keep, target, kv_cache)
 
 
-def project_kernel(tokens, wq, wkv, out):
+def terms(value):
+    high = value.astype(BF).astype(F32)
+    middle = (value - high).astype(BF).astype(F32)
+    return high, middle, value - high - middle
+
+
+def project_kernel(tokens, wq, wkv, samples, out, rows, extra):
     i = pl.program_id(0)
-    x = tokens[...]
+    x = jnp.concatenate([tokens[t, r : r + 1, :].astype(F32) for r in range(2) for t in range(4)], axis=0)
+    x = x.astype(BF)
     part = jnp.dot(x, wq[...], preferred_element_type=F32)
     for r in range(2):
         for g in range(8):
-            out[r * 8 + i * 2 + g // 4, (g % 4) * 4 : (g % 4) * 4 + 4, :] = part[
+            rows[r * 8 + i * 2 + g // 4, (g % 4) * 4 : (g % 4) * 4 + 4, :] = part[
                 r * 4 : r * 4 + 4, g * 128 : g * 128 + 128
             ]
 
     @pl.when(i == 0)
     def _():
+        for r in range(2):
+            for c in range(32):
+                out[r * 8 + c // 4, (c % 4) * 16 : (c % 4) * 16 + 16, :] = samples[
+                    r, :, c * 128 : c * 128 + 128
+                ]
         heads = pltpu.einshape("nhd->hnd", wkv[...])
         wide = x.astype(F32)
         squares = jnp.sum(wide * wide, axis=1, keepdims=True)
@@ -102,55 +118,97 @@
         line = jnp.sum(jnp.where(row == lane, squares, 0.0), axis=0, keepdims=True)
         line = jnp.concatenate([line, jnp.zeros((3, 128), F32)], axis=0)
         for p in range(16):
-            out[p, 20:24, :] = line
+            extra[p, 4:8, :] = line
         for j in range(4):
             pair = jnp.dot(x, heads[j], preferred_element_type=F32)
             for r in range(2):
                 for half in range(2):
-                    out[r * 8 + j * 2 + half, 16:20, :] = pair[
+                    extra[r * 8 + j * 2 + half, 0:4, :] = pair[
                         r * 4 : r * 4 + 4, half * 128 : half * 128 + 128
                     ]
 
-
-def project(tokens, w_query, w_keyval):
+    @pl.when(i == 3)
+    def _():
+        for at, term in enumerate(terms(rows[...])):
+            out[:, 64 + at * 16 : 80 + at * 16, :] = term.astype(BF)
+        first, second, third = terms(extra[...])
+        out[:, 112:128, :] = jnp.concatenate([first, second], axis=1).astype(BF)
+        out[:, 128:144, :] = jnp.concatenate([third, jnp.zeros((16, 8, 128), F32)], axis=1).astype(BF)
+
+
+def project(tokens, w_query, w_keyval, samples):
     depth, columns = w_query.shape
     step = columns // 4
     return pl.pallas_call(
         project_kernel,
-        out_shape=jax.ShapeDtypeStruct((16, 24, 128), F32),
+        out_shape=jax.ShapeDtypeStruct((16, 144, 128), BF),
         grid=(4,),
         in_specs=[
-            pl.BlockSpec((8, depth), lambda i: (0, 0)),
+            pl.BlockSpec(tokens.shape, lambda i: (0, 0, 0)),
             pl.BlockSpec((depth, step), lambda i: (0, i)),
             pl.BlockSpec(w_keyval.shape, lambda i: (0, 0, 0)),
+            pl.BlockSpec(samples.shape, lambda i: (0, 0, 0)),
         ],
-        out_specs=pl.BlockSpec((16, 24, 128), lambda i: (0, 0, 0)),
+        out_specs=pl.BlockSpec((16, 144, 128), lambda i: (0, 0, 0)),
+        scratch_shapes=[pltpu.VMEM((16, 16, 128), F32), pltpu.VMEM((16, 8, 128), F32)],
         compiler_params=params(),
         name="project_tokens",
-    )(tokens, w_query, w_keyval)
-
-
-def normalize_kernel(place, parts, out):
-    total = jnp.sum(parts[...], axis=0)
+    )(tokens, hbm(w_query), hbm(w_keyval), hbm(samples))
+
+
+def settle_kernel(place, parts, out):
     request = place[0] // 8
-    row = lax.broadcasted_iota(jnp.int32, (24, 128), 0)
-    lane = lax.broadcasted_iota(jnp.int32, (24, 128), 1)
-    squares = jnp.where(lane == request * 4 + row % 4, total[20:21, :], 0.0)
+    total = jnp.sum(parts[:, 64:80, :].astype(F32), axis=0)
+    total = total + jnp.sum(parts[:, 80:96, :].astype(F32), axis=0)
+    total = total + jnp.sum(parts[:, 96:112, :].astype(F32), axis=0)
+    both = jnp.sum(parts[:, 112:128, :].astype(F32), axis=0)
+    rest = jnp.sum(parts[:, 128:144, :].astype(F32), axis=0)
+    both = both[0:8] + both[8:16] + rest[0:8]
+    row = lax.broadcasted_iota(jnp.int32, (16, 128), 0)
+    lane = lax.broadcasted_iota(jnp.int32, (16, 128), 1)
+    squares = jnp.where(lane == request * 4 + row % 4, both[4:5, :], 0.0)
     inverse = lax.rsqrt(jnp.sum(squares, axis=1, keepdims=True) / D + EPSILON)
-    scaled = jnp.where(row < 20, total * inverse, 0.0)
-    rounded = jnp.concatenate([scaled, jnp.zeros((8, 128), F32)], axis=0).astype(BF)
+    own = total * inverse
+    fresh = jnp.where(row[0:8] < 4, both * inverse[0:8], 0.0)
+    rounded = jnp.concatenate([own, fresh, jnp.zeros((8, 128), F32)], axis=0).astype(BF)
     out[...] = jnp.broadcast_to(rounded[None], out.shape)
 
 
-def normalize(place, parts):
-    return pl.pallas_call(
-        normalize_kernel,
+def moments_kernel(parts, stat):
+    for i in range(4):
+        q = parts[:, i * 16 : i * 16 + 16, :].reshape(256, 128)
+        second = lax.dot_general(q, q, TN, preferred_element_type=F32)
+        mean = jnp.sum(q.astype(F32), axis=0, keepdims=True) / QS
+        first = jnp.concatenate([mean, jnp.zeros((7, 128), F32)], axis=0)
+        outer = lax.dot_general(first, first, TN, preferred_element_type=F32, precision=HIGHEST)
+        cov = second / QS - outer
+        scaled = mean / math.sqrt(128)
+        high = scaled.astype(BF).astype(F32)
+        lines = jnp.concatenate([high, scaled - high, jnp.zeros((14, 128), F32)], axis=0)
+        stat[0, i, 0:128, :] = cov.astype(BF)
+        stat[0, i, 128:144, :] = lines.astype(BF)
+
+
+def settle(place, parts):
+    return pl.pallas_call(
+        settle_kernel,
         out_shape=jax.ShapeDtypeStruct((16, 32, 128), BF),
         in_specs=[SMEM, VMEM],
         out_specs=VMEM,
         compiler_params=params(),
-        name="normalize_tokens",
+        name="settle_tokens",
     )(place, parts)
+
+
+def head_moments(parts):
+    return pl.pallas_call(
+        moments_kernel,
+        out_shape=jax.ShapeDtypeStruct((1, 4, STAT, 128), BF),
+        in_specs=[VMEM],
+        out_specs=VMEM,
+        compiler_params=params(),
+        name="head_moments",
+    )(parts)
 
 
 def attend_kernel(target, query, bias, send, out, rows, logits, sem):
@@ -205,10 +263,10 @@
         ],
         compiler_params=params(),
         name="attend_kept",
-    )(target, query, bias, send)
-
-
-def combine_kernel(place, parts, query, out):
+    )(target, query, bias, hbm(send))
+
+
+def combine_kernel(place, target, parts, query, out, scores):
     p = place[0]
     mine = query[p, 0:16, :]
     pair = (p // 2) * 2
@@ -236,44 +294,23 @@
         total = total + totals[s] * factor
         weighted = weighted + parts[s, 0:16, :] * factor
     out[...] = jnp.broadcast_to((weighted / total).astype(BF)[None], out.shape)
-
-
-def combine(place, parts, query):
+    for m in range(16):
+        start = pl.multiple_of(target[m, 1] * 128, 128)
+        scores[m // 8, :, pl.ds(start, 128)] = parts[sender(m, p, target, 16), 18:22, :]
+
+
+def combine(place, target, parts, query):
     return pl.pallas_call(
         combine_kernel,
-        out_shape=jax.ShapeDtypeStruct((16, 16, 128), BF),
-        in_specs=[SMEM, VMEM, VMEM],
-        out_specs=VMEM,
+        out_shape=(
+            jax.ShapeDtypeStruct((16, 16, 128), BF),
+            jax.ShapeDtypeStruct((2, 4, 1024), F32),
+        ),
+        in_specs=[SMEM, SMEM, VMEM, VMEM],
+        out_specs=(VMEM, VMEM),
         compiler_params=params(),
         name="combine_parts",
-    )(place, parts, query)
-
-
-def moments_kernel(samples, out):
-    for i in range(4):
-        q = samples[:, i * 128 : i * 128 + 128]
-        second = lax.dot_general(q, q, TN, preferred_element_type=F32)
-        mean = jnp.sum(q.astype(F32), axis=0, keepdims=True) / QS
-        first = jnp.concatenate([mean, jnp.zeros((7, 128), F32)], axis=0)
-        outer = lax.dot_general(first, first, TN, preferred_element_type=F32, precision=HIGHEST)
-        cov = second / QS - outer
-        scaled = mean / math.sqrt(128)
-        high = scaled.astype(BF).astype(F32)
-        low = scaled - high
-        lines = jnp.concatenate([high, low, jnp.zeros((14, 128), F32)], axis=0)
-        out[i, 0:128, :] = cov.astype(BF)
-        out[i, 128:144, :] = lines.astype(BF)
-
-
-def head_moments(samples):
-    return pl.pallas_call(
-        moments_kernel,
-        out_shape=jax.ShapeDtypeStruct((4, STAT, 128), BF),
-        in_specs=[VMEM],
-        out_specs=VMEM,
-        compiler_params=params(),
-        name="moments",
-    )(samples)
+    )(place, target, parts, query)
 
 
 def reverse_bits(value, order):
@@ -283,96 +320,126 @@
     return place
 
 
-def score_kernel(orders, place, target, arrived, stat_a, stat_b, packed, scores, blocks, stats, in_sem, out_sem, a_sem, b_sem):
+def score_kernel(orders, place, target, stat_a, stat_b, send, parts, out, blocks, sem):
     items = blocks.shape[0]
     lists = items // 2
     me = place[0]
 
-    def at(m):
-        return (m // lists) * lists + target[m, 1]
-
     def fetch(m):
-        source = (2 * me - target[m, 0] + 16) % 16
-        return pltpu.make_async_copy(arrived.at[source], blocks.at[at(m)], in_sem.at[m])
-
-    def put(m):
-        return pltpu.make_async_copy(blocks.at[m], packed.at[m], out_sem.at[m])
-
-    def take(o, half, stat, sem):
-        index = reverse_bits(jnp.bitwise_xor(me, o), orders[half])
-        return pltpu.make_async_copy(stat.at[index], stats.at[o, pl.ds(half * 2, 2)], sem.at[o])
+        return pltpu.make_async_copy(send.at[target[m, 0]], blocks.at[m], sem.at[m])
 
     for m in range(items):
         fetch(m).start()
-    for o in range(16):
-        take(o, 0, stat_a, a_sem).start()
-        take(o, 1, stat_b, b_sem).start()
+    out[...] = parts[...]
     for m in range(items):
         fetch(m).wait()
-    for m in range(items):
-        put(m).start()
-    for o in range(16):
-        take(o, 0, stat_a, a_sem).wait()
-        take(o, 1, stat_b, b_sem).wait()
     for r in range(2):
         for j in range(4):
-            first = r * 8 + j * 2
-            table = stats[first : first + 2].reshape(8 * STAT, 128)
-            for c in range(4):
-                keys = blocks[r * 8 + c * 2 : r * 8 + c * 2 + 2, :, j, 0:128].reshape(256, 128)
-                turned = lax.dot_general(table, keys, NT, preferred_element_type=F32)
+            tables = []
+            for o in range(2):
+                owner = jnp.bitwise_xor(me, r * 8 + j * 2 + o)
+                for half, stat in enumerate((stat_a, stat_b)):
+                    tables.append(stat[reverse_bits(owner, orders[half])].reshape(2 * STAT, 128))
+            for c in range(lists // 2):
+                first = r * lists + c * 2
+                keys = blocks[first : first + 2, :, j, 0:128].reshape(256, 128)
                 flipped = keys.astype(F32).T
-                lines = []
-                for g in range(8):
-                    base = g * STAT
-                    quadratic = jnp.sum(turned[base : base + 128] * flipped, axis=0, keepdims=True)
-                    linear = turned[base + 128 : base + 129] + turned[base + 129 : base + 130]
-                    lines.append(linear + quadratic / 256.0)
-                logit = jnp.concatenate(lines, axis=0)
+                logits = []
+                for table in tables:
+                    turned = lax.dot_general(table, keys, NT, preferred_element_type=F32)
+                    for g in range(2):
+                        base = g * STAT
+                        quadratic = jnp.sum(
+                            turned[base : base + 128] * flipped, axis=0, keepdims=True
+                        )
+                        linear = turned[base + 128 : base + 129] + turned[base + 129 : base + 130]
+                        logits.append(linear + quadratic / 256.0)
+                logit = jnp.concatenate(logits, axis=0)
                 top = jnp.max(logit, axis=0, keepdims=True)
                 mean = jnp.sum(jnp.exp(logit - top), axis=0, keepdims=True) / 8.0
-                scores[r, j : j + 1, c * 256 : c * 256 + 256] = top + jnp.log(mean)
-    for m in range(items):
-        put(m).wait()
-
-
-def score(orders, place, target, arrived, stat_a, stat_b):
-    items, width = arrived.shape[:2]
+                line = top + jnp.log(mean)
+                for u in range(2):
+                    p = target[first + u, 0]
+                    out[p, 18 + j : 19 + j, :] = line[:, u * 128 : u * 128 + 128]
+
+
+def score(orders, place, target, stat_a, stat_b, send, parts):
+    items = send.shape[0]
 
     def kernel(*refs):
         score_kernel(orders, *refs)
 
     return pl.pallas_call(
         kernel,
-        out_shape=(
-            jax.ShapeDtypeStruct(arrived.shape, arrived.dtype),
-            jax.ShapeDtypeStruct((2, 4, items // 2 * width), F32),
-        ),
-        in_specs=[SMEM, SMEM, ANY, ANY, ANY],
-        out_specs=(ANY, VMEM),
+        out_shape=jax.ShapeDtypeStruct(parts.shape, parts.dtype),
+        in_specs=[SMEM, SMEM, VMEM, VMEM, ANY, VMEM],
+        out_specs=VMEM,
+        scratch_shapes=[
+            pltpu.VMEM(send.shape, send.dtype),
+            pltpu.SemaphoreType.DMA((items,)),
+        ],
+        compiler_params=params(),
+        name="score_kept",
+    )(place, target, stat_a, stat_b, hbm(send), parts)
+
+
+def sender(m, me, target, count):
+    return (2 * me - target[m, 0] + count) % count
+
+
+def place_kernel(place, target, arrived, packed, blocks, in_sem, out_sem):
+    items = arrived.shape[0]
+    lists = items // 2
+
+    def fetch(m):
+        return pltpu.make_async_copy(
+            arrived.at[sender(m, place[0], target, items)], blocks.at[m], in_sem.at[m]
+        )
+
+    def put(m):
+        slot = (m // lists) * lists + target[m, 1]
+        return pltpu.make_async_copy(blocks.at[m], packed.at[slot], out_sem.at[m])
+
+    for m in range(items):
+        fetch(m).start()
+    for m in range(items):
+        fetch(m).wait()
+        put(m).start()
+    for m in range(items):
+        put(m).wait()
+
+
+def put_blocks(place, target, arrived):
+    items = arrived.shape[0]
+    return pl.pallas_call(
+        place_kernel,
+        out_shape=pltpu.HBM(arrived.shape, arrived.dtype),
+        in_specs=[SMEM, SMEM, ANY],
+        out_specs=ANY,
         scratch_shapes=[
             pltpu.VMEM(arrived.shape, arrived.dtype),
-            pltpu.VMEM((16, 4, STAT, 128), BF),
             pltpu.SemaphoreType.DMA((items,)),
             pltpu.SemaphoreType.DMA((items,)),
-            pltpu.SemaphoreType.DMA((16,)),
-            pltpu.SemaphoreType.DMA((16,)),
         ],
         compiler_params=params(),
-        name="place_and_score",
-    )(place, target, arrived, stat_a, stat_b)
+        name="place_blocks",
+    )(place, target, hbm(arrived))
 
 
 def exchange(value):
     return lax.all_to_all(value, "ctx", split_axis=0, concat_axis=0, tiled=True)
 
 
-def doubled(value, order):
-    value = value[None]
-    for bit in order:
-        pairs = [(i, i ^ bit) for i in range(16)]
-        value = jnp.concatenate([value, lax.ppermute(value, "ctx", pairs)], axis=0)
-    return value
+def doubled(value, bit):
+    pairs = [(i, i ^ bit) for i in range(16)]
+    return jnp.concatenate([value, lax.ppermute(value, "ctx", pairs)], axis=0)
+
+
+def after(values, token):
+    return lax.optimization_barrier((values, token))[0]
+
+
+ORDERS = ((8, 4, 2, 1), (8, 4, 1, 2))
 
 
 def sixteen(
@@ -384,29 +451,31 @@
     keep = keep_rows.reshape(items, width)
     target = block_target.reshape(items, 2)
     place = lax.axis_index("ctx").astype(jnp.int32).reshape(1)
-    tokens = jnp.transpose(new_tokens, (1, 0, 2)).reshape(8, new_tokens.shape[2])
-    samples = future_queries.reshape(2, 16, 8, 512)
-    samples = jnp.transpose(samples, (0, 2, 1, 3)).reshape(16, 16, 512)
-    samples = exchange(samples).reshape(256, 512)
-    parts = exchange(project(tokens, w_query, w_keyval))
+    parts = exchange(project(new_tokens, w_query, w_keyval, future_queries))
     send = pack(kv_cache, keep, target)
-    bias = jnp.where(keep < 2 * width, 0.0, -LARGE).astype(F32)
+    parts = after(parts, send)
+    own = settle(place, parts)
+    query = exchange(own)
+    stat = head_moments(after(parts, own))
+    stat = doubled(doubled(stat, 8), 4)
+    arrived = exchange(after(send, (query, stat)))
+    bias = jnp.where(after(keep, query) < 2 * width, 0.0, -LARGE).astype(F32)
     bias = jnp.broadcast_to(bias[:, :, None], (items, width, 4)).reshape(items, width * 4)
-    query = exchange(normalize(place, parts))
-    stat = head_moments(samples)
-    orders = ((8, 4, 2, 1), (8, 4, 1, 2))
-    stat_a = doubled(stat[:2], orders[0])
-    stat_b = doubled(stat[2:], orders[1])
-    joined = exchange(attend(target, query, bias, send))
-    attended = exchange(combine(place, joined, query))
-    send, attended = lax.optimization_barrier((send, attended))
-    arrived = exchange(send)
-    packed, scores = score(orders, place, target, arrived, stat_a, stat_b)
+    stat_a = doubled(doubled(stat[:, :2], 2), 1)
+    stat_b = doubled(doubled(stat[:, 2:], 1), 2)
+    softmax = attend(target, query, bias, send)
+    softmax = score(ORDERS, place, target, stat_a, stat_b, send, softmax)
+    parts = exchange(after(softmax, arrived))
+    packed = put_blocks(place, target, arrived)
+    share, scores = combine(place, target, after(parts, packed), query)
+    attended = exchange(share)
     rows = attended.reshape(requests, 32, 4, 128)
     rows = jnp.transpose(rows, (2, 0, 1, 3)).reshape(8, 4096)
     partial_value = jnp.dot(rows, w_out, preferred_element_type=F32)
     decoded = lax.psum(partial_value, "head").astype(BF).reshape(4, requests, w_out.shape[1])
     return packed.reshape(requests, lists * width, local_kv, pair), scores, decoded
+
+
 def joined(value, axis, join):
     pieces = jax.tree.map(lambda part: lax.all_gather(part, axis), value)
     head = jax.tree.map(lambda part: part[0], pieces)

time: 237 us -> 186 us (0.78)
  waiting for transfers between devices: 135 us -> 75.5 us
  local copies, waits for them, and re-layouts: 12.2 us -> 1.69 us
  blocking collectives: 4 us -> 14.1 us
  Pallas kernels: 38.9 us -> 45.1 us
    ppermute x8 -> x6, waiting for transfers between devices: 103 us -> 59.3 us  [doubled(): return jnp.concatenate([value, lax.ppermute(value, 'ctx', pairs)], axis=0)]
    all_to_all x6 -> x4, waiting for transfers between devices: 31.8 us -> 16.2 us  [exchange(): return lax.all_to_all(value, 'ctx', split_axis=0, concat_axis=0, tiled=True)]
    all_to_all x0 -> x1, blocking collectives: none -> 10.7 us  [exchange(): return lax.all_to_all(value, 'ctx', split_axis=0, concat_axis=0, tiled=True)]
    unnamed x28 -> x6, local copies, waits for them, and re-layouts: 8.5 us -> 0.7 us
    pallas_call x6 -> x7, Pallas kernels: 32.4 us -> 38.7 us  [the longest x1 16.6 us: score(): pl.pallas_call(kernel, out_shape=jax.ShapeDtypeStruct(parts.shape, parts....]
    all_to_all x6 -> x4, starting transfers between devices: 30.3 us -> 34.6 us  [exchange(): return lax.all_to_all(value, 'ctx', split_axis=0, concat_axis=0, tiled=True)]
    ppermute x8 -> x6, starting transfers between devices: 12.3 us -> 9.29 us  [doubled(): return jnp.concatenate([value, lax.ppermute(value, 'ctx', pairs)], axis=0)]
  transfers between devices with their start and end apart: 14 -> 10, of which waited for: 12 -> 9; matrix products, arithmetic and copies ran while one was open for 2% -> 1% of each run, Pallas kernels for 4% -> 20%
where the time goes in v2:
time: 186 us; the launch traced here: 185 us
  waiting for transfers between devices  75.5 us (41%)
  Pallas kernels  45.1 us (24%)
  starting transfers between devices  43.8 us (24%)
  blocking collectives  14.1 us (8%)
  matrix products  2.83 us (2%)
    ppermute x6, waiting for transfers between devices, doubled(): return jnp.concatenate([value, lax.ppermute(value, 'ctx', pairs)], axis=0)  59.3 us
    all_to_all x4, starting transfers between devices, exchange(): return lax.all_to_all(value, 'ctx', split_axis=0, concat_axis=0, tiled=True)  34.6 us
    pallas_call x1, Pallas kernels, score(): pl.pallas_call(kernel, out_shape=jax.ShapeDtypeStruct(parts.shape, parts....  16.6 us
    all_to_all x4, waiting for transfers between devices, exchange(): return lax.all_to_all(value, 'ctx', split_axis=0, concat_axis=0, tiled=True)  16.2 us
    all_to_all x1, blocking collectives, exchange(): return lax.all_to_all(value, 'ctx', split_axis=0, concat_axis=0, tiled=True)  10.7 us
    pallas_call x1, Pallas kernels, pack(): pl.pallas_call(pack_kernel, out_shape=pltpu.HBM((items, width, *tail), kv...  9.62 us
    ppermute x6, starting transfers between devices, doubled(): return jnp.concatenate([value, lax.ppermute(value, 'ctx', pairs)], axis=0)  9.29 us
    pallas_call x1, Pallas kernels, attend(): pl.pallas_call(attend_kernel, out_shape=jax.ShapeDtypeStruct((16, 24, 128...  6.41 us
  transfers between devices with their start and end apart: 10, of which 9 were waited for; matrix products, arithmetic and copies ran while one was open for 1% of the time, Pallas kernels for 20%

profile of v2, /device:TPU:0, one launch (start us, length us, event | category | flops | bytes accessed | tf_op | source)
XLA Modules:
  0.0 185.3 jit_solution(17107221445390280737)
XLA Ops:
  0.6 0.0 copy-start.1
  0.6 0.7 copy-done.1
  1.3 5.0 %project_tokens.1 = bf16[16,144,128]{2,1,0:T(8,128)(2,1)} custom-call(bf16[4,2,512]{2,1,0:T(2,128)(2,1)S(1)} %copy-done.1, bf16[512,4096]{1,0:T(8,128)(2,1)} %wq.1, bf16[512,4,256]{2,1,0:T(4,128)(2,1)} %wkv.1, bf16[2,16,4096]{2,1,0:T(8,128)(2,1)} %samples.1), custom_call_target="tpu_custom_call" | custom-call | tf_op jit(solution)/shard_map/project_tokens/pallas_call | solution.py:142
  6.3 0.0 copy-start.2
  6.3 0.0 copy-start
  6.3 8.4 %all-to-all-start = ((bf16[16,144,128]{2,1,0:T(8,128)(2,1)}), bf16[16,144,128]{2,1,0:T(8,128)(2,1)S(1)}, u32[]{:S(2)}, u32[]{:S(2)}) async-start(bf16[16,144,128]{2,1,0:T(8,128)(2,1)} %project_tokens.1), calls=%async_computation | async-start | bytes 1179648 | tf_op jit(solution)/shard_map/all_to_all | solution.py:430
  14.8 0.0 copy-done.2
  14.8 0.1 copy.26
  14.9 0.0 copy-done
  14.9 9.6 %pack_rows.1.send.refs_4_ = bf16[16,128,4,256]{3,2,1,0:T(4,128)(2,1)} custom-call(s32[16,128]{1,0:T(8,128)S(1)} %bitcast.18, s32[16,2]{1,0:T(8,128)S(1)} %bitcast.13, bf16[2,2048,4,256]{3,2,1,0:T(4,128)(2,1)} %kv.1), custom_call_target="tpu_custom_call" | custom-call | tf_op jit(solution)/shard_map/pack_rows/pallas_call | solution.py:73
  24.5 6.5 %all-to-all-done.parts = bf16[16,144,128]{2,1,0:T(8,128)(2,1)S(1)} async-done(((bf16[16,144,128]{2,1,0:T(8,128)(2,1)}), bf16[16,144,128]{2,1,0:T(8,128)(2,1)S(1)}, u32[]{:S(2)}, u32[]{:S(2)}) %all-to-all-start) | async-done | bytes 589856 | tf_op jit(solution)/shard_map/all_to_all | solution.py:430
  31.1 0.8 settle_tokens.1
  31.8 0.5 head_moments.1
  32.4 1.0 collective-permute-start
  33.4 6.6 %collective-permute-done = bf16[1,4,144,128]{3,2,1,0:T(8,128)(2,1)S(1)} collective-permute-done((bf16[1,4,144,128]{3,2,1,0:T(8,128)(2,1)S(1)}, bf16[1,4,144,128]{3,2,1,0:T(8,128)(2,1)S(1)}, u32[]{:S(2)}, u32[]{:S(2)}) %collective-permute-start) | collective-permute-done | bytes 147488 | tf_op jit(solution)/shard_map/ppermute | solution.py:435
  40.1 0.1 collective-permute-start.1
  40.2 5.0 %all-to-all-start.1 = ((bf16[16,32,128]{2,1,0:T(8,128)(2,1)}), bf16[16,32,128]{2,1,0:T(8,128)(2,1)S(1)}, u32[]{:S(2)}, u32[]{:S(2)}) async-start(bf16[16,32,128]{2,1,0:T(8,128)(2,1)} %settle_tokens.1), calls=%async_computation.1 | async-start | bytes 262144 | tf_op jit(solution)/shard_map/all_to_all | solution.py:430
  45.2 1.7 collective-permute-done.1
  46.9 0.1 pad_maximum_fusion.2
  46.9 6.1 %all-to-all-done.1.query = bf16[16,32,128]{2,1,0:T(8,128)(2,1)S(1)} async-done(((bf16[16,32,128]{2,1,0:T(8,128)(2,1)}), bf16[16,32,128]{2,1,0:T(8,128)(2,1)S(1)}, u32[]{:S(2)}, u32[]{:S(2)}) %all-to-all-start.1) | async-done | bytes 131104 | tf_op jit(solution)/shard_map/all_to_all | solution.py:430
  53.0 4.7 %all-to-all-start.2 = ((bf16[16,128,4,256]{3,2,1,0:T(4,128)(2,1)}), bf16[16,128,4,256]{3,2,1,0:T(4,128)(2,1)}, u32[]{:S(2)}, u32[]{:S(2)}) async-start(bf16[16,128,4,256]{3,2,1,0:T(4,128)(2,1)} %pack_rows.1.send.refs_4_), calls=%async_computation.2 | async-start | bytes 8388608 | tf_op jit(solution)/shard_map/all_to_all | solution.py:430
  57.8 1.6 collective-permute-start.4
  59.4 1.5 collective-permute-start.2
  60.9 14.7 %collective-permute-done.4 = bf16[4,2,144,128]{3,2,1,0:T(8,128)(2,1)S(1)} collective-permute-done((bf16[4,2,144,128]{3,2,1,0:T(8,128)(2,1)S(1)}, bf16[4,2,144,128]{3,2,1,0:T(8,128)(2,1)S(1)}, u32[]{:S(2)}, u32[]{:S(2)}) %collective-permute-start.4) | collective-permute-done | bytes 294944 | tf_op jit(solution)/shard_map/ppermute | solution.py:435
  75.6 0.1 pad_maximum_fusion.4
  75.7 3.9 %collective-permute-start.5 = (bf16[8,2,144,128]{3,2,1,0:T(8,128)(2,1)S(1)}, bf16[8,2,144,128]{3,2,1,0:T(8,128)(2,1)S(1)}, u32[]{:S(2)}, u32[]{:S(2)}) collective-permute-start(bf16[8,2,144,128]{3,2,1,0:T(8,128)(2,1)S(1)} %pad_maximum_fusion.4), channel_id=1, source_target_pairs={{0,4},{2,6},{4,0},{6,2},{8,12},{10,14},{12,8},{14,10},{16,20},{18,... | collective-permute-start | bytes 1769480 | tf_op jit(solution)/shard_map/ppermute | solution.py:435
  79.6 13.0 %collective-permute-done.2 = bf16[4,2,144,128]{3,2,1,0:T(8,128)(2,1)S(1)} collective-permute-done((bf16[4,2,144,128]{3,2,1,0:T(8,128)(2,1)S(1)}, bf16[4,2,144,128]{3,2,1,0:T(8,128)(2,1)S(1)}, u32[]{:S(2)}, u32[]{:S(2)}) %collective-permute-start.2) | collective-permute-done | bytes 294944 | tf_op jit(solution)/shard_map/ppermute | solution.py:435
  92.6 0.1 pad_maximum_fusion.3
  92.7 1.1 collective-permute-start.3
  93.8 0.1 copy.20
  94.0 0.1 copy.22.bias
  94.1 6.4 %attend_kept.1.refs_5_ = f32[16,24,128]{2,1,0:T(8,128)S(1)} custom-call(s32[16,2]{1,0:T(8,128)S(1)} %bitcast.14, bf16[16,32,128]{2,1,0:T(8,128)(2,1)S(1)} %all-to-all-done.1.query, f32[16,512]{1,0:T(8,128)S(1)} %copy.22.bias, bf16[16,128,4,256]{3,2,1,0:T(4,128)(2,1)} %pack_rows.1.send.refs_4_), custom_call_target="tpu_custom_call" | custom-call | tf_op jit(solution)/shard_map/attend_kept/pallas_call | solution.py:254
  100.5 10.2 %collective-permute-done.5 = bf16[8,2,144,128]{3,2,1,0:T(8,128)(2,1)S(1)} collective-permute-done((bf16[8,2,144,128]{3,2,1,0:T(8,128)(2,1)S(1)}, bf16[8,2,144,128]{3,2,1,0:T(8,128)(2,1)S(1)}, u32[]{:S(2)}, u32[]{:S(2)}) %collective-permute-start.5) | collective-permute-done | bytes 589856 | tf_op jit(solution)/shard_map/ppermute | solution.py:435
  110.7 0.1 pad_maximum_fusion.1.refs_3_
  110.8 13.1 %collective-permute-done.3 = bf16[8,2,144,128]{3,2,1,0:T(8,128)(2,1)} collective-permute-done((bf16[8,2,144,128]{3,2,1,0:T(8,128)(2,1)S(1)}, bf16[8,2,144,128]{3,2,1,0:T(8,128)(2,1)}, u32[]{:S(2)}, u32[]{:S(2)}) %collective-permute-start.3) | collective-permute-done | bytes 589856 | tf_op jit(solution)/shard_map/ppermute | solution.py:435
  123.9 1.2 pad_maximum_fusion.refs_2_
  125.1 16.6 %score_kept.1 = f32[16,24,128]{2,1,0:T(8,128)} custom-call(s32[1]{0:T(128)} %bitcast.place.refs_0_, s32[16,2]{1,0:T(8,128)S(1)} %bitcast.15, bf16[16,2,144,128]{3,2,1,0:T(8,128)(2,1)S(1)} %pad_maximum_fusion.refs_2_, bf16[16,2,144,128]{3,2,1,0:T(8,128)(2,1)S(1)} %pad_maximum_fusion.1.refs_3_, bf16[16,128,4,256]{3,2,1,0:T(4,128)(2,1)} %pack_rows.1.send.refs_4_, ...), custom_call_target="tpu_custom_call" | custom-call | tf_op jit(solution)/shard_map/score_kept/pallas_call | solution.py:372
  141.7 0.0 all-to-all-done.2.arrived
  141.7 16.4 %all-to-all-start.3 = ((f32[16,24,128]{2,1,0:T(8,128)}), f32[16,24,128]{2,1,0:T(8,128)S(1)}, u32[]{:S(2)}, u32[]{:S(2)}) async-start(f32[16,24,128]{2,1,0:T(8,128)} %score_kept.1), calls=%async_computation.3 | async-start | bytes 393216 | tf_op jit(solution)/shard_map/all_to_all | solution.py:430
  158.0 4.5 %place_blocks.1 = bf16[16,128,4,256]{3,2,1,0:T(4,128)(2,1)} custom-call(s32[1]{0:T(128)} %bitcast.place.refs_0_, s32[16,2]{1,0:T(8,128)S(1)} %bitcast.16, bf16[16,128,4,256]{3,2,1,0:T(4,128)(2,1)} %all-to-all-done.2.arrived), custom_call_target="tpu_custom_call" | custom-call | tf_op jit(solution)/shard_map/place_blocks/pallas_call | solution.py:414
  162.6 3.5 %all-to-all-done.3.parts = f32[16,24,128]{2,1,0:T(8,128)S(1)} async-done(((f32[16,24,128]{2,1,0:T(8,128)}), f32[16,24,128]{2,1,0:T(8,128)S(1)}, u32[]{:S(2)}, u32[]{:S(2)}) %all-to-all-start.3) | async-done | bytes 196640 | tf_op jit(solution)/shard_map/all_to_all | solution.py:430
  166.1 1.6 combine_parts.1
  167.8 10.7 %all_to_all.25 = bf16[16,16,128]{2,1,0:T(8,128)(2,1)S(1)} all-to-all(bf16[16,16,128]{2,1,0:T(8,128)(2,1)S(1)} %get-tuple-element.18), channel_id=1, replica_groups=mesh['ctx'=16,'head'=2] {'ctx'}, dimensions={0} | all-to-all | bytes 131072 | tf_op jit(solution)/shard_map/all_to_all | solution.py:430
  178.5 2.8 %fusion = f32[8,512]{1,0:T(8,128)S(1)} fusion(bf16[4096,512]{1,0:T(8,128)(2,1)} %param.15, bf16[1,8,32,128]{3,2,1,0:T(8,128)(2,1)S(1)} %bitcast.22), kind=kOutput, calls=%fused_computation.6 | convolution fusion | flops 33554432 | bytes 4276224 | tf_op jit(solution)/shard_map/dot_general | solution.py:474
  181.3 3.4 %psum.7 = bf16[8,512]{1,0:T(8,128)(2,1)S(1)} all-reduce(f32[8,512]{1,0:T(8,128)S(1)} %fusion), channel_id=1, replica_groups=mesh['ctx'=16,'head'=2] {'head'}, use_global_device_ids=true, to_apply=%region_0.1 | all-reduce | flops 4096 | bytes 24576 | tf_op jit(solution)/shard_map/psum | solution.py:475
  184.7 0.6 reshape.38
  (5 shorter events, 0.1 us)
Async XLA Ops:
  0.6 0.7 copy-start.1
  6.3 8.5 %copy-start.2 = (s32[2,8,2]{1,2,0:T(2,128)S(1)}, s32[2,8,2]{1,2,0:T(2,128)}, u32[]{:S(2)}) copy-start(s32[2,8,2]{1,2,0:T(2,128)} %param.10) | copy-start | bytes 388
  6.3 8.6 %copy-start = (s32[2,8,128]{2,1,0:T(8,128)S(1)}, s32[2,8,128]{2,1,0:T(8,128)}, u32[]{:S(2)}) copy-start(s32[2,8,128]{2,1,0:T(8,128)} %param.9) | copy-start | bytes 24580
  6.3 24.7 %all-to-all-start = ((bf16[16,144,128]{2,1,0:T(8,128)(2,1)}), bf16[16,144,128]{2,1,0:T(8,128)(2,1)S(1)}, u32[]{:S(2)}, u32[]{:S(2)}) async-start(bf16[16,144,128]{2,1,0:T(8,128)(2,1)} %project_tokens.1), calls=%async_computation | async-start | bytes 1179648 | tf_op jit(solution)/shard_map/all_to_all | solution.py:430
  32.4 7.7 %collective-permute-start = (bf16[1,4,144,128]{3,2,1,0:T(8,128)(2,1)S(1)}, bf16[1,4,144,128]{3,2,1,0:T(8,128)(2,1)S(1)}, u32[]{:S(2)}, u32[]{:S(2)}) collective-permute-start(bf16[1,4,144,128]{3,2,1,0:T(8,128)(2,1)S(1)} %head_moments.1), channel_id=1, source_target_pairs={{0,16},{2,18},{4,20},{6,22},{8,24},{10,26},{12,28},{14,30},{16,0},... | collective-permute-start | bytes 442376 | tf_op jit(solution)/shard_map/ppermute | solution.py:435
  40.1 6.8 %collective-permute-start.1 = (bf16[2,4,144,128]{3,2,1,0:T(8,128)(2,1)S(1)}, bf16[2,4,144,128]{3,2,1,0:T(8,128)(2,1)S(1)}, u32[]{:S(2)}, u32[]{:S(2)}) collective-permute-start(bf16[2,4,144,128]{3,2,1,0:T(8,128)(2,1)S(1)} %pad_maximum_fusion.5), channel_id=1, source_target_pairs={{0,8},{2,10},{4,12},{6,14},{8,0},{10,2},{12,4},{14,6},{16,24},{18,... | collective-permute-start | bytes 884744 | tf_op jit(solution)/shard_map/ppermute | solution.py:435
  40.2 12.8 %all-to-all-start.1 = ((bf16[16,32,128]{2,1,0:T(8,128)(2,1)}), bf16[16,32,128]{2,1,0:T(8,128)(2,1)S(1)}, u32[]{:S(2)}, u32[]{:S(2)}) async-start(bf16[16,32,128]{2,1,0:T(8,128)(2,1)} %settle_tokens.1), calls=%async_computation.1 | async-start | bytes 262144 | tf_op jit(solution)/shard_map/all_to_all | solution.py:430
  53.0 88.7 %all-to-all-start.2 = ((bf16[16,128,4,256]{3,2,1,0:T(4,128)(2,1)}), bf16[16,128,4,256]{3,2,1,0:T(4,128)(2,1)}, u32[]{:S(2)}, u32[]{:S(2)}) async-start(bf16[16,128,4,256]{3,2,1,0:T(4,128)(2,1)} %pack_rows.1.send.refs_4_), calls=%async_computation.2 | async-start | bytes 8388608 | tf_op jit(solution)/shard_map/all_to_all | solution.py:430
  57.8 17.8 %collective-permute-start.4 = (bf16[4,2,144,128]{3,2,1,0:T(8,128)(2,1)S(1)}, bf16[4,2,144,128]{3,2,1,0:T(8,128)(2,1)S(1)}, u32[]{:S(2)}, u32[]{:S(2)}) collective-permute-start(bf16[4,2,144,128]{3,2,1,0:T(8,128)(2,1)S(1)} %get-tuple-element.19), channel_id=1, source_target_pairs={{0,2},{2,0},{4,6},{6,4},{8,10},{10,8},{12,14},{14,12},{16,18},{18,... | collective-permute-start | bytes 884744 | tf_op jit(solution)/shard_map/ppermute | solution.py:435
  59.4 33.2 %collective-permute-start.2 = (bf16[4,2,144,128]{3,2,1,0:T(8,128)(2,1)S(1)}, bf16[4,2,144,128]{3,2,1,0:T(8,128)(2,1)S(1)}, u32[]{:S(2)}, u32[]{:S(2)}) collective-permute-start(bf16[4,2,144,128]{3,2,1,0:T(8,128)(2,1)S(1)} %get-tuple-element.20), channel_id=1, source_target_pairs={{0,4},{2,6},{4,0},{6,2},{8,12},{10,14},{12,8},{14,10},{16,20},{18,... | collective-permute-start | bytes 884744 | tf_op jit(solution)/shard_map/ppermute | solution.py:435
  75.7 35.0 %collective-permute-start.5 = (bf16[8,2,144,128]{3,2,1,0:T(8,128)(2,1)S(1)}, bf16[8,2,144,128]{3,2,1,0:T(8,128)(2,1)S(1)}, u32[]{:S(2)}, u32[]{:S(2)}) collective-permute-start(bf16[8,2,144,128]{3,2,1,0:T(8,128)(2,1)S(1)} %pad_maximum_fusion.4), channel_id=1, source_target_pairs={{0,4},{2,6},{4,0},{6,2},{8,12},{10,14},{12,8},{14,10},{16,20},{18,... | collective-permute-start | bytes 1769480 | tf_op jit(solution)/shard_map/ppermute | solution.py:435
  92.7 31.2 %collective-permute-start.3 = (bf16[8,2,144,128]{3,2,1,0:T(8,128)(2,1)S(1)}, bf16[8,2,144,128]{3,2,1,0:T(8,128)(2,1)}, u32[]{:S(2)}, u32[]{:S(2)}) collective-permute-start(bf16[8,2,144,128]{3,2,1,0:T(8,128)(2,1)S(1)} %pad_maximum_fusion.3), channel_id=1, source_target_pairs={{0,2},{2,0},{4,6},{6,4},{8,10},{10,8},{12,14},{14,12},{16,18},{18,... | collective-permute-start | bytes 1769480 | tf_op jit(solution)/shard_map/ppermute | solution.py:435
  141.7 24.4 %all-to-all-start.3 = ((f32[16,24,128]{2,1,0:T(8,128)}), f32[16,24,128]{2,1,0:T(8,128)S(1)}, u32[]{:S(2)}, u32[]{:S(2)}) async-start(f32[16,24,128]{2,1,0:T(8,128)} %score_kept.1), calls=%async_computation.3 | async-start | bytes 393216 | tf_op jit(solution)/shard_map/all_to_all | solution.py:430

commit v3 on v2

--- a/solution.py
+++ b/solution.py
@@ -16,7 +16,6 @@
 F32 = jnp.float32
 STAT = 144
 LARGE = 1e30
-VMEM_LIMIT = 48 << 20
 ANY = pl.BlockSpec(memory_space=pltpu.HBM)
 SMEM = pl.BlockSpec(memory_space=pltpu.SMEM)
 VMEM = pl.BlockSpec(memory_space=pltpu.VMEM)
@@ -28,8 +27,8 @@
     return pltpu.with_memory_space_constraint(value, pltpu.HBM)
 
 
-def params():
-    return pltpu.CompilerParams(vmem_limit_bytes=VMEM_LIMIT)
+def params(megabytes=8):
+    return pltpu.CompilerParams(vmem_limit_bytes=megabytes << 20)
 
 
 def pack_kernel(keep, target, kv, send, spans, blocks, in_sem, out_sem):
@@ -81,35 +80,43 @@
             pltpu.SemaphoreType.DMA((items,)),
             pltpu.SemaphoreType.DMA((items,)),
         ],
+        compiler_params=params(20),
+        name="pack_rows",
+    )(keep, target, hbm(kv_cache))
+
+
+def split_kernel(samples, out):
+    for r in range(2):
+        for c in range(32):
+            out[r * 8 + c // 4, (c % 4) * 16 : (c % 4) * 16 + 16, :] = samples[
+                r, :, c * 128 : c * 128 + 128
+            ]
+
+
+def split_samples(samples):
+    return pl.pallas_call(
+        split_kernel,
+        out_shape=jax.ShapeDtypeStruct((16, 64, 128), BF),
+        in_specs=[VMEM],
+        out_specs=VMEM,
         compiler_params=params(),
-        name="pack_rows",
-    )(keep, target, kv_cache)
-
-
-def terms(value):
-    high = value.astype(BF).astype(F32)
-    middle = (value - high).astype(BF).astype(F32)
-    return high, middle, value - high - middle
-
-
-def project_kernel(tokens, wq, wkv, samples, out, rows, extra):
+        name="split_samples",
+    )(samples)
+
+
+def project_kernel(tokens, wq, wkv, out):
     i = pl.program_id(0)
     x = jnp.concatenate([tokens[t, r : r + 1, :].astype(F32) for r in range(2) for t in range(4)], axis=0)
     x = x.astype(BF)
     part = jnp.dot(x, wq[...], preferred_element_type=F32)
     for r in range(2):
         for g in range(8):
-            rows[r * 8 + i * 2 + g // 4, (g % 4) * 4 : (g % 4) * 4 + 4, :] = part[
+            out[r * 8 + i * 2 + g // 4, (g % 4) * 4 : (g % 4) * 4 + 4, :] = part[
                 r * 4 : r * 4 + 4, g * 128 : g * 128 + 128
             ]
 
     @pl.when(i == 0)
     def _():
-        for r in range(2):
-            for c in range(32):
-                out[r * 8 + c // 4, (c % 4) * 16 : (c % 4) * 16 + 16, :] = samples[
-                    r, :, c * 128 : c * 128 + 128
-                ]
         heads = pltpu.einshape("nhd->hnd", wkv[...])
         wide = x.astype(F32)
         squares = jnp.sum(wide * wide, axis=1, keepdims=True)
@@ -118,60 +125,55 @@
         line = jnp.sum(jnp.where(row == lane, squares, 0.0), axis=0, keepdims=True)
         line = jnp.concatenate([line, jnp.zeros((3, 128), F32)], axis=0)
         for p in range(16):
-            extra[p, 4:8, :] = line
+            out[p, 20:24, :] = line
         for j in range(4):
             pair = jnp.dot(x, heads[j], preferred_element_type=F32)
             for r in range(2):
                 for half in range(2):
-                    extra[r * 8 + j * 2 + half, 0:4, :] = pair[
+                    out[r * 8 + j * 2 + half, 16:20, :] = pair[
                         r * 4 : r * 4 + 4, half * 128 : half * 128 + 128
                     ]
 
-    @pl.when(i == 3)
-    def _():
-        for at, term in enumerate(terms(rows[...])):
-            out[:, 64 + at * 16 : 80 + at * 16, :] = term.astype(BF)
-        first, second, third = terms(extra[...])
-        out[:, 112:128, :] = jnp.concatenate([first, second], axis=1).astype(BF)
-        out[:, 128:144, :] = jnp.concatenate([third, jnp.zeros((16, 8, 128), F32)], axis=1).astype(BF)
-
-
-def project(tokens, w_query, w_keyval, samples):
+
+def project(tokens, w_query, w_keyval):
     depth, columns = w_query.shape
     step = columns // 4
     return pl.pallas_call(
         project_kernel,
-        out_shape=jax.ShapeDtypeStruct((16, 144, 128), BF),
+        out_shape=jax.ShapeDtypeStruct((16, 24, 128), F32),
         grid=(4,),
         in_specs=[
             pl.BlockSpec(tokens.shape, lambda i: (0, 0, 0)),
             pl.BlockSpec((depth, step), lambda i: (0, i)),
             pl.BlockSpec(w_keyval.shape, lambda i: (0, 0, 0)),
-            pl.BlockSpec(samples.shape, lambda i: (0, 0, 0)),
         ],
-        out_specs=pl.BlockSpec((16, 144, 128), lambda i: (0, 0, 0)),
-        scratch_shapes=[pltpu.VMEM((16, 16, 128), F32), pltpu.VMEM((16, 8, 128), F32)],
+        out_specs=pl.BlockSpec((16, 24, 128), lambda i: (0, 0, 0)),
+        compiler_params=params(16),
+        name="project_tokens",
+    )(hbm(tokens), hbm(w_query), hbm(w_keyval))
+
+
+def normalize_kernel(place, parts, out):
+    total = jnp.sum(parts[...], axis=0)
+    request = place[0] // 8
+    row = lax.broadcasted_iota(jnp.int32, (24, 128), 0)
+    lane = lax.broadcasted_iota(jnp.int32, (24, 128), 1)
+    squares = jnp.where(lane == request * 4 + row % 4, total[20:21, :], 0.0)
+    inverse = lax.rsqrt(jnp.sum(squares, axis=1, keepdims=True) / D + EPSILON)
+    scaled = jnp.where(row < 20, total * inverse, 0.0)
+    rounded = jnp.concatenate([scaled, jnp.zeros((8, 128), F32)], axis=0).astype(BF)
+    out[...] = jnp.broadcast_to(rounded[None], out.shape)
+
+
+def normalize(place, parts):
+    return pl.pallas_call(
+        normalize_kernel,
+        out_shape=jax.ShapeDtypeStruct((16, 32, 128), BF),
+        in_specs=[SMEM, VMEM],
+        out_specs=VMEM,
         compiler_params=params(),
-        name="project_tokens",
-    )(tokens, hbm(w_query), hbm(w_keyval), hbm(samples))
-
-
-def settle_kernel(place, parts, out):
-    request = place[0] // 8
-    total = jnp.sum(parts[:, 64:80, :].astype(F32), axis=0)
-    total = total + jnp.sum(parts[:, 80:96, :].astype(F32), axis=0)
-    total = total + jnp.sum(parts[:, 96:112, :].astype(F32), axis=0)
-    both = jnp.sum(parts[:, 112:128, :].astype(F32), axis=0)
-    rest = jnp.sum(parts[:, 128:144, :].astype(F32), axis=0)
-    both = both[0:8] + both[8:16] + rest[0:8]
-    row = lax.broadcasted_iota(jnp.int32, (16, 128), 0)
-    lane = lax.broadcasted_iota(jnp.int32, (16, 128), 1)
-    squares = jnp.where(lane == request * 4 + row % 4, both[4:5, :], 0.0)
-    inverse = lax.rsqrt(jnp.sum(squares, axis=1, keepdims=True) / D + EPSILON)
-    own = total * inverse
-    fresh = jnp.where(row[0:8] < 4, both * inverse[0:8], 0.0)
-    rounded = jnp.concatenate([own, fresh, jnp.zeros((8, 128), F32)], axis=0).astype(BF)
-    out[...] = jnp.broadcast_to(rounded[None], out.shape)
+        name="normalize_tokens",
+    )(place, parts)
 
 
 def moments_kernel(parts, stat):
@@ -187,17 +189,6 @@
         lines = jnp.concatenate([high, scaled - high, jnp.zeros((14, 128), F32)], axis=0)
         stat[0, i, 0:128, :] = cov.astype(BF)
         stat[0, i, 128:144, :] = lines.astype(BF)
-
-
-def settle(place, parts):
-    return pl.pallas_call(
-        settle_kernel,
-        out_shape=jax.ShapeDtypeStruct((16, 32, 128), BF),
-        in_specs=[SMEM, VMEM],
-        out_specs=VMEM,
-        compiler_params=params(),
-        name="settle_tokens",
-    )(place, parts)
 
 
 def head_moments(parts):
@@ -261,7 +252,7 @@
             pltpu.VMEM((128, 8 * width * 4), F32),
             pltpu.SemaphoreType.DMA((items,)),
         ],
-        compiler_params=params(),
+        compiler_params=params(16),
         name="attend_kept",
     )(target, query, bias, hbm(send))
 
@@ -378,7 +369,7 @@
             pltpu.VMEM(send.shape, send.dtype),
             pltpu.SemaphoreType.DMA((items,)),
         ],
-        compiler_params=params(),
+        compiler_params=params(24),
         name="score_kept",
     )(place, target, stat_a, stat_b, hbm(send), parts)
 
@@ -426,6 +417,31 @@
     )(place, target, hbm(arrived))
 
 
+def finish_kernel(joined, w, out, rows):
+    for r in range(2):
+        for h in range(32):
+            at = (h % 4) * 4
+            rows[r * 4 : r * 4 + 4, h * 128 : h * 128 + 128] = joined[
+                r * 8 + h // 4, at : at + 4, :
+            ].astype(F32)
+    value = jnp.dot(rows[...].astype(BF), w[...], preferred_element_type=F32)
+    for r in range(2):
+        for t in range(4):
+            out[t, r : r + 1, :] = value[r * 4 + t : r * 4 + t + 1, :]
+
+
+def finish(joined, w_out):
+    return pl.pallas_call(
+        finish_kernel,
+        out_shape=jax.ShapeDtypeStruct((4, 2, w_out.shape[1]), F32),
+        in_specs=[VMEM, VMEM],
+        out_specs=VMEM,
+        scratch_shapes=[pltpu.VMEM((8, w_out.shape[0]), F32)],
+        compiler_params=params(),
+        name="project_out",
+    )(joined, w_out)
+
+
 def exchange(value):
     return lax.all_to_all(value, "ctx", split_axis=0, concat_axis=0, tiled=True)
 
@@ -451,13 +467,13 @@
     keep = keep_rows.reshape(items, width)
     target = block_target.reshape(items, 2)
     place = lax.axis_index("ctx").astype(jnp.int32).reshape(1)
-    parts = exchange(project(new_tokens, w_query, w_keyval, future_queries))
-    send = pack(kv_cache, keep, target)
-    parts = after(parts, send)
-    own = settle(place, parts)
-    query = exchange(own)
-    stat = head_moments(after(parts, own))
-    stat = doubled(doubled(stat, 8), 4)
+    samples = exchange(split_samples(future_queries))
+    parts, samples = lax.optimization_barrier((project(new_tokens, w_query, w_keyval), samples))
+    parts = exchange(parts)
+    stat = doubled(head_moments(samples), 8)
+    send = pack(kv_cache, after(keep, samples), target)
+    stat = doubled(after(stat, send), 4)
+    query = exchange(normalize(place, after(parts, send)))
     arrived = exchange(after(send, (query, stat)))
     bias = jnp.where(after(keep, query) < 2 * width, 0.0, -LARGE).astype(F32)
     bias = jnp.broadcast_to(bias[:, :, None], (items, width, 4)).reshape(items, width * 4)
@@ -469,10 +485,7 @@
     packed = put_blocks(place, target, arrived)
     share, scores = combine(place, target, after(parts, packed), query)
     attended = exchange(share)
-    rows = attended.reshape(requests, 32, 4, 128)
-    rows = jnp.transpose(rows, (2, 0, 1, 3)).reshape(8, 4096)
-    partial_value = jnp.dot(rows, w_out, preferred_element_type=F32)
-    decoded = lax.psum(partial_value, "head").astype(BF).reshape(4, requests, w_out.shape[1])
+    decoded = lax.psum(finish(attended, w_out), "head").astype(BF)
     return packed.reshape(requests, lists * width, local_kv, pair), scores, decoded
 
 

time: 186 us -> 180 us (0.968)
  waiting for transfers between devices: 75.5 us -> 64.7 us
  starting transfers between devices: 43.8 us -> 47.7 us
  matrix products: 2.83 us -> 0 us
  local copies, waits for them, and re-layouts: 1.69 us -> 3.58 us
    ppermute x6, waiting for transfers between devices: 59.3 us -> 48.4 us  [doubled(): return jnp.concatenate([value, lax.ppermute(value, 'ctx', pairs)], axis=0)]
    dot_general x1 -> x0, matrix products: 2.83 us -> none  [sixteen(): partial_value = jnp.dot(rows, w_out, preferred_element_type=F32)]
    unnamed x6 -> x9, local copies, waits for them, and re-layouts: 0.7 us -> 3.16 us
    ppermute x6, starting transfers between devices: 9.29 us -> 11.5 us  [doubled(): return jnp.concatenate([value, lax.ppermute(value, 'ctx', pairs)], axis=0)]
    all_to_all x4 -> x5, starting transfers between devices: 34.6 us -> 36.2 us  [exchange(): return lax.all_to_all(value, 'ctx', split_axis=0, concat_axis=0, tiled=True)]
    pallas_call x2 -> x4, Pallas kernels: 5.78 us -> 6.95 us  [the longest x1 4.79 us: project(): pl.pallas_call(project_kernel, out_shape=jax.ShapeDtypeStruct((16, 24, 12...]
    all_to_all x4 -> x5, waiting for transfers between devices: 16.2 us -> 16.3 us  [exchange(): return lax.all_to_all(value, 'ctx', split_axis=0, concat_axis=0, tiled=True)]
  transfers between devices with their start and end apart: 10 -> 11, of which waited for: 9 -> 7; matrix products, arithmetic and copies ran while one was open for 1% -> 1% of each run, Pallas kernels for 20% -> 24%
where the time goes in v3:
time: 180 us; the launch traced here: 179 us
  waiting for transfers between devices  64.7 us (36%)
  starting transfers between devices  47.7 us (26%)
  Pallas kernels  46.3 us (26%)
  blocking collectives  14.7 us (8%)
  local copies, waits for them, and re-layouts  3.58 us (2%)
    ppermute x6, waiting for transfers between devices, doubled(): return jnp.concatenate([value, lax.ppermute(value, 'ctx', pairs)], axis=0)  48.4 us
    all_to_all x5, starting transfers between devices, exchange(): return lax.all_to_all(value, 'ctx', split_axis=0, concat_axis=0, tiled=True)  36.2 us
    pallas_call x1, Pallas kernels, score(): pl.pallas_call(kernel, out_shape=jax.ShapeDtypeStruct(parts.shape, parts....  16.6 us
    all_to_all x5, waiting for transfers between devices, exchange(): return lax.all_to_all(value, 'ctx', split_axis=0, concat_axis=0, tiled=True)  16.3 us
    ppermute x6, starting transfers between devices, doubled(): return jnp.concatenate([value, lax.ppermute(value, 'ctx', pairs)], axis=0)  11.5 us
    all_to_all x1, blocking collectives, exchange(): return lax.all_to_all(value, 'ctx', split_axis=0, concat_axis=0, tiled=True)  10.7 us
    pallas_call x1, Pallas kernels, pack(): pl.pallas_call(pack_kernel, out_shape=pltpu.HBM((items, width, *tail), kv...  9.62 us
    pallas_call x1, Pallas kernels, attend(): pl.pallas_call(attend_kernel, out_shape=jax.ShapeDtypeStruct((16, 24, 128...  6.41 us
  transfers between devices with their start and end apart: 11, of which 7 were waited for; matrix products, arithmetic and copies ran while one was open for 1% of the time, Pallas kernels for 24%

profile of v3, /device:TPU:0, one launch (start us, length us, event | category | flops | bytes accessed | tf_op | source)
XLA Modules:
  0.0 179.2 jit_solution(14546349927472350879)
XLA Ops:
  0.6 0.0 copy-start.1
  0.6 0.9 copy-done.1
  1.6 0.7 split_samples.1
  2.3 8.3 %all-to-all-start = ((bf16[16,64,128]{2,1,0:T(8,128)(2,1)}), bf16[16,64,128]{2,1,0:T(8,128)(2,1)S(1)}, u32[]{:S(2)}, u32[]{:S(2)}) async-start(bf16[16,64,128]{2,1,0:T(8,128)(2,1)} %split_samples.1), calls=%async_computation | async-start | bytes 524288 | tf_op jit(solution)/shard_map/all_to_all | solution.py:446
  10.6 0.0 copy-start.3
  10.7 0.0 copy-start.2
  10.7 4.8 %project_tokens.1 = f32[16,24,128]{2,1,0:T(8,128)} custom-call(bf16[4,2,512]{2,1,0:T(2,128)(2,1)} %tokens.1, bf16[512,4096]{1,0:T(8,128)(2,1)} %wq.1, bf16[512,4,256]{2,1,0:T(4,128)(2,1)} %wkv.1), custom_call_target="tpu_custom_call" | custom-call | tf_op jit(solution)/shard_map/project_tokens/pallas_call | solution.py:141
  15.5 5.1 %all-to-all-done.parts = bf16[16,64,128]{2,1,0:T(8,128)(2,1)S(1)} async-done(((bf16[16,64,128]{2,1,0:T(8,128)(2,1)}), bf16[16,64,128]{2,1,0:T(8,128)(2,1)S(1)}, u32[]{:S(2)}, u32[]{:S(2)}) %all-to-all-start) | async-done | bytes 262176 | tf_op jit(solution)/shard_map/all_to_all | solution.py:446
  20.5 0.5 head_moments.1
  21.0 0.7 collective-permute-start
  21.8 4.3 %all-to-all-start.1 = ((f32[16,24,128]{2,1,0:T(8,128)}), f32[16,24,128]{2,1,0:T(8,128)S(1)}, u32[]{:S(2)}, u32[]{:S(2)}) async-start(f32[16,24,128]{2,1,0:T(8,128)} %project_tokens.1), calls=%async_computation.1 | async-start | bytes 393216 | tf_op jit(solution)/shard_map/all_to_all | solution.py:446
  26.1 0.0 copy-done.3
  26.1 0.1 copy.25
  26.2 0.0 copy-done.2
  26.2 9.6 %pack_rows.1.send.refs_4_ = bf16[16,128,4,256]{3,2,1,0:T(4,128)(2,1)} custom-call(s32[16,128]{1,0:T(8,128)S(1)} %bitcast.10, s32[16,2]{1,0:T(8,128)S(1)} %bitcast.5, bf16[2,2048,4,256]{3,2,1,0:T(4,128)(2,1)} %kv.1), custom_call_target="tpu_custom_call" | custom-call | tf_op jit(solution)/shard_map/pack_rows/pallas_call | solution.py:72
  35.8 0.0 collective-permute-done
  35.9 2.0 %collective-permute-start.1 = (bf16[2,4,144,128]{3,2,1,0:T(8,128)(2,1)S(1)}, bf16[2,4,144,128]{3,2,1,0:T(8,128)(2,1)S(1)}, u32[]{:S(2)}, u32[]{:S(2)}) collective-permute-start(bf16[2,4,144,128]{3,2,1,0:T(8,128)(2,1)S(1)} %pad_maximum_fusion.4), channel_id=1, source_target_pairs={{0,8},{2,10},{4,12},{6,14},{8,0},{10,2},{12,4},{14,6},{16,24},{18,... | collective-permute-start | bytes 884744 | tf_op jit(solution)/shard_map/ppermute | solution.py:451
  37.9 0.0 all-to-all-done.1.parts
  37.9 0.8 normalize_tokens.1
  38.7 5.5 %all-to-all-start.2 = ((bf16[16,32,128]{2,1,0:T(8,128)(2,1)}), bf16[16,32,128]{2,1,0:T(8,128)(2,1)S(1)}, u32[]{:S(2)}, u32[]{:S(2)}) async-start(bf16[16,32,128]{2,1,0:T(8,128)(2,1)} %normalize_tokens.1), calls=%async_computation.2 | async-start | bytes 262144 | tf_op jit(solution)/shard_map/all_to_all | solution.py:446
  44.2 0.0 collective-permute-done.1
  44.3 7.7 %all-to-all-done.2.query = bf16[16,32,128]{2,1,0:T(8,128)(2,1)S(1)} async-done(((bf16[16,32,128]{2,1,0:T(8,128)(2,1)}), bf16[16,32,128]{2,1,0:T(8,128)(2,1)S(1)}, u32[]{:S(2)}, u32[]{:S(2)}) %all-to-all-start.2) | async-done | bytes 131104 | tf_op jit(solution)/shard_map/all_to_all | solution.py:446
  52.0 4.7 %all-to-all-start.3 = ((bf16[16,128,4,256]{3,2,1,0:T(4,128)(2,1)}), bf16[16,128,4,256]{3,2,1,0:T(4,128)(2,1)}, u32[]{:S(2)}, u32[]{:S(2)}) async-start(bf16[16,128,4,256]{3,2,1,0:T(4,128)(2,1)} %pack_rows.1.send.refs_4_), calls=%async_computation.3 | async-start | bytes 8388608 | tf_op jit(solution)/shard_map/all_to_all | solution.py:446
  56.8 1.6 collective-permute-start.4
  58.4 1.5 collective-permute-start.2
  59.9 12.9 %collective-permute-done.4 = bf16[4,2,144,128]{3,2,1,0:T(8,128)(2,1)S(1)} collective-permute-done((bf16[4,2,144,128]{3,2,1,0:T(8,128)(2,1)S(1)}, bf16[4,2,144,128]{3,2,1,0:T(8,128)(2,1)S(1)}, u32[]{:S(2)}, u32[]{:S(2)}) %collective-permute-start.4) | collective-permute-done | bytes 294944 | tf_op jit(solution)/shard_map/ppermute | solution.py:451
  72.8 0.1 pad_maximum_fusion.3
  72.8 3.6 %collective-permute-start.5 = (bf16[8,2,144,128]{3,2,1,0:T(8,128)(2,1)S(1)}, bf16[8,2,144,128]{3,2,1,0:T(8,128)(2,1)S(1)}, u32[]{:S(2)}, u32[]{:S(2)}) collective-permute-start(bf16[8,2,144,128]{3,2,1,0:T(8,128)(2,1)S(1)} %pad_maximum_fusion.3), channel_id=1, source_target_pairs={{0,4},{2,6},{4,0},{6,2},{8,12},{10,14},{12,8},{14,10},{16,20},{18,... | collective-permute-start | bytes 1769480 | tf_op jit(solution)/shard_map/ppermute | solution.py:451
  76.4 12.6 %collective-permute-done.2 = bf16[4,2,144,128]{3,2,1,0:T(8,128)(2,1)S(1)} collective-permute-done((bf16[4,2,144,128]{3,2,1,0:T(8,128)(2,1)S(1)}, bf16[4,2,144,128]{3,2,1,0:T(8,128)(2,1)S(1)}, u32[]{:S(2)}, u32[]{:S(2)}) %collective-permute-start.2) | collective-permute-done | bytes 294944 | tf_op jit(solution)/shard_map/ppermute | solution.py:451
  89.0 0.1 pad_maximum_fusion.2
  89.0 2.1 %collective-permute-start.3 = (bf16[8,2,144,128]{3,2,1,0:T(8,128)(2,1)S(1)}, bf16[8,2,144,128]{3,2,1,0:T(8,128)(2,1)}, u32[]{:S(2)}, u32[]{:S(2)}) collective-permute-start(bf16[8,2,144,128]{3,2,1,0:T(8,128)(2,1)S(1)} %pad_maximum_fusion.2), channel_id=1, source_target_pairs={{0,2},{2,0},{4,6},{6,4},{8,10},{10,8},{12,14},{14,12},{16,18},{18,... | collective-permute-start | bytes 1769480 | tf_op jit(solution)/shard_map/ppermute | solution.py:451
  91.1 0.1 copy.20
  91.3 0.1 copy.22.bias
  91.4 6.4 %attend_kept.1.refs_5_ = f32[16,24,128]{2,1,0:T(8,128)S(1)} custom-call(s32[16,2]{1,0:T(8,128)S(1)} %bitcast.6, bf16[16,32,128]{2,1,0:T(8,128)(2,1)S(1)} %all-to-all-done.2.query, f32[16,512]{1,0:T(8,128)S(1)} %copy.22.bias, bf16[16,128,4,256]{3,2,1,0:T(4,128)(2,1)} %pack_rows.1.send.refs_4_), custom_call_target="tpu_custom_call" | custom-call | tf_op jit(solution)/shard_map/attend_kept/pallas_call | solution.py:245
  97.8 10.0 %collective-permute-done.5 = bf16[8,2,144,128]{3,2,1,0:T(8,128)(2,1)S(1)} collective-permute-done((bf16[8,2,144,128]{3,2,1,0:T(8,128)(2,1)S(1)}, bf16[8,2,144,128]{3,2,1,0:T(8,128)(2,1)S(1)}, u32[]{:S(2)}, u32[]{:S(2)}) %collective-permute-start.5) | collective-permute-done | bytes 589856 | tf_op jit(solution)/shard_map/ppermute | solution.py:451
  107.8 0.1 pad_maximum_fusion.1.refs_3_
  108.0 12.9 %collective-permute-done.3 = bf16[8,2,144,128]{3,2,1,0:T(8,128)(2,1)} collective-permute-done((bf16[8,2,144,128]{3,2,1,0:T(8,128)(2,1)S(1)}, bf16[8,2,144,128]{3,2,1,0:T(8,128)(2,1)}, u32[]{:S(2)}, u32[]{:S(2)}) %collective-permute-start.3) | collective-permute-done | bytes 589856 | tf_op jit(solution)/shard_map/ppermute | solution.py:451
  120.9 1.2 pad_maximum_fusion.refs_2_
  122.1 16.6 %score_kept.1 = f32[16,24,128]{2,1,0:T(8,128)} custom-call(s32[1]{0:T(128)} %bitcast.place.refs_0_, s32[16,2]{1,0:T(8,128)S(1)} %bitcast.7, bf16[16,2,144,128]{3,2,1,0:T(8,128)(2,1)S(1)} %pad_maximum_fusion.refs_2_, bf16[16,2,144,128]{3,2,1,0:T(8,128)(2,1)S(1)} %pad_maximum_fusion.1.refs_3_, bf16[16,128,4,256]{3,2,1,0:T(4,128)(2,1)} %pack_rows.1.send.refs_4_, ...), custom_call_target="tpu_custom_call" | custom-call | tf_op jit(solution)/shard_map/score_kept/pallas_call | solution.py:363
  138.6 0.0 all-to-all-done.3.arrived
  138.6 13.3 %all-to-all-start.4 = ((f32[16,24,128]{2,1,0:T(8,128)}), f32[16,24,128]{2,1,0:T(8,128)S(1)}, u32[]{:S(2)}, u32[]{:S(2)}) async-start(f32[16,24,128]{2,1,0:T(8,128)} %score_kept.1), calls=%async_computation.4 | async-start | bytes 393216 | tf_op jit(solution)/shard_map/all_to_all | solution.py:446
  151.9 4.5 %place_blocks.1 = bf16[16,128,4,256]{3,2,1,0:T(4,128)(2,1)} custom-call(s32[1]{0:T(128)} %bitcast.place.refs_0_, s32[16,2]{1,0:T(8,128)S(1)} %bitcast.8, bf16[16,128,4,256]{3,2,1,0:T(4,128)(2,1)} %all-to-all-done.3.arrived), custom_call_target="tpu_custom_call" | custom-call | tf_op jit(solution)/shard_map/place_blocks/pallas_call | solution.py:405
  156.5 3.5 %all-to-all-done.4.parts = f32[16,24,128]{2,1,0:T(8,128)S(1)} async-done(((f32[16,24,128]{2,1,0:T(8,128)}), f32[16,24,128]{2,1,0:T(8,128)S(1)}, u32[]{:S(2)}, u32[]{:S(2)}) %all-to-all-start.4) | async-done | bytes 196640 | tf_op jit(solution)/shard_map/all_to_all | solution.py:446
  160.0 1.7 combine_parts.1
  161.7 10.7 %all_to_all.30.joined = bf16[16,16,128]{2,1,0:T(8,128)(2,1)S(1)} all-to-all(bf16[16,16,128]{2,1,0:T(8,128)(2,1)S(1)} %get-tuple-element.24), channel_id=1, replica_groups=mesh['ctx'=16,'head'=2] {'ctx'}, dimensions={0} | all-to-all | bytes 131072 | tf_op jit(solution)/shard_map/all_to_all | solution.py:446
  172.4 0.0 copy-start
  172.4 2.2 %copy-done = bf16[4096,512]{1,0:T(8,128)(2,1)S(1)} copy-done((bf16[4096,512]{1,0:T(8,128)(2,1)S(1)}, bf16[4096,512]{1,0:T(8,128)(2,1)}, u32[]{:S(2)}) %copy-start) | copy-done | bytes 4194328
  174.6 0.7 project_out.1
  175.2 4.0 %psum.7 = bf16[4,2,512]{2,1,0:T(2,128)(2,1)} all-reduce(f32[4,2,512]{2,1,0:T(2,128)S(1)} %project_out.1), channel_id=1, replica_groups=mesh['ctx'=16,'head'=2] {'head'}, use_global_device_ids=true, to_apply=%region_0.1 | all-reduce | flops 4096 | bytes 24576 | tf_op jit(solution)/shard_map/psum | solution.py:488
  (6 shorter events, 0.2 us)
Async XLA Ops:
  0.6 1.0 copy-start.1
  2.3 18.2 %all-to-all-start = ((bf16[16,64,128]{2,1,0:T(8,128)(2,1)}), bf16[16,64,128]{2,1,0:T(8,128)(2,1)S(1)}, u32[]{:S(2)}, u32[]{:S(2)}) async-start(bf16[16,64,128]{2,1,0:T(8,128)(2,1)} %split_samples.1), calls=%async_computation | async-start | bytes 524288 | tf_op jit(solution)/shard_map/all_to_all | solution.py:446
  10.6 15.5 %copy-start.3 = (s32[2,8,2]{1,2,0:T(2,128)S(1)}, s32[2,8,2]{1,2,0:T(2,128)}, u32[]{:S(2)}) copy-start(s32[2,8,2]{1,2,0:T(2,128)} %param.10) | copy-start | bytes 388
  10.7 15.6 %copy-start.2 = (s32[2,8,128]{2,1,0:T(8,128)S(1)}, s32[2,8,128]{2,1,0:T(8,128)}, u32[]{:S(2)}) copy-start(s32[2,8,128]{2,1,0:T(8,128)} %param.9) | copy-start | bytes 24580
  21.0 14.8 %collective-permute-start = (bf16[1,4,144,128]{3,2,1,0:T(8,128)(2,1)S(1)}, bf16[1,4,144,128]{3,2,1,0:T(8,128)(2,1)S(1)}, u32[]{:S(2)}, u32[]{:S(2)}) collective-permute-start(bf16[1,4,144,128]{3,2,1,0:T(8,128)(2,1)S(1)} %head_moments.1), channel_id=1, source_target_pairs={{0,16},{2,18},{4,20},{6,22},{8,24},{10,26},{12,28},{14,30},{16,0},... | collective-permute-start | bytes 442376 | tf_op jit(solution)/shard_map/ppermute | solution.py:451
  21.8 16.1 %all-to-all-start.1 = ((f32[16,24,128]{2,1,0:T(8,128)}), f32[16,24,128]{2,1,0:T(8,128)S(1)}, u32[]{:S(2)}, u32[]{:S(2)}) async-start(f32[16,24,128]{2,1,0:T(8,128)} %project_tokens.1), calls=%async_computation.1 | async-start | bytes 393216 | tf_op jit(solution)/shard_map/all_to_all | solution.py:446
  35.9 8.3 %collective-permute-start.1 = (bf16[2,4,144,128]{3,2,1,0:T(8,128)(2,1)S(1)}, bf16[2,4,144,128]{3,2,1,0:T(8,128)(2,1)S(1)}, u32[]{:S(2)}, u32[]{:S(2)}) collective-permute-start(bf16[2,4,144,128]{3,2,1,0:T(8,128)(2,1)S(1)} %pad_maximum_fusion.4), channel_id=1, source_target_pairs={{0,8},{2,10},{4,12},{6,14},{8,0},{10,2},{12,4},{14,6},{16,24},{18,... | collective-permute-start | bytes 884744 | tf_op jit(solution)/shard_map/ppermute | solution.py:451
  38.7 13.3 %all-to-all-start.2 = ((bf16[16,32,128]{2,1,0:T(8,128)(2,1)}), bf16[16,32,128]{2,1,0:T(8,128)(2,1)S(1)}, u32[]{:S(2)}, u32[]{:S(2)}) async-start(bf16[16,32,128]{2,1,0:T(8,128)(2,1)} %normalize_tokens.1), calls=%async_computation.2 | async-start | bytes 262144 | tf_op jit(solution)/shard_map/all_to_all | solution.py:446
  52.0 86.6 %all-to-all-start.3 = ((bf16[16,128,4,256]{3,2,1,0:T(4,128)(2,1)}), bf16[16,128,4,256]{3,2,1,0:T(4,128)(2,1)}, u32[]{:S(2)}, u32[]{:S(2)}) async-start(bf16[16,128,4,256]{3,2,1,0:T(4,128)(2,1)} %pack_rows.1.send.refs_4_), calls=%async_computation.3 | async-start | bytes 8388608 | tf_op jit(solution)/shard_map/all_to_all | solution.py:446
  56.8 16.0 %collective-permute-start.4 = (bf16[4,2,144,128]{3,2,1,0:T(8,128)(2,1)S(1)}, bf16[4,2,144,128]{3,2,1,0:T(8,128)(2,1)S(1)}, u32[]{:S(2)}, u32[]{:S(2)}) collective-permute-start(bf16[4,2,144,128]{3,2,1,0:T(8,128)(2,1)S(1)} %get-tuple-element.25), channel_id=1, source_target_pairs={{0,2},{2,0},{4,6},{6,4},{8,10},{10,8},{12,14},{14,12},{16,18},{18,... | collective-permute-start | bytes 884744 | tf_op jit(solution)/shard_map/ppermute | solution.py:451
  58.4 30.6 %collective-permute-start.2 = (bf16[4,2,144,128]{3,2,1,0:T(8,128)(2,1)S(1)}, bf16[4,2,144,128]{3,2,1,0:T(8,128)(2,1)S(1)}, u32[]{:S(2)}, u32[]{:S(2)}) collective-permute-start(bf16[4,2,144,128]{3,2,1,0:T(8,128)(2,1)S(1)} %get-tuple-element.26), channel_id=1, source_target_pairs={{0,4},{2,6},{4,0},{6,2},{8,12},{10,14},{12,8},{14,10},{16,20},{18,... | collective-permute-start | bytes 884744 | tf_op jit(solution)/shard_map/ppermute | solution.py:451
  72.8 35.0 %collective-permute-start.5 = (bf16[8,2,144,128]{3,2,1,0:T(8,128)(2,1)S(1)}, bf16[8,2,144,128]{3,2,1,0:T(8,128)(2,1)S(1)}, u32[]{:S(2)}, u32[]{:S(2)}) collective-permute-start(bf16[8,2,144,128]{3,2,1,0:T(8,128)(2,1)S(1)} %pad_maximum_fusion.3), channel_id=1, source_target_pairs={{0,4},{2,6},{4,0},{6,2},{8,12},{10,14},{12,8},{14,10},{16,20},{18,... | collective-permute-start | bytes 1769480 | tf_op jit(solution)/shard_map/ppermute | solution.py:451
  89.0 31.8 %collective-permute-start.3 = (bf16[8,2,144,128]{3,2,1,0:T(8,128)(2,1)S(1)}, bf16[8,2,144,128]{3,2,1,0:T(8,128)(2,1)}, u32[]{:S(2)}, u32[]{:S(2)}) collective-permute-start(bf16[8,2,144,128]{3,2,1,0:T(8,128)(2,1)S(1)} %pad_maximum_fusion.2), channel_id=1, source_target_pairs={{0,2},{2,0},{4,6},{6,4},{8,10},{10,8},{12,14},{14,12},{16,18},{18,... | collective-permute-start | bytes 1769480 | tf_op jit(solution)/shard_map/ppermute | solution.py:451
  138.6 21.4 %all-to-all-start.4 = ((f32[16,24,128]{2,1,0:T(8,128)}), f32[16,24,128]{2,1,0:T(8,128)S(1)}, u32[]{:S(2)}, u32[]{:S(2)}) async-start(f32[16,24,128]{2,1,0:T(8,128)} %score_kept.1), calls=%async_computation.4 | async-start | bytes 393216 | tf_op jit(solution)/shard_map/all_to_all | solution.py:446
  172.4 2.2 %copy-start = (bf16[4096,512]{1,0:T(8,128)(2,1)S(1)}, bf16[4096,512]{1,0:T(8,128)(2,1)}, u32[]{:S(2)}) copy-start(bf16[4096,512]{1,0:T(8,128)(2,1)} %w.1) | copy-start | bytes 12582916

commit v4 on v3

--- a/solution.py
+++ b/solution.py
@@ -331,20 +331,19 @@
                 owner = jnp.bitwise_xor(me, r * 8 + j * 2 + o)
                 for half, stat in enumerate((stat_a, stat_b)):
                     tables.append(stat[reverse_bits(owner, orders[half])].reshape(2 * STAT, 128))
+            table = jnp.concatenate(tables, axis=0)
             for c in range(lists // 2):
                 first = r * lists + c * 2
                 keys = blocks[first : first + 2, :, j, 0:128].reshape(256, 128)
-                flipped = keys.astype(F32).T
+                turned_keys = keys.T
+                flipped = turned_keys.astype(F32)
                 logits = []
-                for table in tables:
-                    turned = lax.dot_general(table, keys, NT, preferred_element_type=F32)
-                    for g in range(2):
-                        base = g * STAT
-                        quadratic = jnp.sum(
-                            turned[base : base + 128] * flipped, axis=0, keepdims=True
-                        )
-                        linear = turned[base + 128 : base + 129] + turned[base + 129 : base + 130]
-                        logits.append(linear + quadratic / 256.0)
+                turned = jnp.dot(table, turned_keys, preferred_element_type=F32)
+                for g in range(8):
+                    base = g * STAT
+                    quadratic = jnp.sum(turned[base : base + 128] * flipped, axis=0, keepdims=True)
+                    linear = turned[base + 128 : base + 129] + turned[base + 129 : base + 130]
+                    logits.append(linear + quadratic / 256.0)
                 logit = jnp.concatenate(logits, axis=0)
                 top = jnp.max(logit, axis=0, keepdims=True)
                 mean = jnp.sum(jnp.exp(logit - top), axis=0, keepdims=True) / 8.0
@@ -417,14 +416,28 @@
     )(place, target, hbm(arrived))
 
 
-def finish_kernel(joined, w, out, rows):
+def finish_kernel(joined, w, out, rows, weight, sem):
+    quarter = w.shape[0] // 4
+
+    def fetch(i):
+        part = pl.ds(i * quarter, quarter)
+        return pltpu.make_async_copy(w.at[part], weight.at[part], sem.at[i])
+
+    for i in range(4):
+        fetch(i).start()
     for r in range(2):
         for h in range(32):
             at = (h % 4) * 4
             rows[r * 4 : r * 4 + 4, h * 128 : h * 128 + 128] = joined[
                 r * 8 + h // 4, at : at + 4, :
             ].astype(F32)
-    value = jnp.dot(rows[...].astype(BF), w[...], preferred_element_type=F32)
+    value = jnp.zeros((8, w.shape[1]), F32)
+    for i in range(4):
+        fetch(i).wait()
+        part = slice(i * quarter, i * quarter + quarter)
+        value = value + jnp.dot(
+            rows[:, part].astype(BF), weight[part, :], preferred_element_type=F32
+        )
     for r in range(2):
         for t in range(4):
             out[t, r : r + 1, :] = value[r * 4 + t : r * 4 + t + 1, :]
@@ -434,12 +447,16 @@
     return pl.pallas_call(
         finish_kernel,
         out_shape=jax.ShapeDtypeStruct((4, 2, w_out.shape[1]), F32),
-        in_specs=[VMEM, VMEM],
+        in_specs=[VMEM, ANY],
         out_specs=VMEM,
-        scratch_shapes=[pltpu.VMEM((8, w_out.shape[0]), F32)],
+        scratch_shapes=[
+            pltpu.VMEM((8, w_out.shape[0]), F32),
+            pltpu.VMEM(w_out.shape, w_out.dtype),
+            pltpu.SemaphoreType.DMA((4,)),
+        ],
         compiler_params=params(),
         name="project_out",
-    )(joined, w_out)
+    )(joined, hbm(w_out))
 
 
 def exchange(value):

time: 180 us -> 180 us (level)
  starting transfers between devices: 47.7 us -> 52.5 us
  Pallas kernels: 46.3 us -> 43.3 us
  local copies, waits for them, and re-layouts: 3.58 us -> 1.39 us
    all_to_all x5, starting transfers between devices: 36.2 us -> 41 us  [exchange(): return lax.all_to_all(value, 'ctx', split_axis=0, concat_axis=0, tiled=True)]
    pallas_call x1, Pallas kernels: 16.6 us -> 11.8 us  [score(): pl.pallas_call(kernel, out_shape=jax.ShapeDtypeStruct(parts.shape, parts....]
    unnamed x9 -> x7, local copies, waits for them, and re-layouts: 3.16 us -> 0.98 us
    pallas_call x1, Pallas kernels: 0.65 us -> 2.46 us  [finish(): pl.pallas_call(finish_kernel, out_shape=jax.ShapeDtypeStruct((4, 2, w_out...]
  transfers between devices with their start and end apart: 11 -> 11, of which waited for: 7 -> 7; matrix products, arithmetic and copies ran while one was open for 1% -> 1% of each run, Pallas kernels for 24% -> 21%
where the time goes in v4:
time: 180 us; the launch traced here: 179 us
  waiting for transfers between devices  64.7 us (36%)
  starting transfers between devices  52.5 us (29%)
  Pallas kernels  43.3 us (24%)
  blocking collectives  14.7 us (8%)
    ppermute x6, waiting for transfers between devices, doubled(): return jnp.concatenate([value, lax.ppermute(value, 'ctx', pairs)], axis=0)  48.4 us
    all_to_all x5, starting transfers between devices, exchange(): return lax.all_to_all(value, 'ctx', split_axis=0, concat_axis=0, tiled=True)  41 us
    all_to_all x5, waiting for transfers between devices, exchange(): return lax.all_to_all(value, 'ctx', split_axis=0, concat_axis=0, tiled=True)  16.3 us
    pallas_call x1, Pallas kernels, score(): pl.pallas_call(kernel, out_shape=jax.ShapeDtypeStruct(parts.shape, parts....  11.8 us
    ppermute x6, starting transfers between devices, doubled(): return jnp.concatenate([value, lax.ppermute(value, 'ctx', pairs)], axis=0)  11.5 us
    all_to_all x1, blocking collectives, exchange(): return lax.all_to_all(value, 'ctx', split_axis=0, concat_axis=0, tiled=True)  10.7 us
    pallas_call x1, Pallas kernels, pack(): pl.pallas_call(pack_kernel, out_shape=pltpu.HBM((items, width, *tail), kv...  9.62 us
    pallas_call x1, Pallas kernels, attend(): pl.pallas_call(attend_kernel, out_shape=jax.ShapeDtypeStruct((16, 24, 128...  6.41 us
  transfers between devices with their start and end apart: 11, of which 7 were waited for; matrix products, arithmetic and copies ran while one was open for 1% of the time, Pallas kernels for 21%

profile of v4, /device:TPU:0, one launch (start us, length us, event | category | flops | bytes accessed | tf_op | source)
XLA Modules:
  0.0 178.8 jit_solution(6569979557251212359)
XLA Ops:
  0.6 0.0 copy-start
  0.6 0.9 copy-done
  1.6 0.7 split_samples.1
  2.3 8.3 %all-to-all-start = ((bf16[16,64,128]{2,1,0:T(8,128)(2,1)}), bf16[16,64,128]{2,1,0:T(8,128)(2,1)S(1)}, u32[]{:S(2)}, u32[]{:S(2)}) async-start(bf16[16,64,128]{2,1,0:T(8,128)(2,1)} %split_samples.1), calls=%async_computation | async-start | bytes 524288 | tf_op jit(solution)/shard_map/all_to_all | solution.py:463
  10.6 0.0 copy-start.2
  10.7 0.0 copy-start.1
  10.7 4.8 %project_tokens.1 = f32[16,24,128]{2,1,0:T(8,128)} custom-call(bf16[4,2,512]{2,1,0:T(2,128)(2,1)} %tokens.1, bf16[512,4096]{1,0:T(8,128)(2,1)} %wq.1, bf16[512,4,256]{2,1,0:T(4,128)(2,1)} %wkv.1), custom_call_target="tpu_custom_call" | custom-call | tf_op jit(solution)/shard_map/project_tokens/pallas_call | solution.py:141
  15.5 5.0 %all-to-all-done.parts = bf16[16,64,128]{2,1,0:T(8,128)(2,1)S(1)} async-done(((bf16[16,64,128]{2,1,0:T(8,128)(2,1)}), bf16[16,64,128]{2,1,0:T(8,128)(2,1)S(1)}, u32[]{:S(2)}, u32[]{:S(2)}) %all-to-all-start) | async-done | bytes 262176 | tf_op jit(solution)/shard_map/all_to_all | solution.py:463
  20.5 0.5 head_moments.1
  21.0 0.7 collective-permute-start
  21.8 4.3 %all-to-all-start.1 = ((f32[16,24,128]{2,1,0:T(8,128)}), f32[16,24,128]{2,1,0:T(8,128)S(1)}, u32[]{:S(2)}, u32[]{:S(2)}) async-start(f32[16,24,128]{2,1,0:T(8,128)} %project_tokens.1), calls=%async_computation.1 | async-start | bytes 393216 | tf_op jit(solution)/shard_map/all_to_all | solution.py:463
  26.1 0.0 copy-done.2
  26.1 0.1 copy.25
  26.2 0.0 copy-done.1
  26.2 9.6 %pack_rows.1.send.refs_4_ = bf16[16,128,4,256]{3,2,1,0:T(4,128)(2,1)} custom-call(s32[16,128]{1,0:T(8,128)S(1)} %bitcast.10, s32[16,2]{1,0:T(8,128)S(1)} %bitcast.5, bf16[2,2048,4,256]{3,2,1,0:T(4,128)(2,1)} %kv.1), custom_call_target="tpu_custom_call" | custom-call | tf_op jit(solution)/shard_map/pack_rows/pallas_call | solution.py:72
  35.8 0.0 collective-permute-done
  35.9 2.0 %collective-permute-start.1 = (bf16[2,4,144,128]{3,2,1,0:T(8,128)(2,1)S(1)}, bf16[2,4,144,128]{3,2,1,0:T(8,128)(2,1)S(1)}, u32[]{:S(2)}, u32[]{:S(2)}) collective-permute-start(bf16[2,4,144,128]{3,2,1,0:T(8,128)(2,1)S(1)} %pad_maximum_fusion.4), channel_id=1, source_target_pairs={{0,8},{2,10},{4,12},{6,14},{8,0},{10,2},{12,4},{14,6},{16,24},{18,... | collective-permute-start | bytes 884744 | tf_op jit(solution)/shard_map/ppermute | solution.py:468
  37.9 0.0 all-to-all-done.1.parts
  37.9 0.8 normalize_tokens.1
  38.7 5.5 %all-to-all-start.2 = ((bf16[16,32,128]{2,1,0:T(8,128)(2,1)}), bf16[16,32,128]{2,1,0:T(8,128)(2,1)S(1)}, u32[]{:S(2)}, u32[]{:S(2)}) async-start(bf16[16,32,128]{2,1,0:T(8,128)(2,1)} %normalize_tokens.1), calls=%async_computation.2 | async-start | bytes 262144 | tf_op jit(solution)/shard_map/all_to_all | solution.py:463
  44.3 0.0 collective-permute-done.1
  44.3 7.7 %all-to-all-done.2.query = bf16[16,32,128]{2,1,0:T(8,128)(2,1)S(1)} async-done(((bf16[16,32,128]{2,1,0:T(8,128)(2,1)}), bf16[16,32,128]{2,1,0:T(8,128)(2,1)S(1)}, u32[]{:S(2)}, u32[]{:S(2)}) %all-to-all-start.2) | async-done | bytes 131104 | tf_op jit(solution)/shard_map/all_to_all | solution.py:463
  52.0 4.7 %all-to-all-start.3 = ((bf16[16,128,4,256]{3,2,1,0:T(4,128)(2,1)}), bf16[16,128,4,256]{3,2,1,0:T(4,128)(2,1)}, u32[]{:S(2)}, u32[]{:S(2)}) async-start(bf16[16,128,4,256]{3,2,1,0:T(4,128)(2,1)} %pack_rows.1.send.refs_4_), calls=%async_computation.3 | async-start | bytes 8388608 | tf_op jit(solution)/shard_map/all_to_all | solution.py:463
  56.8 1.6 collective-permute-start.4
  58.4 1.5 collective-permute-start.2
  59.9 12.9 %collective-permute-done.4 = bf16[4,2,144,128]{3,2,1,0:T(8,128)(2,1)S(1)} collective-permute-done((bf16[4,2,144,128]{3,2,1,0:T(8,128)(2,1)S(1)}, bf16[4,2,144,128]{3,2,1,0:T(8,128)(2,1)S(1)}, u32[]{:S(2)}, u32[]{:S(2)}) %collective-permute-start.4) | collective-permute-done | bytes 294944 | tf_op jit(solution)/shard_map/ppermute | solution.py:468
  72.8 0.1 pad_maximum_fusion.3
  72.9 3.6 %collective-permute-start.5 = (bf16[8,2,144,128]{3,2,1,0:T(8,128)(2,1)S(1)}, bf16[8,2,144,128]{3,2,1,0:T(8,128)(2,1)S(1)}, u32[]{:S(2)}, u32[]{:S(2)}) collective-permute-start(bf16[8,2,144,128]{3,2,1,0:T(8,128)(2,1)S(1)} %pad_maximum_fusion.3), channel_id=1, source_target_pairs={{0,4},{2,6},{4,0},{6,2},{8,12},{10,14},{12,8},{14,10},{16,20},{18,... | collective-permute-start | bytes 1769480 | tf_op jit(solution)/shard_map/ppermute | solution.py:468
  76.5 12.6 %collective-permute-done.2 = bf16[4,2,144,128]{3,2,1,0:T(8,128)(2,1)S(1)} collective-permute-done((bf16[4,2,144,128]{3,2,1,0:T(8,128)(2,1)S(1)}, bf16[4,2,144,128]{3,2,1,0:T(8,128)(2,1)S(1)}, u32[]{:S(2)}, u32[]{:S(2)}) %collective-permute-start.2) | collective-permute-done | bytes 294944 | tf_op jit(solution)/shard_map/ppermute | solution.py:468
  89.0 0.1 pad_maximum_fusion.2
  89.1 2.1 %collective-permute-start.3 = (bf16[8,2,144,128]{3,2,1,0:T(8,128)(2,1)S(1)}, bf16[8,2,144,128]{3,2,1,0:T(8,128)(2,1)}, u32[]{:S(2)}, u32[]{:S(2)}) collective-permute-start(bf16[8,2,144,128]{3,2,1,0:T(8,128)(2,1)S(1)} %pad_maximum_fusion.2), channel_id=1, source_target_pairs={{0,2},{2,0},{4,6},{6,4},{8,10},{10,8},{12,14},{14,12},{16,18},{18,... | collective-permute-start | bytes 1769480 | tf_op jit(solution)/shard_map/ppermute | solution.py:468
  91.2 0.1 copy.20
  91.3 0.1 copy.22.bias
  91.4 6.4 %attend_kept.1.refs_5_ = f32[16,24,128]{2,1,0:T(8,128)S(1)} custom-call(s32[16,2]{1,0:T(8,128)S(1)} %bitcast.6, bf16[16,32,128]{2,1,0:T(8,128)(2,1)S(1)} %all-to-all-done.2.query, f32[16,512]{1,0:T(8,128)S(1)} %copy.22.bias, bf16[16,128,4,256]{3,2,1,0:T(4,128)(2,1)} %pack_rows.1.send.refs_4_), custom_call_target="tpu_custom_call" | custom-call | tf_op jit(solution)/shard_map/attend_kept/pallas_call | solution.py:245
  97.8 10.0 %collective-permute-done.5 = bf16[8,2,144,128]{3,2,1,0:T(8,128)(2,1)S(1)} collective-permute-done((bf16[8,2,144,128]{3,2,1,0:T(8,128)(2,1)S(1)}, bf16[8,2,144,128]{3,2,1,0:T(8,128)(2,1)S(1)}, u32[]{:S(2)}, u32[]{:S(2)}) %collective-permute-start.5) | collective-permute-done | bytes 589856 | tf_op jit(solution)/shard_map/ppermute | solution.py:468
  107.9 0.1 pad_maximum_fusion.1.refs_3_
  108.0 12.9 %collective-permute-done.3 = bf16[8,2,144,128]{3,2,1,0:T(8,128)(2,1)} collective-permute-done((bf16[8,2,144,128]{3,2,1,0:T(8,128)(2,1)S(1)}, bf16[8,2,144,128]{3,2,1,0:T(8,128)(2,1)}, u32[]{:S(2)}, u32[]{:S(2)}) %collective-permute-start.3) | collective-permute-done | bytes 589856 | tf_op jit(solution)/shard_map/ppermute | solution.py:468
  120.9 1.2 pad_maximum_fusion.refs_2_
  122.1 11.8 %score_kept.1 = f32[16,24,128]{2,1,0:T(8,128)} custom-call(s32[1]{0:T(128)} %bitcast.place.refs_0_, s32[16,2]{1,0:T(8,128)S(1)} %bitcast.7, bf16[16,2,144,128]{3,2,1,0:T(8,128)(2,1)S(1)} %pad_maximum_fusion.refs_2_, bf16[16,2,144,128]{3,2,1,0:T(8,128)(2,1)S(1)} %pad_maximum_fusion.1.refs_3_, bf16[16,128,4,256]{3,2,1,0:T(4,128)(2,1)} %pack_rows.1.send.refs_4_, ...), custom_call_target="tpu_custom_call" | custom-call | tf_op jit(solution)/shard_map/score_kept/pallas_call | solution.py:362
  133.9 0.0 all-to-all-done.3.arrived
  133.9 18.1 %all-to-all-start.4 = ((f32[16,24,128]{2,1,0:T(8,128)}), f32[16,24,128]{2,1,0:T(8,128)S(1)}, u32[]{:S(2)}, u32[]{:S(2)}) async-start(f32[16,24,128]{2,1,0:T(8,128)} %score_kept.1), calls=%async_computation.4 | async-start | bytes 393216 | tf_op jit(solution)/shard_map/all_to_all | solution.py:463
  152.0 4.5 %place_blocks.1 = bf16[16,128,4,256]{3,2,1,0:T(4,128)(2,1)} custom-call(s32[1]{0:T(128)} %bitcast.place.refs_0_, s32[16,2]{1,0:T(8,128)S(1)} %bitcast.8, bf16[16,128,4,256]{3,2,1,0:T(4,128)(2,1)} %all-to-all-done.3.arrived), custom_call_target="tpu_custom_call" | custom-call | tf_op jit(solution)/shard_map/place_blocks/pallas_call | solution.py:404
  156.5 3.5 %all-to-all-done.4.parts = f32[16,24,128]{2,1,0:T(8,128)S(1)} async-done(((f32[16,24,128]{2,1,0:T(8,128)}), f32[16,24,128]{2,1,0:T(8,128)S(1)}, u32[]{:S(2)}, u32[]{:S(2)}) %all-to-all-start.4) | async-done | bytes 196640 | tf_op jit(solution)/shard_map/all_to_all | solution.py:463
  160.0 1.6 combine_parts.1
  161.7 10.7 %all_to_all.30.joined = bf16[16,16,128]{2,1,0:T(8,128)(2,1)S(1)} all-to-all(bf16[16,16,128]{2,1,0:T(8,128)(2,1)S(1)} %get-tuple-element.24), channel_id=1, replica_groups=mesh['ctx'=16,'head'=2] {'ctx'}, dimensions={0} | all-to-all | bytes 131072 | tf_op jit(solution)/shard_map/all_to_all | solution.py:463
  172.4 2.5 %project_out.1 = f32[4,2,512]{2,1,0:T(2,128)S(1)} custom-call(bf16[16,16,128]{2,1,0:T(8,128)(2,1)S(1)} %all_to_all.30.joined, bf16[4096,512]{1,0:T(8,128)(2,1)} %w.1), custom_call_target="tpu_custom_call" | custom-call | tf_op jit(solution)/shard_map/project_out/pallas_call | solution.py:447
  174.9 4.0 %psum.7 = bf16[4,2,512]{2,1,0:T(2,128)(2,1)} all-reduce(f32[4,2,512]{2,1,0:T(2,128)S(1)} %project_out.1), channel_id=1, replica_groups=mesh['ctx'=16,'head'=2] {'head'}, use_global_device_ids=true, to_apply=%region_0.1 | all-reduce | flops 4096 | bytes 24576 | tf_op jit(solution)/shard_map/psum | solution.py:505
  (6 shorter events, 0.2 us)
Async XLA Ops:
  0.6 1.0 copy-start
  2.3 18.2 %all-to-all-start = ((bf16[16,64,128]{2,1,0:T(8,128)(2,1)}), bf16[16,64,128]{2,1,0:T(8,128)(2,1)S(1)}, u32[]{:S(2)}, u32[]{:S(2)}) async-start(bf16[16,64,128]{2,1,0:T(8,128)(2,1)} %split_samples.1), calls=%async_computation | async-start | bytes 524288 | tf_op jit(solution)/shard_map/all_to_all | solution.py:463
  10.6 15.5 %copy-start.2 = (s32[2,8,2]{1,2,0:T(2,128)S(1)}, s32[2,8,2]{1,2,0:T(2,128)}, u32[]{:S(2)}) copy-start(s32[2,8,2]{1,2,0:T(2,128)} %param.10) | copy-start | bytes 388
  10.7 15.6 %copy-start.1 = (s32[2,8,128]{2,1,0:T(8,128)S(1)}, s32[2,8,128]{2,1,0:T(8,128)}, u32[]{:S(2)}) copy-start(s32[2,8,128]{2,1,0:T(8,128)} %param.9) | copy-start | bytes 24580
  21.0 14.8 %collective-permute-start = (bf16[1,4,144,128]{3,2,1,0:T(8,128)(2,1)S(1)}, bf16[1,4,144,128]{3,2,1,0:T(8,128)(2,1)S(1)}, u32[]{:S(2)}, u32[]{:S(2)}) collective-permute-start(bf16[1,4,144,128]{3,2,1,0:T(8,128)(2,1)S(1)} %head_moments.1), channel_id=1, source_target_pairs={{0,16},{2,18},{4,20},{6,22},{8,24},{10,26},{12,28},{14,30},{16,0},... | collective-permute-start | bytes 442376 | tf_op jit(solution)/shard_map/ppermute | solution.py:468
  21.8 16.1 %all-to-all-start.1 = ((f32[16,24,128]{2,1,0:T(8,128)}), f32[16,24,128]{2,1,0:T(8,128)S(1)}, u32[]{:S(2)}, u32[]{:S(2)}) async-start(f32[16,24,128]{2,1,0:T(8,128)} %project_tokens.1), calls=%async_computation.1 | async-start | bytes 393216 | tf_op jit(solution)/shard_map/all_to_all | solution.py:463
  35.9 8.4 %collective-permute-start.1 = (bf16[2,4,144,128]{3,2,1,0:T(8,128)(2,1)S(1)}, bf16[2,4,144,128]{3,2,1,0:T(8,128)(2,1)S(1)}, u32[]{:S(2)}, u32[]{:S(2)}) collective-permute-start(bf16[2,4,144,128]{3,2,1,0:T(8,128)(2,1)S(1)} %pad_maximum_fusion.4), channel_id=1, source_target_pairs={{0,8},{2,10},{4,12},{6,14},{8,0},{10,2},{12,4},{14,6},{16,24},{18,... | collective-permute-start | bytes 884744 | tf_op jit(solution)/shard_map/ppermute | solution.py:468
  38.7 13.3 %all-to-all-start.2 = ((bf16[16,32,128]{2,1,0:T(8,128)(2,1)}), bf16[16,32,128]{2,1,0:T(8,128)(2,1)S(1)}, u32[]{:S(2)}, u32[]{:S(2)}) async-start(bf16[16,32,128]{2,1,0:T(8,128)(2,1)} %normalize_tokens.1), calls=%async_computation.2 | async-start | bytes 262144 | tf_op jit(solution)/shard_map/all_to_all | solution.py:463
  52.0 81.9 %all-to-all-start.3 = ((bf16[16,128,4,256]{3,2,1,0:T(4,128)(2,1)}), bf16[16,128,4,256]{3,2,1,0:T(4,128)(2,1)}, u32[]{:S(2)}, u32[]{:S(2)}) async-start(bf16[16,128,4,256]{3,2,1,0:T(4,128)(2,1)} %pack_rows.1.send.refs_4_), calls=%async_computation.3 | async-start | bytes 8388608 | tf_op jit(solution)/shard_map/all_to_all | solution.py:463
  56.8 16.0 %collective-permute-start.4 = (bf16[4,2,144,128]{3,2,1,0:T(8,128)(2,1)S(1)}, bf16[4,2,144,128]{3,2,1,0:T(8,128)(2,1)S(1)}, u32[]{:S(2)}, u32[]{:S(2)}) collective-permute-start(bf16[4,2,144,128]{3,2,1,0:T(8,128)(2,1)S(1)} %get-tuple-element.25), channel_id=1, source_target_pairs={{0,2},{2,0},{4,6},{6,4},{8,10},{10,8},{12,14},{14,12},{16,18},{18,... | collective-permute-start | bytes 884744 | tf_op jit(solution)/shard_map/ppermute | solution.py:468
  58.4 30.6 %collective-permute-start.2 = (bf16[4,2,144,128]{3,2,1,0:T(8,128)(2,1)S(1)}, bf16[4,2,144,128]{3,2,1,0:T(8,128)(2,1)S(1)}, u32[]{:S(2)}, u32[]{:S(2)}) collective-permute-start(bf16[4,2,144,128]{3,2,1,0:T(8,128)(2,1)S(1)} %get-tuple-element.26), channel_id=1, source_target_pairs={{0,4},{2,6},{4,0},{6,2},{8,12},{10,14},{12,8},{14,10},{16,20},{18,... | collective-permute-start | bytes 884744 | tf_op jit(solution)/shard_map/ppermute | solution.py:468
  72.9 35.0 %collective-permute-start.5 = (bf16[8,2,144,128]{3,2,1,0:T(8,128)(2,1)S(1)}, bf16[8,2,144,128]{3,2,1,0:T(8,128)(2,1)S(1)}, u32[]{:S(2)}, u32[]{:S(2)}) collective-permute-start(bf16[8,2,144,128]{3,2,1,0:T(8,128)(2,1)S(1)} %pad_maximum_fusion.3), channel_id=1, source_target_pairs={{0,4},{2,6},{4,0},{6,2},{8,12},{10,14},{12,8},{14,10},{16,20},{18,... | collective-permute-start | bytes 1769480 | tf_op jit(solution)/shard_map/ppermute | solution.py:468
  89.1 31.8 %collective-permute-start.3 = (bf16[8,2,144,128]{3,2,1,0:T(8,128)(2,1)S(1)}, bf16[8,2,144,128]{3,2,1,0:T(8,128)(2,1)}, u32[]{:S(2)}, u32[]{:S(2)}) collective-permute-start(bf16[8,2,144,128]{3,2,1,0:T(8,128)(2,1)S(1)} %pad_maximum_fusion.2), channel_id=1, source_target_pairs={{0,2},{2,0},{4,6},{6,4},{8,10},{10,8},{12,14},{14,12},{16,18},{18,... | collective-permute-start | bytes 1769480 | tf_op jit(solution)/shard_map/ppermute | solution.py:468
  133.9 26.1 %all-to-all-start.4 = ((f32[16,24,128]{2,1,0:T(8,128)}), f32[16,24,128]{2,1,0:T(8,128)S(1)}, u32[]{:S(2)}, u32[]{:S(2)}) async-start(f32[16,24,128]{2,1,0:T(8,128)} %score_kept.1), calls=%async_computation.4 | async-start | bytes 393216 | tf_op jit(solution)/shard_map/all_to_all | solution.py:463

commit v5 on v4

--- a/solution.py
+++ b/solution.py
@@ -48,7 +48,7 @@
         fetch(m).start()
         spans[m, span] = jnp.zeros(spans.shape[2:], spans.dtype)
 
-    def one(m, carry):
+    for m in range(items):
         fetch(m).wait()
 
         def rows(j, inner):
@@ -59,9 +59,6 @@
 
         lax.fori_loop(0, width // 16, rows, 0)
         put(m).start()
-        return carry
-
-    lax.fori_loop(0, items, one, 0)
     for m in range(items):
         put(m).wait()
 

time: 180 us -> 178 us (0.989)
  no operation moved by 1% of the time
where the time goes in v5:
time: 178 us; the launch traced here: 177 us
  waiting for transfers between devices  64.7 us (36%)
  starting transfers between devices  52.5 us (29%)
  Pallas kernels  41.9 us (24%)
  blocking collectives  14.7 us (8%)
    ppermute x6, waiting for transfers between devices, doubled(): return jnp.concatenate([value, lax.ppermute(value, 'ctx', pairs)], axis=0)  48.4 us
    all_to_all x5, starting transfers between devices, exchange(): return lax.all_to_all(value, 'ctx', split_axis=0, concat_axis=0, tiled=True)  41 us
    all_to_all x5, waiting for transfers between devices, exchange(): return lax.all_to_all(value, 'ctx', split_axis=0, concat_axis=0, tiled=True)  16.3 us
    pallas_call x1, Pallas kernels, score(): pl.pallas_call(kernel, out_shape=jax.ShapeDtypeStruct(parts.shape, parts....  11.8 us
    ppermute x6, starting transfers between devices, doubled(): return jnp.concatenate([value, lax.ppermute(value, 'ctx', pairs)], axis=0)  11.5 us
    all_to_all x1, blocking collectives, exchange(): return lax.all_to_all(value, 'ctx', split_axis=0, concat_axis=0, tiled=True)  10.7 us
    pallas_call x1, Pallas kernels, pack(): pl.pallas_call(pack_kernel, out_shape=pltpu.HBM((items, width, *tail), kv...  8.19 us
    pallas_call x1, Pallas kernels, attend(): pl.pallas_call(attend_kernel, out_shape=jax.ShapeDtypeStruct((16, 24, 128...  6.41 us
  transfers between devices with their start and end apart: 11, of which 7 were waited for; matrix products, arithmetic and copies ran while one was open for 1% of the time, Pallas kernels for 21%

profile of v5, /device:TPU:0, one launch (start us, length us, event | category | flops | bytes accessed | tf_op | source)
XLA Modules:
  0.0 177.4 jit_solution(267208415670108869)
XLA Ops:
  0.6 0.0 copy-start
  0.6 0.9 copy-done
  1.6 0.7 split_samples.1
  2.3 8.3 %all-to-all-start = ((bf16[16,64,128]{2,1,0:T(8,128)(2,1)}), bf16[16,64,128]{2,1,0:T(8,128)(2,1)S(1)}, u32[]{:S(2)}, u32[]{:S(2)}) async-start(bf16[16,64,128]{2,1,0:T(8,128)(2,1)} %split_samples.1), calls=%async_computation | async-start | bytes 524288 | tf_op jit(solution)/shard_map/all_to_all | solution.py:460
  10.6 0.0 copy-start.2
  10.7 0.0 copy-start.1
  10.7 4.8 %project_tokens.1 = f32[16,24,128]{2,1,0:T(8,128)} custom-call(bf16[4,2,512]{2,1,0:T(2,128)(2,1)} %tokens.1, bf16[512,4096]{1,0:T(8,128)(2,1)} %wq.1, bf16[512,4,256]{2,1,0:T(4,128)(2,1)} %wkv.1), custom_call_target="tpu_custom_call" | custom-call | tf_op jit(solution)/shard_map/project_tokens/pallas_call | solution.py:138
  15.5 5.0 %all-to-all-done.parts = bf16[16,64,128]{2,1,0:T(8,128)(2,1)S(1)} async-done(((bf16[16,64,128]{2,1,0:T(8,128)(2,1)}), bf16[16,64,128]{2,1,0:T(8,128)(2,1)S(1)}, u32[]{:S(2)}, u32[]{:S(2)}) %all-to-all-start) | async-done | bytes 262176 | tf_op jit(solution)/shard_map/all_to_all | solution.py:460
  20.5 0.5 head_moments.1
  21.0 0.7 collective-permute-start
  21.8 4.3 %all-to-all-start.1 = ((f32[16,24,128]{2,1,0:T(8,128)}), f32[16,24,128]{2,1,0:T(8,128)S(1)}, u32[]{:S(2)}, u32[]{:S(2)}) async-start(f32[16,24,128]{2,1,0:T(8,128)} %project_tokens.1), calls=%async_computation.1 | async-start | bytes 393216 | tf_op jit(solution)/shard_map/all_to_all | solution.py:460
  26.1 0.0 copy-done.2
  26.1 0.1 copy.25
  26.2 0.0 copy-done.1
  26.2 8.2 %pack_rows.1.send.refs_4_ = bf16[16,128,4,256]{3,2,1,0:T(4,128)(2,1)} custom-call(s32[16,128]{1,0:T(8,128)S(1)} %bitcast.10, s32[16,2]{1,0:T(8,128)S(1)} %bitcast.5, bf16[2,2048,4,256]{3,2,1,0:T(4,128)(2,1)} %kv.1), custom_call_target="tpu_custom_call" | custom-call | tf_op jit(solution)/shard_map/pack_rows/pallas_call | solution.py:69
  34.4 0.0 collective-permute-done
  34.5 2.0 %collective-permute-start.1 = (bf16[2,4,144,128]{3,2,1,0:T(8,128)(2,1)S(1)}, bf16[2,4,144,128]{3,2,1,0:T(8,128)(2,1)S(1)}, u32[]{:S(2)}, u32[]{:S(2)}) collective-permute-start(bf16[2,4,144,128]{3,2,1,0:T(8,128)(2,1)S(1)} %pad_maximum_fusion.4), channel_id=1, source_target_pairs={{0,8},{2,10},{4,12},{6,14},{8,0},{10,2},{12,4},{14,6},{16,24},{18,... | collective-permute-start | bytes 884744 | tf_op jit(solution)/shard_map/ppermute | solution.py:465
  36.5 0.0 all-to-all-done.1.parts
  36.5 0.8 normalize_tokens.1
  37.2 5.5 %all-to-all-start.2 = ((bf16[16,32,128]{2,1,0:T(8,128)(2,1)}), bf16[16,32,128]{2,1,0:T(8,128)(2,1)S(1)}, u32[]{:S(2)}, u32[]{:S(2)}) async-start(bf16[16,32,128]{2,1,0:T(8,128)(2,1)} %normalize_tokens.1), calls=%async_computation.2 | async-start | bytes 262144 | tf_op jit(solution)/shard_map/all_to_all | solution.py:460
  42.8 0.0 collective-permute-done.1
  42.9 7.7 %all-to-all-done.2.query = bf16[16,32,128]{2,1,0:T(8,128)(2,1)S(1)} async-done(((bf16[16,32,128]{2,1,0:T(8,128)(2,1)}), bf16[16,32,128]{2,1,0:T(8,128)(2,1)S(1)}, u32[]{:S(2)}, u32[]{:S(2)}) %all-to-all-start.2) | async-done | bytes 131104 | tf_op jit(solution)/shard_map/all_to_all | solution.py:460
  50.6 4.7 %all-to-all-start.3 = ((bf16[16,128,4,256]{3,2,1,0:T(4,128)(2,1)}), bf16[16,128,4,256]{3,2,1,0:T(4,128)(2,1)}, u32[]{:S(2)}, u32[]{:S(2)}) async-start(bf16[16,128,4,256]{3,2,1,0:T(4,128)(2,1)} %pack_rows.1.send.refs_4_), calls=%async_computation.3 | async-start | bytes 8388608 | tf_op jit(solution)/shard_map/all_to_all | solution.py:460
  55.4 1.6 collective-permute-start.4
  57.0 1.5 collective-permute-start.2
  58.5 12.9 %collective-permute-done.4 = bf16[4,2,144,128]{3,2,1,0:T(8,128)(2,1)S(1)} collective-permute-done((bf16[4,2,144,128]{3,2,1,0:T(8,128)(2,1)S(1)}, bf16[4,2,144,128]{3,2,1,0:T(8,128)(2,1)S(1)}, u32[]{:S(2)}, u32[]{:S(2)}) %collective-permute-start.4) | collective-permute-done | bytes 294944 | tf_op jit(solution)/shard_map/ppermute | solution.py:465
  71.4 0.1 pad_maximum_fusion.3
  71.4 3.6 %collective-permute-start.5 = (bf16[8,2,144,128]{3,2,1,0:T(8,128)(2,1)S(1)}, bf16[8,2,144,128]{3,2,1,0:T(8,128)(2,1)S(1)}, u32[]{:S(2)}, u32[]{:S(2)}) collective-permute-start(bf16[8,2,144,128]{3,2,1,0:T(8,128)(2,1)S(1)} %pad_maximum_fusion.3), channel_id=1, source_target_pairs={{0,4},{2,6},{4,0},{6,2},{8,12},{10,14},{12,8},{14,10},{16,20},{18,... | collective-permute-start | bytes 1769480 | tf_op jit(solution)/shard_map/ppermute | solution.py:465
  75.0 12.6 %collective-permute-done.2 = bf16[4,2,144,128]{3,2,1,0:T(8,128)(2,1)S(1)} collective-permute-done((bf16[4,2,144,128]{3,2,1,0:T(8,128)(2,1)S(1)}, bf16[4,2,144,128]{3,2,1,0:T(8,128)(2,1)S(1)}, u32[]{:S(2)}, u32[]{:S(2)}) %collective-permute-start.2) | collective-permute-done | bytes 294944 | tf_op jit(solution)/shard_map/ppermute | solution.py:465
  87.6 0.1 pad_maximum_fusion.2
  87.6 2.1 %collective-permute-start.3 = (bf16[8,2,144,128]{3,2,1,0:T(8,128)(2,1)S(1)}, bf16[8,2,144,128]{3,2,1,0:T(8,128)(2,1)}, u32[]{:S(2)}, u32[]{:S(2)}) collective-permute-start(bf16[8,2,144,128]{3,2,1,0:T(8,128)(2,1)S(1)} %pad_maximum_fusion.2), channel_id=1, source_target_pairs={{0,2},{2,0},{4,6},{6,4},{8,10},{10,8},{12,14},{14,12},{16,18},{18,... | collective-permute-start | bytes 1769480 | tf_op jit(solution)/shard_map/ppermute | solution.py:465
  89.7 0.1 copy.20
  89.9 0.1 copy.22.bias
  90.0 6.4 %attend_kept.1.refs_5_ = f32[16,24,128]{2,1,0:T(8,128)S(1)} custom-call(s32[16,2]{1,0:T(8,128)S(1)} %bitcast.6, bf16[16,32,128]{2,1,0:T(8,128)(2,1)S(1)} %all-to-all-done.2.query, f32[16,512]{1,0:T(8,128)S(1)} %copy.22.bias, bf16[16,128,4,256]{3,2,1,0:T(4,128)(2,1)} %pack_rows.1.send.refs_4_), custom_call_target="tpu_custom_call" | custom-call | tf_op jit(solution)/shard_map/attend_kept/pallas_call | solution.py:242
  96.4 10.0 %collective-permute-done.5 = bf16[8,2,144,128]{3,2,1,0:T(8,128)(2,1)S(1)} collective-permute-done((bf16[8,2,144,128]{3,2,1,0:T(8,128)(2,1)S(1)}, bf16[8,2,144,128]{3,2,1,0:T(8,128)(2,1)S(1)}, u32[]{:S(2)}, u32[]{:S(2)}) %collective-permute-start.5) | collective-permute-done | bytes 589856 | tf_op jit(solution)/shard_map/ppermute | solution.py:465
  106.5 0.1 pad_maximum_fusion.1.refs_3_
  106.6 12.9 %collective-permute-done.3 = bf16[8,2,144,128]{3,2,1,0:T(8,128)(2,1)} collective-permute-done((bf16[8,2,144,128]{3,2,1,0:T(8,128)(2,1)S(1)}, bf16[8,2,144,128]{3,2,1,0:T(8,128)(2,1)}, u32[]{:S(2)}, u32[]{:S(2)}) %collective-permute-start.3) | collective-permute-done | bytes 589856 | tf_op jit(solution)/shard_map/ppermute | solution.py:465
  119.5 1.2 pad_maximum_fusion.refs_2_
  120.7 11.8 %score_kept.1 = f32[16,24,128]{2,1,0:T(8,128)} custom-call(s32[1]{0:T(128)} %bitcast.place.refs_0_, s32[16,2]{1,0:T(8,128)S(1)} %bitcast.7, bf16[16,2,144,128]{3,2,1,0:T(8,128)(2,1)S(1)} %pad_maximum_fusion.refs_2_, bf16[16,2,144,128]{3,2,1,0:T(8,128)(2,1)S(1)} %pad_maximum_fusion.1.refs_3_, bf16[16,128,4,256]{3,2,1,0:T(4,128)(2,1)} %pack_rows.1.send.refs_4_, ...), custom_call_target="tpu_custom_call" | custom-call | tf_op jit(solution)/shard_map/score_kept/pallas_call | solution.py:359
  132.5 0.0 all-to-all-done.3.arrived
  132.5 18.1 %all-to-all-start.4 = ((f32[16,24,128]{2,1,0:T(8,128)}), f32[16,24,128]{2,1,0:T(8,128)S(1)}, u32[]{:S(2)}, u32[]{:S(2)}) async-start(f32[16,24,128]{2,1,0:T(8,128)} %score_kept.1), calls=%async_computation.4 | async-start | bytes 393216 | tf_op jit(solution)/shard_map/all_to_all | solution.py:460
  150.5 4.5 %place_blocks.1 = bf16[16,128,4,256]{3,2,1,0:T(4,128)(2,1)} custom-call(s32[1]{0:T(128)} %bitcast.place.refs_0_, s32[16,2]{1,0:T(8,128)S(1)} %bitcast.8, bf16[16,128,4,256]{3,2,1,0:T(4,128)(2,1)} %all-to-all-done.3.arrived), custom_call_target="tpu_custom_call" | custom-call | tf_op jit(solution)/shard_map/place_blocks/pallas_call | solution.py:401
  155.1 3.5 %all-to-all-done.4.parts = f32[16,24,128]{2,1,0:T(8,128)S(1)} async-done(((f32[16,24,128]{2,1,0:T(8,128)}), f32[16,24,128]{2,1,0:T(8,128)S(1)}, u32[]{:S(2)}, u32[]{:S(2)}) %all-to-all-start.4) | async-done | bytes 196640 | tf_op jit(solution)/shard_map/all_to_all | solution.py:460
  158.6 1.6 combine_parts.1
  160.3 10.7 %all_to_all.30.joined = bf16[16,16,128]{2,1,0:T(8,128)(2,1)S(1)} all-to-all(bf16[16,16,128]{2,1,0:T(8,128)(2,1)S(1)} %get-tuple-element.24), channel_id=1, replica_groups=mesh['ctx'=16,'head'=2] {'ctx'}, dimensions={0} | all-to-all | bytes 131072 | tf_op jit(solution)/shard_map/all_to_all | solution.py:460
  171.0 2.5 %project_out.1 = f32[4,2,512]{2,1,0:T(2,128)S(1)} custom-call(bf16[16,16,128]{2,1,0:T(8,128)(2,1)S(1)} %all_to_all.30.joined, bf16[4096,512]{1,0:T(8,128)(2,1)} %w.1), custom_call_target="tpu_custom_call" | custom-call | tf_op jit(solution)/shard_map/project_out/pallas_call | solution.py:444
  173.4 4.0 %psum.7 = bf16[4,2,512]{2,1,0:T(2,128)(2,1)} all-reduce(f32[4,2,512]{2,1,0:T(2,128)S(1)} %project_out.1), channel_id=1, replica_groups=mesh['ctx'=16,'head'=2] {'head'}, use_global_device_ids=true, to_apply=%region_0.1 | all-reduce | flops 4096 | bytes 24576 | tf_op jit(solution)/shard_map/psum | solution.py:502
  (6 shorter events, 0.2 us)
Async XLA Ops:
  0.6 1.0 copy-start
  2.3 18.2 %all-to-all-start = ((bf16[16,64,128]{2,1,0:T(8,128)(2,1)}), bf16[16,64,128]{2,1,0:T(8,128)(2,1)S(1)}, u32[]{:S(2)}, u32[]{:S(2)}) async-start(bf16[16,64,128]{2,1,0:T(8,128)(2,1)} %split_samples.1), calls=%async_computation | async-start | bytes 524288 | tf_op jit(solution)/shard_map/all_to_all | solution.py:460
  10.6 15.5 %copy-start.2 = (s32[2,8,2]{1,2,0:T(2,128)S(1)}, s32[2,8,2]{1,2,0:T(2,128)}, u32[]{:S(2)}) copy-start(s32[2,8,2]{1,2,0:T(2,128)} %param.10) | copy-start | bytes 388
  10.7 15.6 %copy-start.1 = (s32[2,8,128]{2,1,0:T(8,128)S(1)}, s32[2,8,128]{2,1,0:T(8,128)}, u32[]{:S(2)}) copy-start(s32[2,8,128]{2,1,0:T(8,128)} %param.9) | copy-start | bytes 24580
  21.0 13.4 %collective-permute-start = (bf16[1,4,144,128]{3,2,1,0:T(8,128)(2,1)S(1)}, bf16[1,4,144,128]{3,2,1,0:T(8,128)(2,1)S(1)}, u32[]{:S(2)}, u32[]{:S(2)}) collective-permute-start(bf16[1,4,144,128]{3,2,1,0:T(8,128)(2,1)S(1)} %head_moments.1), channel_id=1, source_target_pairs={{0,16},{2,18},{4,20},{6,22},{8,24},{10,26},{12,28},{14,30},{16,0},... | collective-permute-start | bytes 442376 | tf_op jit(solution)/shard_map/ppermute | solution.py:465
  21.8 14.7 %all-to-all-start.1 = ((f32[16,24,128]{2,1,0:T(8,128)}), f32[16,24,128]{2,1,0:T(8,128)S(1)}, u32[]{:S(2)}, u32[]{:S(2)}) async-start(f32[16,24,128]{2,1,0:T(8,128)} %project_tokens.1), calls=%async_computation.1 | async-start | bytes 393216 | tf_op jit(solution)/shard_map/all_to_all | solution.py:460
  34.5 8.4 %collective-permute-start.1 = (bf16[2,4,144,128]{3,2,1,0:T(8,128)(2,1)S(1)}, bf16[2,4,144,128]{3,2,1,0:T(8,128)(2,1)S(1)}, u32[]{:S(2)}, u32[]{:S(2)}) collective-permute-start(bf16[2,4,144,128]{3,2,1,0:T(8,128)(2,1)S(1)} %pad_maximum_fusion.4), channel_id=1, source_target_pairs={{0,8},{2,10},{4,12},{6,14},{8,0},{10,2},{12,4},{14,6},{16,24},{18,... | collective-permute-start | bytes 884744 | tf_op jit(solution)/shard_map/ppermute | solution.py:465
  37.2 13.3 %all-to-all-start.2 = ((bf16[16,32,128]{2,1,0:T(8,128)(2,1)}), bf16[16,32,128]{2,1,0:T(8,128)(2,1)S(1)}, u32[]{:S(2)}, u32[]{:S(2)}) async-start(bf16[16,32,128]{2,1,0:T(8,128)(2,1)} %normalize_tokens.1), calls=%async_computation.2 | async-start | bytes 262144 | tf_op jit(solution)/shard_map/all_to_all | solution.py:460
  50.6 81.9 %all-to-all-start.3 = ((bf16[16,128,4,256]{3,2,1,0:T(4,128)(2,1)}), bf16[16,128,4,256]{3,2,1,0:T(4,128)(2,1)}, u32[]{:S(2)}, u32[]{:S(2)}) async-start(bf16[16,128,4,256]{3,2,1,0:T(4,128)(2,1)} %pack_rows.1.send.refs_4_), calls=%async_computation.3 | async-start | bytes 8388608 | tf_op jit(solution)/shard_map/all_to_all | solution.py:460
  55.4 16.0 %collective-permute-start.4 = (bf16[4,2,144,128]{3,2,1,0:T(8,128)(2,1)S(1)}, bf16[4,2,144,128]{3,2,1,0:T(8,128)(2,1)S(1)}, u32[]{:S(2)}, u32[]{:S(2)}) collective-permute-start(bf16[4,2,144,128]{3,2,1,0:T(8,128)(2,1)S(1)} %get-tuple-element.25), channel_id=1, source_target_pairs={{0,2},{2,0},{4,6},{6,4},{8,10},{10,8},{12,14},{14,12},{16,18},{18,... | collective-permute-start | bytes 884744 | tf_op jit(solution)/shard_map/ppermute | solution.py:465
  57.0 30.6 %collective-permute-start.2 = (bf16[4,2,144,128]{3,2,1,0:T(8,128)(2,1)S(1)}, bf16[4,2,144,128]{3,2,1,0:T(8,128)(2,1)S(1)}, u32[]{:S(2)}, u32[]{:S(2)}) collective-permute-start(bf16[4,2,144,128]{3,2,1,0:T(8,128)(2,1)S(1)} %get-tuple-element.26), channel_id=1, source_target_pairs={{0,4},{2,6},{4,0},{6,2},{8,12},{10,14},{12,8},{14,10},{16,20},{18,... | collective-permute-start | bytes 884744 | tf_op jit(solution)/shard_map/ppermute | solution.py:465
  71.4 35.0 %collective-permute-start.5 = (bf16[8,2,144,128]{3,2,1,0:T(8,128)(2,1)S(1)}, bf16[8,2,144,128]{3,2,1,0:T(8,128)(2,1)S(1)}, u32[]{:S(2)}, u32[]{:S(2)}) collective-permute-start(bf16[8,2,144,128]{3,2,1,0:T(8,128)(2,1)S(1)} %pad_maximum_fusion.3), channel_id=1, source_target_pairs={{0,4},{2,6},{4,0},{6,2},{8,12},{10,14},{12,8},{14,10},{16,20},{18,... | collective-permute-start | bytes 1769480 | tf_op jit(solution)/shard_map/ppermute | solution.py:465
  87.6 31.8 %collective-permute-start.3 = (bf16[8,2,144,128]{3,2,1,0:T(8,128)(2,1)S(1)}, bf16[8,2,144,128]{3,2,1,0:T(8,128)(2,1)}, u32[]{:S(2)}, u32[]{:S(2)}) collective-permute-start(bf16[8,2,144,128]{3,2,1,0:T(8,128)(2,1)S(1)} %pad_maximum_fusion.2), channel_id=1, source_target_pairs={{0,2},{2,0},{4,6},{6,4},{8,10},{10,8},{12,14},{14,12},{16,18},{18,... | collective-permute-start | bytes 1769480 | tf_op jit(solution)/shard_map/ppermute | solution.py:465
  132.5 26.1 %all-to-all-start.4 = ((f32[16,24,128]{2,1,0:T(8,128)}), f32[16,24,128]{2,1,0:T(8,128)S(1)}, u32[]{:S(2)}, u32[]{:S(2)}) async-start(f32[16,24,128]{2,1,0:T(8,128)} %score_kept.1), calls=%async_computation.4 | async-start | bytes 393216 | tf_op jit(solution)/shard_map/all_to_all | solution.py:460

commit v6 on v5

--- a/solution.py
+++ b/solution.py
@@ -52,12 +52,12 @@
         fetch(m).wait()
 
         def rows(j, inner):
-            values = [spans[m, keep[m, j * 16 + u]] for u in range(16)]
-            for u in range(16):
-                blocks[m, j * 16 + u] = values[u]
+            values = [spans[m, keep[m, j * 32 + u]] for u in range(32)]
+            for u in range(32):
+                blocks[m, j * 32 + u] = values[u]
             return inner
 
-        lax.fori_loop(0, width // 16, rows, 0)
+        lax.fori_loop(0, width // 32, rows, 0)
         put(m).start()
     for m in range(items):
         put(m).wait()

time: 178 us -> 178 us (level)
  transfers between devices with their start and end apart: 11 -> 11, of which waited for: 7 -> 7; matrix products, arithmetic and copies ran while one was open for 1% -> 1% of each run, Pallas kernels for 21% -> 20%
where the time goes in v6:
time: 178 us; the launch traced here: 177 us
  waiting for transfers between devices  64.7 us (36%)
  starting transfers between devices  52.5 us (29%)
  Pallas kernels  41.6 us (23%)
  blocking collectives  14.7 us (8%)
    ppermute x6, waiting for transfers between devices, doubled(): return jnp.concatenate([value, lax.ppermute(value, 'ctx', pairs)], axis=0)  48.4 us
    all_to_all x5, starting transfers between devices, exchange(): return lax.all_to_all(value, 'ctx', split_axis=0, concat_axis=0, tiled=True)  41 us
    all_to_all x5, waiting for transfers between devices, exchange(): return lax.all_to_all(value, 'ctx', split_axis=0, concat_axis=0, tiled=True)  16.3 us
    pallas_call x1, Pallas kernels, score(): pl.pallas_call(kernel, out_shape=jax.ShapeDtypeStruct(parts.shape, parts....  11.8 us
    ppermute x6, starting transfers between devices, doubled(): return jnp.concatenate([value, lax.ppermute(value, 'ctx', pairs)], axis=0)  11.5 us
    all_to_all x1, blocking collectives, exchange(): return lax.all_to_all(value, 'ctx', split_axis=0, concat_axis=0, tiled=True)  10.7 us
    pallas_call x1, Pallas kernels, pack(): pl.pallas_call(pack_kernel, out_shape=pltpu.HBM((items, width, *tail), kv...  7.85 us
    pallas_call x1, Pallas kernels, attend(): pl.pallas_call(attend_kernel, out_shape=jax.ShapeDtypeStruct((16, 24, 128...  6.41 us
  transfers between devices with their start and end apart: 11, of which 7 were waited for; matrix products, arithmetic and copies ran while one was open for 1% of the time, Pallas kernels for 20%

profile of v6, /device:TPU:0, one launch (start us, length us, event | category | flops | bytes accessed | tf_op | source)
XLA Modules:
  0.0 177.1 jit_solution(14517079460548691157)
XLA Ops:
  0.6 0.0 copy-start
  0.6 0.9 copy-done
  1.6 0.7 split_samples.1
  2.3 8.3 %all-to-all-start = ((bf16[16,64,128]{2,1,0:T(8,128)(2,1)}), bf16[16,64,128]{2,1,0:T(8,128)(2,1)S(1)}, u32[]{:S(2)}, u32[]{:S(2)}) async-start(bf16[16,64,128]{2,1,0:T(8,128)(2,1)} %split_samples.1), calls=%async_computation | async-start | bytes 524288 | tf_op jit(solution)/shard_map/all_to_all | solution.py:460
  10.6 0.0 copy-start.2
  10.7 0.0 copy-start.1
  10.7 4.8 %project_tokens.1 = f32[16,24,128]{2,1,0:T(8,128)} custom-call(bf16[4,2,512]{2,1,0:T(2,128)(2,1)} %tokens.1, bf16[512,4096]{1,0:T(8,128)(2,1)} %wq.1, bf16[512,4,256]{2,1,0:T(4,128)(2,1)} %wkv.1), custom_call_target="tpu_custom_call" | custom-call | tf_op jit(solution)/shard_map/project_tokens/pallas_call | solution.py:138
  15.5 5.0 %all-to-all-done.parts = bf16[16,64,128]{2,1,0:T(8,128)(2,1)S(1)} async-done(((bf16[16,64,128]{2,1,0:T(8,128)(2,1)}), bf16[16,64,128]{2,1,0:T(8,128)(2,1)S(1)}, u32[]{:S(2)}, u32[]{:S(2)}) %all-to-all-start) | async-done | bytes 262176 | tf_op jit(solution)/shard_map/all_to_all | solution.py:460
  20.5 0.5 head_moments.1
  21.0 0.7 collective-permute-start
  21.8 4.3 %all-to-all-start.1 = ((f32[16,24,128]{2,1,0:T(8,128)}), f32[16,24,128]{2,1,0:T(8,128)S(1)}, u32[]{:S(2)}, u32[]{:S(2)}) async-start(f32[16,24,128]{2,1,0:T(8,128)} %project_tokens.1), calls=%async_computation.1 | async-start | bytes 393216 | tf_op jit(solution)/shard_map/all_to_all | solution.py:460
  26.1 0.0 copy-done.2
  26.1 0.1 copy.25
  26.2 0.0 copy-done.1
  26.2 7.9 %pack_rows.1.send.refs_4_ = bf16[16,128,4,256]{3,2,1,0:T(4,128)(2,1)} custom-call(s32[16,128]{1,0:T(8,128)S(1)} %bitcast.10, s32[16,2]{1,0:T(8,128)S(1)} %bitcast.5, bf16[2,2048,4,256]{3,2,1,0:T(4,128)(2,1)} %kv.1), custom_call_target="tpu_custom_call" | custom-call | tf_op jit(solution)/shard_map/pack_rows/pallas_call | solution.py:69
  34.1 0.0 collective-permute-done
  34.1 2.0 %collective-permute-start.1 = (bf16[2,4,144,128]{3,2,1,0:T(8,128)(2,1)S(1)}, bf16[2,4,144,128]{3,2,1,0:T(8,128)(2,1)S(1)}, u32[]{:S(2)}, u32[]{:S(2)}) collective-permute-start(bf16[2,4,144,128]{3,2,1,0:T(8,128)(2,1)S(1)} %pad_maximum_fusion.4), channel_id=1, source_target_pairs={{0,8},{2,10},{4,12},{6,14},{8,0},{10,2},{12,4},{14,6},{16,24},{18,... | collective-permute-start | bytes 884744 | tf_op jit(solution)/shard_map/ppermute | solution.py:465
  36.1 0.0 all-to-all-done.1.parts
  36.1 0.8 normalize_tokens.1
  36.9 5.5 %all-to-all-start.2 = ((bf16[16,32,128]{2,1,0:T(8,128)(2,1)}), bf16[16,32,128]{2,1,0:T(8,128)(2,1)S(1)}, u32[]{:S(2)}, u32[]{:S(2)}) async-start(bf16[16,32,128]{2,1,0:T(8,128)(2,1)} %normalize_tokens.1), calls=%async_computation.2 | async-start | bytes 262144 | tf_op jit(solution)/shard_map/all_to_all | solution.py:460
  42.5 0.0 collective-permute-done.1
  42.5 7.7 %all-to-all-done.2.query = bf16[16,32,128]{2,1,0:T(8,128)(2,1)S(1)} async-done(((bf16[16,32,128]{2,1,0:T(8,128)(2,1)}), bf16[16,32,128]{2,1,0:T(8,128)(2,1)S(1)}, u32[]{:S(2)}, u32[]{:S(2)}) %all-to-all-start.2) | async-done | bytes 131104 | tf_op jit(solution)/shard_map/all_to_all | solution.py:460
  50.3 4.7 %all-to-all-start.3 = ((bf16[16,128,4,256]{3,2,1,0:T(4,128)(2,1)}), bf16[16,128,4,256]{3,2,1,0:T(4,128)(2,1)}, u32[]{:S(2)}, u32[]{:S(2)}) async-start(bf16[16,128,4,256]{3,2,1,0:T(4,128)(2,1)} %pack_rows.1.send.refs_4_), calls=%async_computation.3 | async-start | bytes 8388608 | tf_op jit(solution)/shard_map/all_to_all | solution.py:460
  55.0 1.6 collective-permute-start.4
  56.7 1.5 collective-permute-start.2
  58.1 12.9 %collective-permute-done.4 = bf16[4,2,144,128]{3,2,1,0:T(8,128)(2,1)S(1)} collective-permute-done((bf16[4,2,144,128]{3,2,1,0:T(8,128)(2,1)S(1)}, bf16[4,2,144,128]{3,2,1,0:T(8,128)(2,1)S(1)}, u32[]{:S(2)}, u32[]{:S(2)}) %collective-permute-start.4) | collective-permute-done | bytes 294944 | tf_op jit(solution)/shard_map/ppermute | solution.py:465
  71.0 0.1 pad_maximum_fusion.3
  71.1 3.6 %collective-permute-start.5 = (bf16[8,2,144,128]{3,2,1,0:T(8,128)(2,1)S(1)}, bf16[8,2,144,128]{3,2,1,0:T(8,128)(2,1)S(1)}, u32[]{:S(2)}, u32[]{:S(2)}) collective-permute-start(bf16[8,2,144,128]{3,2,1,0:T(8,128)(2,1)S(1)} %pad_maximum_fusion.3), channel_id=1, source_target_pairs={{0,4},{2,6},{4,0},{6,2},{8,12},{10,14},{12,8},{14,10},{16,20},{18,... | collective-permute-start | bytes 1769480 | tf_op jit(solution)/shard_map/ppermute | solution.py:465
  74.7 12.6 %collective-permute-done.2 = bf16[4,2,144,128]{3,2,1,0:T(8,128)(2,1)S(1)} collective-permute-done((bf16[4,2,144,128]{3,2,1,0:T(8,128)(2,1)S(1)}, bf16[4,2,144,128]{3,2,1,0:T(8,128)(2,1)S(1)}, u32[]{:S(2)}, u32[]{:S(2)}) %collective-permute-start.2) | collective-permute-done | bytes 294944 | tf_op jit(solution)/shard_map/ppermute | solution.py:465
  87.2 0.1 pad_maximum_fusion.2
  87.3 2.1 %collective-permute-start.3 = (bf16[8,2,144,128]{3,2,1,0:T(8,128)(2,1)S(1)}, bf16[8,2,144,128]{3,2,1,0:T(8,128)(2,1)}, u32[]{:S(2)}, u32[]{:S(2)}) collective-permute-start(bf16[8,2,144,128]{3,2,1,0:T(8,128)(2,1)S(1)} %pad_maximum_fusion.2), channel_id=1, source_target_pairs={{0,2},{2,0},{4,6},{6,4},{8,10},{10,8},{12,14},{14,12},{16,18},{18,... | collective-permute-start | bytes 1769480 | tf_op jit(solution)/shard_map/ppermute | solution.py:465
  89.4 0.1 copy.20
  89.6 0.1 copy.22.bias
  89.6 6.4 %attend_kept.1.refs_5_ = f32[16,24,128]{2,1,0:T(8,128)S(1)} custom-call(s32[16,2]{1,0:T(8,128)S(1)} %bitcast.6, bf16[16,32,128]{2,1,0:T(8,128)(2,1)S(1)} %all-to-all-done.2.query, f32[16,512]{1,0:T(8,128)S(1)} %copy.22.bias, bf16[16,128,4,256]{3,2,1,0:T(4,128)(2,1)} %pack_rows.1.send.refs_4_), custom_call_target="tpu_custom_call" | custom-call | tf_op jit(solution)/shard_map/attend_kept/pallas_call | solution.py:242
  96.1 10.0 %collective-permute-done.5 = bf16[8,2,144,128]{3,2,1,0:T(8,128)(2,1)S(1)} collective-permute-done((bf16[8,2,144,128]{3,2,1,0:T(8,128)(2,1)S(1)}, bf16[8,2,144,128]{3,2,1,0:T(8,128)(2,1)S(1)}, u32[]{:S(2)}, u32[]{:S(2)}) %collective-permute-start.5) | collective-permute-done | bytes 589856 | tf_op jit(solution)/shard_map/ppermute | solution.py:465
  106.1 0.1 pad_maximum_fusion.1.refs_3_
  106.2 12.9 %collective-permute-done.3 = bf16[8,2,144,128]{3,2,1,0:T(8,128)(2,1)} collective-permute-done((bf16[8,2,144,128]{3,2,1,0:T(8,128)(2,1)S(1)}, bf16[8,2,144,128]{3,2,1,0:T(8,128)(2,1)}, u32[]{:S(2)}, u32[]{:S(2)}) %collective-permute-start.3) | collective-permute-done | bytes 589856 | tf_op jit(solution)/shard_map/ppermute | solution.py:465
  119.1 1.2 pad_maximum_fusion.refs_2_
  120.3 11.8 %score_kept.1 = f32[16,24,128]{2,1,0:T(8,128)} custom-call(s32[1]{0:T(128)} %bitcast.place.refs_0_, s32[16,2]{1,0:T(8,128)S(1)} %bitcast.7, bf16[16,2,144,128]{3,2,1,0:T(8,128)(2,1)S(1)} %pad_maximum_fusion.refs_2_, bf16[16,2,144,128]{3,2,1,0:T(8,128)(2,1)S(1)} %pad_maximum_fusion.1.refs_3_, bf16[16,128,4,256]{3,2,1,0:T(4,128)(2,1)} %pack_rows.1.send.refs_4_, ...), custom_call_target="tpu_custom_call" | custom-call | tf_op jit(solution)/shard_map/score_kept/pallas_call | solution.py:359
  132.1 0.0 all-to-all-done.3.arrived
  132.1 18.1 %all-to-all-start.4 = ((f32[16,24,128]{2,1,0:T(8,128)}), f32[16,24,128]{2,1,0:T(8,128)S(1)}, u32[]{:S(2)}, u32[]{:S(2)}) async-start(f32[16,24,128]{2,1,0:T(8,128)} %score_kept.1), calls=%async_computation.4 | async-start | bytes 393216 | tf_op jit(solution)/shard_map/all_to_all | solution.py:460
  150.2 4.5 %place_blocks.1 = bf16[16,128,4,256]{3,2,1,0:T(4,128)(2,1)} custom-call(s32[1]{0:T(128)} %bitcast.place.refs_0_, s32[16,2]{1,0:T(8,128)S(1)} %bitcast.8, bf16[16,128,4,256]{3,2,1,0:T(4,128)(2,1)} %all-to-all-done.3.arrived), custom_call_target="tpu_custom_call" | custom-call | tf_op jit(solution)/shard_map/place_blocks/pallas_call | solution.py:401
  154.7 3.5 %all-to-all-done.4.parts = f32[16,24,128]{2,1,0:T(8,128)S(1)} async-done(((f32[16,24,128]{2,1,0:T(8,128)}), f32[16,24,128]{2,1,0:T(8,128)S(1)}, u32[]{:S(2)}, u32[]{:S(2)}) %all-to-all-start.4) | async-done | bytes 196640 | tf_op jit(solution)/shard_map/all_to_all | solution.py:460
  158.3 1.6 combine_parts.1
  159.9 10.7 %all_to_all.30.joined = bf16[16,16,128]{2,1,0:T(8,128)(2,1)S(1)} all-to-all(bf16[16,16,128]{2,1,0:T(8,128)(2,1)S(1)} %get-tuple-element.24), channel_id=1, replica_groups=mesh['ctx'=16,'head'=2] {'ctx'}, dimensions={0} | all-to-all | bytes 131072 | tf_op jit(solution)/shard_map/all_to_all | solution.py:460
  170.6 2.5 %project_out.1 = f32[4,2,512]{2,1,0:T(2,128)S(1)} custom-call(bf16[16,16,128]{2,1,0:T(8,128)(2,1)S(1)} %all_to_all.30.joined, bf16[4096,512]{1,0:T(8,128)(2,1)} %w.1), custom_call_target="tpu_custom_call" | custom-call | tf_op jit(solution)/shard_map/project_out/pallas_call | solution.py:444
  173.1 4.0 %psum.7 = bf16[4,2,512]{2,1,0:T(2,128)(2,1)} all-reduce(f32[4,2,512]{2,1,0:T(2,128)S(1)} %project_out.1), channel_id=1, replica_groups=mesh['ctx'=16,'head'=2] {'head'}, use_global_device_ids=true, to_apply=%region_0.1 | all-reduce | flops 4096 | bytes 24576 | tf_op jit(solution)/shard_map/psum | solution.py:502
  (6 shorter events, 0.2 us)
Async XLA Ops:
  0.6 1.0 copy-start
  2.3 18.2 %all-to-all-start = ((bf16[16,64,128]{2,1,0:T(8,128)(2,1)}), bf16[16,64,128]{2,1,0:T(8,128)(2,1)S(1)}, u32[]{:S(2)}, u32[]{:S(2)}) async-start(bf16[16,64,128]{2,1,0:T(8,128)(2,1)} %split_samples.1), calls=%async_computation | async-start | bytes 524288 | tf_op jit(solution)/shard_map/all_to_all | solution.py:460
  10.6 15.5 %copy-start.2 = (s32[2,8,2]{1,2,0:T(2,128)S(1)}, s32[2,8,2]{1,2,0:T(2,128)}, u32[]{:S(2)}) copy-start(s32[2,8,2]{1,2,0:T(2,128)} %param.10) | copy-start | bytes 388
  10.7 15.6 %copy-start.1 = (s32[2,8,128]{2,1,0:T(8,128)S(1)}, s32[2,8,128]{2,1,0:T(8,128)}, u32[]{:S(2)}) copy-start(s32[2,8,128]{2,1,0:T(8,128)} %param.9) | copy-start | bytes 24580
  21.0 13.0 %collective-permute-start = (bf16[1,4,144,128]{3,2,1,0:T(8,128)(2,1)S(1)}, bf16[1,4,144,128]{3,2,1,0:T(8,128)(2,1)S(1)}, u32[]{:S(2)}, u32[]{:S(2)}) collective-permute-start(bf16[1,4,144,128]{3,2,1,0:T(8,128)(2,1)S(1)} %head_moments.1), channel_id=1, source_target_pairs={{0,16},{2,18},{4,20},{6,22},{8,24},{10,26},{12,28},{14,30},{16,0},... | collective-permute-start | bytes 442376 | tf_op jit(solution)/shard_map/ppermute | solution.py:465
  21.8 14.3 %all-to-all-start.1 = ((f32[16,24,128]{2,1,0:T(8,128)}), f32[16,24,128]{2,1,0:T(8,128)S(1)}, u32[]{:S(2)}, u32[]{:S(2)}) async-start(f32[16,24,128]{2,1,0:T(8,128)} %project_tokens.1), calls=%async_computation.1 | async-start | bytes 393216 | tf_op jit(solution)/shard_map/all_to_all | solution.py:460
  34.1 8.4 %collective-permute-start.1 = (bf16[2,4,144,128]{3,2,1,0:T(8,128)(2,1)S(1)}, bf16[2,4,144,128]{3,2,1,0:T(8,128)(2,1)S(1)}, u32[]{:S(2)}, u32[]{:S(2)}) collective-permute-start(bf16[2,4,144,128]{3,2,1,0:T(8,128)(2,1)S(1)} %pad_maximum_fusion.4), channel_id=1, source_target_pairs={{0,8},{2,10},{4,12},{6,14},{8,0},{10,2},{12,4},{14,6},{16,24},{18,... | collective-permute-start | bytes 884744 | tf_op jit(solution)/shard_map/ppermute | solution.py:465
  36.9 13.3 %all-to-all-start.2 = ((bf16[16,32,128]{2,1,0:T(8,128)(2,1)}), bf16[16,32,128]{2,1,0:T(8,128)(2,1)S(1)}, u32[]{:S(2)}, u32[]{:S(2)}) async-start(bf16[16,32,128]{2,1,0:T(8,128)(2,1)} %normalize_tokens.1), calls=%async_computation.2 | async-start | bytes 262144 | tf_op jit(solution)/shard_map/all_to_all | solution.py:460
  50.3 81.9 %all-to-all-start.3 = ((bf16[16,128,4,256]{3,2,1,0:T(4,128)(2,1)}), bf16[16,128,4,256]{3,2,1,0:T(4,128)(2,1)}, u32[]{:S(2)}, u32[]{:S(2)}) async-start(bf16[16,128,4,256]{3,2,1,0:T(4,128)(2,1)} %pack_rows.1.send.refs_4_), calls=%async_computation.3 | async-start | bytes 8388608 | tf_op jit(solution)/shard_map/all_to_all | solution.py:460
  55.0 16.0 %collective-permute-start.4 = (bf16[4,2,144,128]{3,2,1,0:T(8,128)(2,1)S(1)}, bf16[4,2,144,128]{3,2,1,0:T(8,128)(2,1)S(1)}, u32[]{:S(2)}, u32[]{:S(2)}) collective-permute-start(bf16[4,2,144,128]{3,2,1,0:T(8,128)(2,1)S(1)} %get-tuple-element.25), channel_id=1, source_target_pairs={{0,2},{2,0},{4,6},{6,4},{8,10},{10,8},{12,14},{14,12},{16,18},{18,... | collective-permute-start | bytes 884744 | tf_op jit(solution)/shard_map/ppermute | solution.py:465
  56.7 30.6 %collective-permute-start.2 = (bf16[4,2,144,128]{3,2,1,0:T(8,128)(2,1)S(1)}, bf16[4,2,144,128]{3,2,1,0:T(8,128)(2,1)S(1)}, u32[]{:S(2)}, u32[]{:S(2)}) collective-permute-start(bf16[4,2,144,128]{3,2,1,0:T(8,128)(2,1)S(1)} %get-tuple-element.26), channel_id=1, source_target_pairs={{0,4},{2,6},{4,0},{6,2},{8,12},{10,14},{12,8},{14,10},{16,20},{18,... | collective-permute-start | bytes 884744 | tf_op jit(solution)/shard_map/ppermute | solution.py:465
  71.1 35.0 %collective-permute-start.5 = (bf16[8,2,144,128]{3,2,1,0:T(8,128)(2,1)S(1)}, bf16[8,2,144,128]{3,2,1,0:T(8,128)(2,1)S(1)}, u32[]{:S(2)}, u32[]{:S(2)}) collective-permute-start(bf16[8,2,144,128]{3,2,1,0:T(8,128)(2,1)S(1)} %pad_maximum_fusion.3), channel_id=1, source_target_pairs={{0,4},{2,6},{4,0},{6,2},{8,12},{10,14},{12,8},{14,10},{16,20},{18,... | collective-permute-start | bytes 1769480 | tf_op jit(solution)/shard_map/ppermute | solution.py:465
  87.3 31.8 %collective-permute-start.3 = (bf16[8,2,144,128]{3,2,1,0:T(8,128)(2,1)S(1)}, bf16[8,2,144,128]{3,2,1,0:T(8,128)(2,1)}, u32[]{:S(2)}, u32[]{:S(2)}) collective-permute-start(bf16[8,2,144,128]{3,2,1,0:T(8,128)(2,1)S(1)} %pad_maximum_fusion.2), channel_id=1, source_target_pairs={{0,2},{2,0},{4,6},{6,4},{8,10},{10,8},{12,14},{14,12},{16,18},{18,... | collective-permute-start | bytes 1769480 | tf_op jit(solution)/shard_map/ppermute | solution.py:465
  132.1 26.1 %all-to-all-start.4 = ((f32[16,24,128]{2,1,0:T(8,128)}), f32[16,24,128]{2,1,0:T(8,128)S(1)}, u32[]{:S(2)}, u32[]{:S(2)}) async-start(f32[16,24,128]{2,1,0:T(8,128)} %score_kept.1), calls=%async_computation.4 | async-start | bytes 393216 | tf_op jit(solution)/shard_map/all_to_all | solution.py:460
